TPU v7x, 32 devices: a whole 2x2x4 slice. The times are simulated.
32 devices in a mesh: sector: 4 (over z), group: 8 (over y, x, core).
Axes of the slice: x: 2, y: 2, z: 4, core: 2. Of those that a mesh axis runs over, the one named last changes fastest.
Arguments:
- spectrum: float32 [1152, 128, 512], P('group', None, 'sector'), may hold values from 0.1 to 2
- land_mask: int32 [128, 512], P(None, 'sector'), may hold values 0 or 1
- wind_field: float32 [2, 128, 512], P(None, 'group', 'sector'), may hold values from -3 to 3
- assignment: int32 [1152], replicated, may hold values from 0 to 1151, each once
- courant: float32 [32], replicated, may hold values from 0.3 to 0.65
- growth: float32 [32], replicated, may hold values from 0.1 to 0.5
- whitecap: float32 [32], replicated, may hold values from 0.2 to 1
- weights: float32 [32], replicated, may hold values from 0.5 to 5
- spread: float32 [32, 36, 36], replicated, may hold values from -1 to 1
Outputs:
- updated: float32 [1152, 128, 512], P('group', None, 'sector')
Inputs may be any that keep to these rules, and one draw needn't show every extreme that they name: `assignment`: each component number appears exactly once.
All inputs are finite; a program needn't handle non-finite values. No bound on the sum of `land_mask` on one device may be relied on, other than what follows from the above.
Results may differ from a plain program's by a relative error of at most 0.00007.
Values sent between devices are 32-bit elements; how exact they have to be, the bound alone decides.
No kernel may reach another device: no remote copies, remote signals or barrier semaphores. Data moves between devices by JAX's collectives and lax.ppermute only.
A program may use at most 128 MiB of HBM per device.

v0:
```python
import math

import jax
import jax.numpy as jnp
from jax import lax
from jax.sharding import PartitionSpec as P

DIRS = 36
FREQ = 32
SUBSTEPS = 6
LAT = 128


def extended(cells, sides, width):
    for axis, dim in sides:
        count = lax.axis_size(axis)
        head = lax.slice_in_dim(cells, 0, width, axis=dim)
        tail = lax.slice_in_dim(cells, cells.shape[dim] - width, cells.shape[dim], axis=dim)
        cells = jnp.concatenate(
            [
                lax.ppermute(tail, axis, [(i, (i + 1) % count) for i in range(count)]),
                cells,
                lax.ppermute(head, axis, [((i + 1) % count, i) for i in range(count)]),
            ],
            axis=dim,
        )
    return cells


def freq_onehot(frequency):
    return (frequency[:, None] == jnp.arange(FREQ)[None, :]).astype(jnp.float32)


def flow_terms(kinds, courant):
    direction = kinds % DIRS
    frequency = kinds // DIRS
    angles = (direction.astype(jnp.float32) + 0.5) * (2.0 * math.pi / DIRS)
    speeds = jnp.dot(freq_onehot(frequency), courant, precision=lax.Precision.HIGHEST)
    latitude = (jnp.arange(LAT).astype(jnp.float32) + 0.5 - LAT / 2) * (math.pi / 2160.0)
    flow_x = speeds[:, None] * jnp.cos(angles)[:, None] / jnp.cos(latitude)[None, :]
    flow_y = speeds * jnp.sin(angles)
    return (flow_x, flow_y)


def combine(centre, from_west, from_east, rates):
    keep_rate, east_rate, west_rate, north_rate, south_rate = rates
    from_south = jnp.pad(centre[:, :-1], ((0, 0), (1, 0), (0, 0)))
    from_north = jnp.pad(centre[:, 1:], ((0, 0), (0, 1), (0, 0)))
    return (
        keep_rate * centre
        + east_rate * from_west
        + west_rate * from_east
        + north_rate * from_south
        + south_rate * from_north
    )


def propagate(wave, flow_x, flow_y, sea_mask):
    rates = (
        1.0 - jnp.abs(flow_x)[:, :, None] - jnp.abs(flow_y)[:, None, None],
        jnp.maximum(flow_x, 0.0)[:, :, None],
        jnp.maximum(-flow_x, 0.0)[:, :, None],
        jnp.maximum(flow_y, 0.0)[:, None, None],
        jnp.maximum(-flow_y, 0.0)[:, None, None],
    )
    for substep in range(SUBSTEPS):
        padded = extended(wave, (("sector", 2),), 1)
        wave = combine(wave, padded[:, :, :-2], padded[:, :, 2:], rates) * sea_mask[None]
    return wave


def local(spectrum, land_mask, wind_field, assignment, courant, growth, whitecap, weights, spread):
    member = lax.axis_index("group")
    comps_dev = spectrum.shape[0]
    lon_local = spectrum.shape[2]
    all_comps = assignment.shape[0]
    rows_dev = wind_field.shape[1]
    sea_mask = land_mask.astype(jnp.float32)
    kinds = lax.dynamic_slice_in_dim(assignment, member * comps_dev, comps_dev, 0)
    flow_x, flow_y = flow_terms(kinds, courant)
    moved = lax.all_to_all(
        propagate(spectrum, flow_x, flow_y, sea_mask),
        "group",
        split_axis=1,
        concat_axis=0,
        tiled=True,
    )
    points = rows_dev * lon_local
    energy = moved.reshape(all_comps, points)
    sea_rows = lax.dynamic_slice_in_dim(sea_mask, member * rows_dev, rows_dev, 0).reshape(points)
    winds = wind_field.reshape(2, points)
    direction = assignment % DIRS
    frequency = assignment // DIRS
    angles = (direction.astype(jnp.float32) + 0.5) * (2.0 * math.pi / DIRS)
    per_freq = jnp.stack((growth, whitecap, weights), axis=1)
    picked = jnp.dot(freq_onehot(frequency), per_freq, precision=lax.Precision.HIGHEST)
    kind_onehot = (assignment[:, None] == jnp.arange(all_comps)[None, :]).astype(jnp.float32)
    picked_rows = jnp.dot(
        kind_onehot, spread.reshape(FREQ * DIRS, DIRS), precision=lax.Precision.HIGHEST
    )
    dir_onehot = (jnp.arange(DIRS)[:, None] == direction[None, :]).astype(jnp.float32)
    same_freq = (frequency[:, None] == frequency[None, :]).astype(jnp.float32)
    coupling = jnp.dot(picked_rows, dir_onehot, precision=lax.Precision.HIGHEST) * same_freq
    loading = jnp.sum(picked[:, 2][:, None] * energy, axis=0) / all_comps
    drive = (
        jnp.cos(angles)[:, None] * winds[0][None, :] + jnp.sin(angles)[:, None] * winds[1][None, :]
    )
    exponent = (
        picked[:, 0][:, None] * jnp.maximum(drive, 0.0)
        - picked[:, 1][:, None] * (loading / (1.0 + loading))[None, :]
    )
    mixed = jnp.dot(coupling, energy, precision=lax.Precision.HIGHEST)
    renewed = (energy * jnp.exp(exponent) + 0.5 * mixed) * sea_rows[None, :]
    return lax.all_to_all(
        renewed.reshape(all_comps, rows_dev, lon_local),
        "group",
        split_axis=0,
        concat_axis=1,
        tiled=True,
    )


def solution(mesh):
    in_specs = (
        P("group", None, "sector"),
        P(None, "sector"),
        P(None, "group", "sector"),
        P(),
        P(),
        P(),
        P(),
        P(),
        P(),
    )
    out_specs = P("group", None, "sector")
    return jax.shard_map(local, mesh=mesh, in_specs=in_specs, out_specs=out_specs, check_vma=False)
```

profile of v0, /device:TPU:0, one launch (start us, length us, event | category | flops | bytes accessed | tf_op | source)
XLA Modules:
  0.0 494.8 jit_solution(8796984362894581755)
XLA Ops:
  0.0 9.6 %copy.15 = f32[144,128,128]{1,0,2:T(8,128)} copy(f32[144,128,128]{2,1,0:T(8,128)} %param.9) | data formatting | bytes 18874368 | tf_op args[0]
  9.6 0.9 fusion.83
  10.5 3.1 collective-permute-start
  13.6 2.1 collective-permute-start.1
  15.8 0.0 copy-start.4
  15.8 0.0 copy-start.3
  15.8 14.2 %fusion.82 = (f32[144,127,128]{1,0,2:T(8,128)}, f32[144,127,128]{1,0,2:T(8,128)}) fusion(f32[144,128,128]{1,0,2:T(8,128)} %copy.15), kind=kLoop, calls=%fused_computation.122 | loop fusion | bytes 37453824 | tf_op jit(solution)/shard_map/slice | solution.py:47
  30.0 0.1 and_select_fusion.1
  30.1 0.2 fusion.55
  30.3 0.2 fusion.70
  30.6 0.1 subtract_subtract_fusion
  30.7 0.1 copy.22
  30.8 0.0 collective-permute-done
  30.8 16.4 %fusion.43 = f32[144,128,128]{1,0,2:T(8,128)S(1)} fusion(f32[144,128,1]{1,0,2:T(8,128)S(1)} %collective-permute-done.1, f32[144,128,128]{1,0,2:T(8,128)} %copy.15, f32[144,128,1]{1,0,2:T(8,128)S(1)} %collective-permute-done, f32[144,127,128]{1,0,2:T(8,128)} %get-tuple-element.31, f32[144,127,128]{1,0,2:T(8,128)} %get-tuple-element.30, ...), kind=kLoop, calls=%fused_computation.57 | loop fusion | flops 28311552 | bytes 38036608 | tf_op jit(solution)/shard_map/mul | solution.py:68
  47.2 0.1 collective-permute-start.2
  47.3 3.8 collective-permute-start.3
  51.1 8.1 %fusion.80 = (f32[144,127,128]{1,0,2:T(8,128)}, f32[144,127,128]{1,0,2:T(8,128)}) fusion(f32[144,128,128]{1,0,2:T(8,128)S(1)} %fusion.43), kind=kLoop, calls=%fused_computation.120 | loop fusion | bytes 37453824 | tf_op jit(solution)/shard_map/slice | solution.py:47
  59.2 0.0 collective-permute-done.2
  59.2 0.0 collective-permute-done.3
  59.2 13.2 %fusion.36 = f32[144,128,128]{1,0,2:T(8,128)} fusion(f32[144,128,1]{1,0,2:T(8,128)S(1)} %collective-permute-done.3, f32[144,128,128]{1,0,2:T(8,128)S(1)} %fusion.43, f32[144,128,1]{1,0,2:T(8,128)S(1)} %collective-permute-done.2, f32[144,127,128]{1,0,2:T(8,128)} %get-tuple-element.27, f32[144,127,128]{1,0,2:T(8,128)} %get-tuple-element.26, ...), kind=kLoop, calls=%fused_computation.48 | loop fusion | flops 28311552 | bytes 38036608 | tf_op jit(solution)/shard_map/mul | solution.py:68
  72.4 0.9 fusion.79
  73.3 0.1 collective-permute-start.4
  73.4 0.0 slice-start
  73.4 0.0 slice-start.1
  73.4 3.8 collective-permute-start.5
  77.2 14.4 %fusion.78 = (f32[144,127,128]{1,0,2:T(8,128)}, f32[144,127,128]{1,0,2:T(8,128)}) fusion(f32[144,128,128]{1,0,2:T(8,128)} %fusion.36), kind=kLoop, calls=%fused_computation.118 | loop fusion | bytes 37453824 | tf_op jit(solution)/shard_map/slice | solution.py:47
  91.6 0.0 collective-permute-done.4
  91.7 13.2 %fusion.29 = f32[144,128,128]{1,0,2:T(8,128)} fusion(f32[144,128,1]{1,0,2:T(8,128)S(1)} %collective-permute-done.5, f32[144,128,128]{1,0,2:T(8,128)S(1)} %bitcast.47, f32[144,128,1]{1,0,2:T(8,128)S(1)} %collective-permute-done.4, f32[144,127,128]{1,0,2:T(8,128)} %get-tuple-element.23, f32[144,127,128]{1,0,2:T(8,128)} %get-tuple-element.22, ...), kind=kLoop, calls=%fused_computation.39 | loop fusion | flops 28311552 | bytes 38036608 | tf_op jit(solution)/shard_map/mul | solution.py:68
  104.9 0.9 fusion.77
  105.8 0.1 collective-permute-start.6
  105.9 0.0 slice-start.3
  105.9 3.9 collective-permute-start.7
  109.9 14.4 %fusion.76 = (f32[144,127,128]{1,0,2:T(8,128)}, f32[144,127,128]{1,0,2:T(8,128)}) fusion(f32[144,128,128]{1,0,2:T(8,128)} %fusion.29), kind=kLoop, calls=%fused_computation.116 | loop fusion | bytes 37453824 | tf_op jit(solution)/shard_map/slice | solution.py:47
  124.3 0.0 collective-permute-done.6
  124.3 0.0 collective-permute-done.7
  124.3 13.2 %fusion.22 = f32[144,128,128]{1,0,2:T(8,128)} fusion(f32[144,128,1]{1,0,2:T(8,128)S(1)} %collective-permute-done.7, f32[144,128,128]{1,0,2:T(8,128)S(1)} %bitcast.49, f32[144,128,1]{1,0,2:T(8,128)S(1)} %collective-permute-done.6, f32[144,127,128]{1,0,2:T(8,128)} %get-tuple-element.19, f32[144,127,128]{1,0,2:T(8,128)} %get-tuple-element.18, ...), kind=kLoop, calls=%fused_computation.30 | loop fusion | flops 28311552 | bytes 38036608 | tf_op jit(solution)/shard_map/mul | solution.py:68
  137.5 0.9 fusion.75
  138.5 0.1 collective-permute-start.8
  138.5 3.8 collective-permute-start.9
  142.3 14.4 %fusion.74 = (f32[144,127,128]{1,0,2:T(8,128)}, f32[144,127,128]{1,0,2:T(8,128)}) fusion(f32[144,128,128]{1,0,2:T(8,128)} %fusion.22), kind=kLoop, calls=%fused_computation.114 | loop fusion | bytes 37453824 | tf_op jit(solution)/shard_map/slice | solution.py:47
  156.8 0.0 collective-permute-done.8
  156.8 16.4 %fusion.15 = f32[144,128,128]{1,0,2:T(8,128)S(1)} fusion(f32[144,128,1]{1,0,2:T(8,128)S(1)} %collective-permute-done.9, f32[144,128,128]{1,0,2:T(8,128)} %fusion.22, f32[144,128,1]{1,0,2:T(8,128)S(1)} %collective-permute-done.8, f32[144,127,128]{1,0,2:T(8,128)} %get-tuple-element.15, f32[144,127,128]{1,0,2:T(8,128)} %get-tuple-element.14, ...), kind=kLoop, calls=%fused_computation.21 | loop fusion | flops 28311552 | bytes 38036608 | tf_op jit(solution)/shard_map/mul | solution.py:68
  173.2 0.1 collective-permute-start.10
  173.2 3.8 collective-permute-start.11
  177.1 8.1 %fusion.72 = (f32[144,127,128]{1,0,2:T(8,128)}, f32[144,127,128]{1,0,2:T(8,128)}) fusion(f32[144,128,128]{1,0,2:T(8,128)S(1)} %fusion.15), kind=kLoop, calls=%fused_computation.112 | loop fusion | bytes 37453824 | tf_op jit(solution)/shard_map/slice | solution.py:47
  185.2 13.1 %fusion.8 = f32[144,128,128]{1,0,2:T(8,128)} fusion(f32[144,128,1]{1,0,2:T(8,128)S(1)} %collective-permute-done.11, f32[144,128,128]{1,0,2:T(8,128)S(1)} %fusion.15, f32[144,128,1]{1,0,2:T(8,128)S(1)} %collective-permute-done.10, f32[144,127,128]{1,0,2:T(8,128)} %get-tuple-element.11, f32[144,127,128]{1,0,2:T(8,128)} %get-tuple-element.10, ...), kind=kLoop, calls=%fused_computation.12 | loop fusion | flops 28311552 | bytes 38036608 | tf_op jit(solution)/shard_map/mul | solution.py:68
  198.3 9.6 %copy.23 = f32[144,128,128]{2,0,1:T(8,128)} copy(f32[144,128,128]{1,0,2:T(8,128)} %fusion.8) | data formatting | bytes 18874368 | tf_op jit(solution)/shard_map/mul | solution.py:68
  207.9 0.0 copy-start.5
  207.9 5.6 %all-to-all-start = ((f32[144,128,128]{2,0,1:T(8,128)}), f32[144,128,128]{2,0,1:T(8,128)}, u32[]{:S(2)}, u32[]{:S(2)}) async-start(f32[144,128,128]{2,0,1:T(8,128)} %copy.23), calls=%async_computation | async-start | bytes 18874368 | tf_op jit(solution)/shard_map/all_to_all | solution.py:81
  213.6 0.5 fusion.52
  214.1 0.1 slice_reduce_fusion.2
  214.2 0.1 mul.415
  214.3 0.7 copy.25
  215.0 0.4 reshape.154
  215.4 0.1 fusion.59
  215.5 2.7 fusion.50
  218.2 4.8 convolution_select_fusion
  223.0 95.8 %all-to-all-done = f32[144,128,128]{2,0,1:T(8,128)} async-done(((f32[144,128,128]{2,0,1:T(8,128)}), f32[144,128,128]{2,0,1:T(8,128)}, u32[]{:S(2)}, u32[]{:S(2)}) %all-to-all-start) | async-done | bytes 9437216 | tf_op jit(solution)/shard_map/all_to_all | solution.py:81
  318.8 6.5 %copy.24 = f32[144,8,16,128]{3,2,0,1:T(8,128)S(1)} copy(f32[144,8,16,128]{3,0,2,1:T(8,128)} %bitcast.2) | data formatting | bytes 18874368 | tf_op jit(solution)/shard_map/all_to_all | solution.py:81
  325.3 7.5 %fusion.46 = f32[16,128]{1,0:T(8,128)S(1)} fusion(f32[8,144]{1,0:T(8,128)S(1)} %mul.415, f32[144,8,16,128]{3,0,2,1:T(8,128)} %bitcast.2), kind=kLoop, calls=%fused_computation.62 | loop fusion | flops 4716544 | bytes 9449984 | tf_op jit(solution)/shard_map/reduce_sum | solution.py:104
  332.9 46.4 %fusion.3 = f32[144,8,16,128]{3,1,2,0:T(8,128)S(1)} fusion(f32[1152,1152]{1,0:T(8,128)} %convolution_select_fusion, f32[144,8,16,128]{3,2,1,0:T(8,128)S(1)} %bitcast.52, f32[2048]{0:T(1024)S(1)} %dynamic-slice_bitcast_fusion, f32[2048]{0:T(1024)S(1)} %add_divide_fusion, f32[1152]{0:T(1024)S(1)} %get-tuple-element.7, f32[2048]{0:T(1024)S(1)} %get-tuple-element.35, ...), kind=kOutput, calls=%fused_computation.6 | convolution fusion | flops 32640860160 | bytes 24233984 | tf_op jit(solution)/shard_map/dot_general | solution.py:112
  379.3 2.3 copy.28
  381.5 107.8 %all_to_all.33 = f32[1152,16,128]{2,1,0:T(8,128)S(1)} all-to-all(f32[1152,16,128]{2,1,0:T(8,128)S(1)} %bitcast.50), channel_id=1, replica_groups=mesh['sector'=4,'group'=8] {'group'}, dimensions={0} | all-to-all | bytes 18874368 | tf_op jit(solution)/shard_map/all_to_all | solution.py:114
  489.3 5.2 %copy.26 = f32[8,144,16,128]{3,2,0,1:T(8,128)} copy(f32[8,144,16,128]{3,2,1,0:T(8,128)S(1)} %bitcast.51) | data formatting | bytes 18874368 | tf_op jit(solution)/shard_map/all_to_all | solution.py:114
  (40 shorter events, 0.2 us)
Async XLA Ops:
  0.0 30.1 %copy-start = (f32[32]{0:T(128)S(1)}, f32[32]{0:T(128)}, u32[]{:S(2)}) copy-start(f32[32]{0:T(128)} %param.13) | copy-start | bytes 388
  10.5 20.3 %collective-permute-start = (f32[144,128,1]{1,0,2:T(8,128)S(1)}, f32[144,128,1]{1,0,2:T(8,128)S(1)}, u32[]{:S(2)}, u32[]{:S(2)}) collective-permute-start(f32[144,128,1]{1,0,2:T(8,128)S(1)} %get-tuple-element.32), channel_id=1, source_target_pairs={{0,8},{8,16},{16,24},{24,0},{1,9},{9,17},{17,25},{25,1},{2,10},{10... | collective-permute-start | bytes 221192 | tf_op jit(solution)/shard_map/ppermute | solution.py:21
  13.6 17.2 %collective-permute-start.1 = (f32[144,128,1]{1,0,2:T(8,128)S(1)}, f32[144,128,1]{1,0,2:T(8,128)S(1)}, u32[]{:S(2)}, u32[]{:S(2)}) collective-permute-start(f32[144,128,1]{1,0,2:T(8,128)S(1)} %get-tuple-element.33), channel_id=1, source_target_pairs={{8,0},{16,8},{24,16},{0,24},{9,1},{17,9},{25,17},{1,25},{10,2},{18... | collective-permute-start | bytes 221192 | tf_op jit(solution)/shard_map/ppermute | solution.py:23
  15.8 14.3 %copy-start.4 = (s32[1152]{0:T(1024)S(1)}, s32[1152]{0:T(1024)}, u32[]{:S(2)}) copy-start(s32[1152]{0:T(1024)} %param.12) | copy-start | bytes 13828
  15.8 14.9 %copy-start.3 = (s32[128,128]{1,0:T(8,128)S(1)}, s32[128,128]{1,0:T(8,128)}, u32[]{:S(2)}) copy-start(s32[128,128]{1,0:T(8,128)} %param.10) | copy-start | bytes 196612
  47.2 12.0 %collective-permute-start.2 = (f32[144,128,1]{1,0,2:T(8,128)S(1)}, f32[144,128,1]{1,0,2:T(8,128)S(1)}, u32[]{:S(2)}, u32[]{:S(2)}) collective-permute-start(f32[144,128,1]{1,0,2:T(8,128)S(1)} %get-tuple-element.28), channel_id=1, source_target_pairs={{0,8},{8,16},{16,24},{24,0},{1,9},{9,17},{17,25},{25,1},{2,10},{10... | collective-permute-start | bytes 221192 | tf_op jit(solution)/shard_map/ppermute | solution.py:21
  47.3 11.9 %collective-permute-start.3 = (f32[144,128,1]{1,0,2:T(8,128)S(1)}, f32[144,128,1]{1,0,2:T(8,128)S(1)}, u32[]{:S(2)}, u32[]{:S(2)}) collective-permute-start(f32[144,128,1]{1,0,2:T(8,128)S(1)} %get-tuple-element.29), channel_id=1, source_target_pairs={{8,0},{16,8},{24,16},{0,24},{9,1},{17,9},{25,17},{1,25},{10,2},{18... | collective-permute-start | bytes 221192 | tf_op jit(solution)/shard_map/ppermute | solution.py:23
  73.3 18.3 %collective-permute-start.4 = (f32[144,128,1]{1,0,2:T(8,128)S(1)}, f32[144,128,1]{1,0,2:T(8,128)S(1)}, u32[]{:S(2)}, u32[]{:S(2)}) collective-permute-start(f32[144,128,1]{1,0,2:T(8,128)S(1)} %get-tuple-element.24), channel_id=1, source_target_pairs={{0,8},{8,16},{16,24},{24,0},{1,9},{9,17},{17,25},{25,1},{2,10},{10... | collective-permute-start | bytes 221192 | tf_op jit(solution)/shard_map/ppermute | solution.py:21
  73.4 18.2 %slice-start = ((s8[9437184]{0:T(1024)(128)(4,1)}), s8[4194304]{0:T(1024)(128)(4,1)S(1)}, s32[]{:S(2)}) async-start(s8[9437184]{0:T(1024)(128)(4,1)} %bitcast.46), calls=%async_computation.2 | async-start | bytes 8388608
  73.4 18.2 %slice-start.1 = ((s8[9437184]{0:T(1024)(128)(4,1)}), s8[4194304]{0:T(1024)(128)(4,1)S(1)}, s32[]{:S(2)}) async-start(s8[9437184]{0:T(1024)(128)(4,1)} %bitcast.46), calls=%async_computation.3 | async-start | bytes 8388608
  73.4 18.2 %slice-start.2 = ((s8[9437184]{0:T(1024)(128)(4,1)}), s8[1048576]{0:T(1024)(128)(4,1)S(1)}, s32[]{:S(2)}) async-start(s8[9437184]{0:T(1024)(128)(4,1)} %bitcast.46), calls=%async_computation.4 | async-start | bytes 2097152
  73.4 18.2 %collective-permute-start.5 = (f32[144,128,1]{1,0,2:T(8,128)S(1)}, f32[144,128,1]{1,0,2:T(8,128)S(1)}, u32[]{:S(2)}, u32[]{:S(2)}) collective-permute-start(f32[144,128,1]{1,0,2:T(8,128)S(1)} %get-tuple-element.25), channel_id=1, source_target_pairs={{8,0},{16,8},{24,16},{0,24},{9,1},{17,9},{25,17},{1,25},{10,2},{18... | collective-permute-start | bytes 221192 | tf_op jit(solution)/shard_map/ppermute | solution.py:23
  105.8 18.5 %collective-permute-start.6 = (f32[144,128,1]{1,0,2:T(8,128)S(1)}, f32[144,128,1]{1,0,2:T(8,128)S(1)}, u32[]{:S(2)}, u32[]{:S(2)}) collective-permute-start(f32[144,128,1]{1,0,2:T(8,128)S(1)} %get-tuple-element.20), channel_id=1, source_target_pairs={{0,8},{8,16},{16,24},{24,0},{1,9},{9,17},{17,25},{25,1},{2,10},{10... | collective-permute-start | bytes 221192 | tf_op jit(solution)/shard_map/ppermute | solution.py:21
  105.9 18.4 %slice-start.3 = ((s8[9437184]{0:T(1024)(128)(4,1)}), s8[4194304]{0:T(1024)(128)(4,1)S(1)}, s32[]{:S(2)}) async-start(s8[9437184]{0:T(1024)(128)(4,1)} %bitcast.48), calls=%async_computation.5 | async-start | bytes 8388608
  105.9 18.4 %slice-start.4 = ((s8[9437184]{0:T(1024)(128)(4,1)}), s8[4194304]{0:T(1024)(128)(4,1)S(1)}, s32[]{:S(2)}) async-start(s8[9437184]{0:T(1024)(128)(4,1)} %bitcast.48), calls=%async_computation.6 | async-start | bytes 8388608
  105.9 18.4 %slice-start.5 = ((s8[9437184]{0:T(1024)(128)(4,1)}), s8[1048576]{0:T(1024)(128)(4,1)S(1)}, s32[]{:S(2)}) async-start(s8[9437184]{0:T(1024)(128)(4,1)} %bitcast.48), calls=%async_computation.7 | async-start | bytes 2097152
  105.9 18.4 %collective-permute-start.7 = (f32[144,128,1]{1,0,2:T(8,128)S(1)}, f32[144,128,1]{1,0,2:T(8,128)S(1)}, u32[]{:S(2)}, u32[]{:S(2)}) collective-permute-start(f32[144,128,1]{1,0,2:T(8,128)S(1)} %get-tuple-element.21), channel_id=1, source_target_pairs={{8,0},{16,8},{24,16},{0,24},{9,1},{17,9},{25,17},{1,25},{10,2},{18... | collective-permute-start | bytes 221192 | tf_op jit(solution)/shard_map/ppermute | solution.py:23
  138.5 18.3 %collective-permute-start.8 = (f32[144,128,1]{1,0,2:T(8,128)S(1)}, f32[144,128,1]{1,0,2:T(8,128)S(1)}, u32[]{:S(2)}, u32[]{:S(2)}) collective-permute-start(f32[144,128,1]{1,0,2:T(8,128)S(1)} %get-tuple-element.16), channel_id=1, source_target_pairs={{0,8},{8,16},{16,24},{24,0},{1,9},{9,17},{17,25},{25,1},{2,10},{10... | collective-permute-start | bytes 221192 | tf_op jit(solution)/shard_map/ppermute | solution.py:21
  138.5 18.2 %collective-permute-start.9 = (f32[144,128,1]{1,0,2:T(8,128)S(1)}, f32[144,128,1]{1,0,2:T(8,128)S(1)}, u32[]{:S(2)}, u32[]{:S(2)}) collective-permute-start(f32[144,128,1]{1,0,2:T(8,128)S(1)} %get-tuple-element.17), channel_id=1, source_target_pairs={{8,0},{16,8},{24,16},{0,24},{9,1},{17,9},{25,17},{1,25},{10,2},{18... | collective-permute-start | bytes 221192 | tf_op jit(solution)/shard_map/ppermute | solution.py:23
  173.2 12.0 %collective-permute-start.10 = (f32[144,128,1]{1,0,2:T(8,128)S(1)}, f32[144,128,1]{1,0,2:T(8,128)S(1)}, u32[]{:S(2)}, u32[]{:S(2)}) collective-permute-start(f32[144,128,1]{1,0,2:T(8,128)S(1)} %get-tuple-element.12), channel_id=1, source_target_pairs={{0,8},{8,16},{16,24},{24,0},{1,9},{9,17},{17,25},{25,1},{2,10},{10... | collective-permute-start | bytes 221192 | tf_op jit(solution)/shard_map/ppermute | solution.py:21
  173.2 11.9 %collective-permute-start.11 = (f32[144,128,1]{1,0,2:T(8,128)S(1)}, f32[144,128,1]{1,0,2:T(8,128)S(1)}, u32[]{:S(2)}, u32[]{:S(2)}) collective-permute-start(f32[144,128,1]{1,0,2:T(8,128)S(1)} %get-tuple-element.13), channel_id=1, source_target_pairs={{8,0},{16,8},{24,16},{0,24},{9,1},{17,9},{25,17},{1,25},{10,2},{18... | collective-permute-start | bytes 221192 | tf_op jit(solution)/shard_map/ppermute | solution.py:23
  207.9 5.7 %copy-start.6 = (f32[32]{0:T(128)S(1)}, f32[32]{0:T(128)}, u32[]{:S(2)}) copy-start(f32[32]{0:T(128)} %param.16) | copy-start | bytes 388
  207.9 5.7 %copy-start.7 = (f32[32]{0:T(128)S(1)}, f32[32]{0:T(128)}, u32[]{:S(2)}) copy-start(f32[32]{0:T(128)} %param.15) | copy-start | bytes 388
  207.9 5.7 %copy-start.8 = (f32[32]{0:T(128)S(1)}, f32[32]{0:T(128)}, u32[]{:S(2)}) copy-start(f32[32]{0:T(128)} %param.14) | copy-start | bytes 388
  207.9 6.3 %copy-start.2 = (f32[32,36,36]{2,0,1:T(8,128)S(1)}, f32[32,36,36]{2,0,1:T(8,128)}, u32[]{:S(2)}) copy-start(f32[32,36,36]{2,0,1:T(8,128)} %param.17) | copy-start | bytes 497668
  207.9 7.5 %copy-start.5 = (f32[2,16,128]{2,1,0:T(8,128)S(1)}, f32[2,16,128]{2,1,0:T(8,128)}, u32[]{:S(2)}) copy-start(f32[2,16,128]{2,1,0:T(8,128)} %param.11) | copy-start | bytes 49156
  207.9 110.9 %all-to-all-start = ((f32[144,128,128]{2,0,1:T(8,128)}), f32[144,128,128]{2,0,1:T(8,128)}, u32[]{:S(2)}, u32[]{:S(2)}) async-start(f32[144,128,128]{2,0,1:T(8,128)} %copy.23), calls=%async_computation | async-start | bytes 18874368 | tf_op jit(solution)/shard_map/all_to_all | solution.py:81
  489.3 5.2 %copy-start.1 = (f32[32]{0:T(128)S(1)}, f32[32]{0:T(128)}, u32[]{:S(2)}) copy-start(f32[32]{0:T(128)} %param.13) | copy-start | bytes 388
where the time goes:
time: 503 us; the launch traced here: 495 us
  local copies, waits for them, and re-layouts  112 us (22%)
  blocking collectives  108 us (21%)
  waiting for transfers between devices  95.8 us (19%)
  other arithmetic  93.6 us (19%)
  matrix products  54.6 us (11%)
  starting transfers between devices  30.3 us (6%)
    all_to_all x1, blocking collectives, local(): lax.all_to_all(renewed.reshape(all_comps, rows_dev, lon_local), 'group',...  108 us
    all_to_all x1, waiting for transfers between devices, local(): lax.all_to_all(propagate(spectrum, flow_x, flow_y, sea_mask), 'group', sp...  95.8 us
    mul x6, other arithmetic, propagate(): combine(wave, padded[:, :, :-2], padded[:, :, 2:], rates) * sea_mask[None]  85.5 us
    slice x6, local copies, waits for them, and re-layouts, combine(): from_south = jnp.pad(centre[:, :-1], ((0, 0), (1, 0), (0, 0)))  73.7 us
    dot_general x1, matrix products, local(): mixed = jnp.dot(coupling, energy, precision=lax.Precision.HIGHEST)  46.4 us
    ppermute x6, starting transfers between devices, extended(): lax.ppermute(head, axis, [((i + 1) % count, i) for i in range(count)])  21.2 us
    unnamed x33, local copies, waits for them, and re-layouts  12.7 us
  transfers between devices with their start and end apart: 13, of which 1 were waited for; matrix products, arithmetic and copies ran while one was open for 17% of the time, Pallas kernels for 0%

commit v1 on v0

v1 whole, which is shorter than its diff:
```python
import math

import jax
import jax.numpy as jnp
from jax import lax
from jax.experimental import pallas as pl
from jax.experimental.pallas import tpu as pltpu
from jax.sharding import PartitionSpec as P


DIRS = 36
FREQ = 32
SUBSTEPS = 6
EDGE = 8
ROWS = 8
UNITS = 24
CHUNKS = (6, 6, 12)
STRIP_BLOCKS = 8
BAND = 4


def edge_strips(place, spectrum, turned_sea, base, made, block):
    _, lat, lon = spectrum.shape

    def kernel(place_ref, wave_ref, sea_ref, near_ref, far_ref, turned):
        step = pl.program_id(0)
        even = place_ref[1] == 0
        near = pl.multiple_of(jnp.where(even, lon - EDGE, 0), EDGE)
        far = pl.multiple_of(jnp.where(even, 0, lon - EDGE), EDGE)
        for b in range(block):
            turned[b] = wave_ref[b].T
            near_ref[step * block + b] = turned[b, pl.ds(near, EDGE)]
            far_ref[step * block + b] = turned[b, pl.ds(far, EDGE)]

        @pl.when(step == 0)
        def _():
            near_ref[made] = sea_ref[pl.ds(near, EDGE)]
            far_ref[made] = sea_ref[pl.ds(far, EDGE)]

    strip = pl.BlockSpec((made + 1, EDGE, lat), lambda i, *_: (0, 0, 0))
    shape = jax.ShapeDtypeStruct((made + 1, EDGE, lat), jnp.float32)
    first = base // block
    return pl.pallas_call(
        kernel,
        grid_spec=pltpu.PrefetchScalarGridSpec(
            num_scalar_prefetch=1,
            grid=(made // block,),
            in_specs=[
                pl.BlockSpec((block, lat, lon), lambda i, *_: (first + i, 0, 0)),
                pl.BlockSpec((lon, lat), lambda i, *_: (0, 0)),
            ],
            out_specs=[strip, strip],
            scratch_shapes=[pltpu.VMEM((block, lon, lat), jnp.float32)],
        ),
        out_shape=[shape, shape],
        cost_estimate=pl.CostEstimate(
            flops=0, bytes_accessed=8 * made * lat * lon, transcendentals=0
        ),
        name="edge_strips",
    )(place, spectrum, turned_sea)


def advance(tables, spectrum, strips, turned_sea, inverse, base, made, block, count, pieces):
    comps_dev, lat, lon = spectrum.shape
    rows_dev = sum(pieces)
    span = lon + EDGE
    tall = lon + 4 * EDGE
    lanes = 2 if block % 2 == 0 else 3 if block % 3 == 0 else 1
    north_row, south_row = 2 * EDGE + lon, EDGE

    def kernel(
        place_ref, kinds_ref, courant_ref, cos_ref, sin_ref,
        wave_ref, near_ref, far_ref, near_sea_ref, far_sea_ref, sea_ref, inverse_ref,
        *rest,
    ):
        outs, rest = rest[: len(pieces) * count], rest[len(pieces) * count :]
        sea, slope, side = rest[:3]
        sets = [rest[3 + 6 * q : 9 + 6 * q] for q in range(lanes)]
        step = pl.program_id(0)
        me = place_ref[0]
        even = place_ref[1] == 0
        near_row = pl.multiple_of(jnp.where(even, north_row, south_row), EDGE)
        far_row = pl.multiple_of(jnp.where(even, south_row, north_row), EDGE)

        @pl.when(step == 0)
        def _():
            for ping, pong, *_ in sets:
                ping[...] = jnp.zeros_like(ping)
                pong[...] = jnp.zeros_like(pong)
            sea[...] = jnp.zeros_like(sea)
            sea[2 * EDGE : 2 * EDGE + lon] = sea_ref[...]
            sea[pl.ds(near_row, EDGE)] = near_sea_ref[0]
            sea[pl.ds(far_row, EDGE)] = far_sea_ref[0]
            whole = sea[...]
            slope[...] = whole * inverse_ref[...]
            lane = lax.broadcasted_iota(jnp.int32, whole.shape, 1)
            side[0] = jnp.where(lane == 0, 0.0, whole)
            side[1] = jnp.where(lane == lat - 1, 0.0, whole)

        def some(i, carry):
            windows, upwinds, turns, heres = [], [], [], []
            for q, (ping, pong, keep, cross, along, result) in enumerate(sets):
                b = i * lanes + q
                kind = kinds_ref[me * comps_dev + base + step * block + b]
                speed = courant_ref[lax.div(kind, DIRS)]
                flow_x = speed * cos_ref[lax.rem(kind, DIRS)]
                flow_y = speed * sin_ref[lax.rem(kind, DIRS)]
                eastward = flow_x > 0.0
                northward = flow_y > 0.0
                first = pl.multiple_of(jnp.where(eastward, EDGE, 2 * EDGE), EDGE)
                windows.append(pl.ds(first, span))
                upwinds.append(pl.ds(jnp.where(eastward, EDGE - 1, 2 * EDGE + 1), span))
                turns.append(jnp.where(northward, 1, lat - 1))
                rate_x, rate_y = jnp.abs(flow_x), jnp.abs(flow_y)
                ratio = rate_x * slope[windows[q]]
                cross[...] = ratio
                along[...] = rate_y * side[jnp.where(northward, 0, 1), windows[q]]
                keep[...] = (1.0 - rate_y) * sea[windows[q]] - ratio
                ping[2 * EDGE : 2 * EDGE + lon] = wave_ref[b].T
                ping[pl.ds(near_row, EDGE)] = near_ref[b]
                ping[pl.ds(far_row, EDGE)] = far_ref[b]
            for q in range(lanes):
                heres.append(sets[q][0][windows[q]])
            for substep in range(SUBSTEPS):
                for q, (ping, pong, keep, cross, along, result) in enumerate(sets):
                    now, then = (ping, pong) if substep % 2 == 0 else (pong, ping)
                    heres[q] = (
                        keep[...] * heres[q]
                        + cross[...] * now[upwinds[q]]
                        + along[...] * pltpu.roll(heres[q], turns[q], 1)
                    )
                    then[windows[q]] = heres[q]
            for q, (ping, pong, keep, cross, along, result) in enumerate(sets):
                b = i * lanes + q
                last = ping if SUBSTEPS % 2 == 0 else pong
                result[...] = last[2 * EDGE : 2 * EDGE + lon].T
                offset = 0
                for p, rows in enumerate(pieces):
                    for k in range(count):
                        row = pl.multiple_of((me ^ k) * rows_dev + offset, ROWS)
                        outs[p * count + k][b] = result[pl.ds(row, rows)]
                    offset += rows
            return carry

        lax.fori_loop(0, block // lanes, some, 0)

    strip = pl.BlockSpec((block, EDGE, lat), lambda i, *_: (i, 0, 0))
    strip_of_sea = pl.BlockSpec((1, EDGE, lat), lambda i, *_: (made, 0, 0))
    fixed = lambda shape: pl.BlockSpec(shape, lambda i, *_: (0,) * len(shape))
    first_block = base // block
    f32 = lambda *shape: pltpu.VMEM(shape, jnp.float32)
    return pl.pallas_call(
        kernel,
        grid_spec=pltpu.PrefetchScalarGridSpec(
            num_scalar_prefetch=5,
            grid=(made // block,),
            in_specs=[
                pl.BlockSpec((block, lat, lon), lambda i, *_: (first_block + i, 0, 0)),
                strip,
                strip,
                strip_of_sea,
                strip_of_sea,
                fixed((lon, lat)),
                fixed((1, lat)),
            ],
            out_specs=[
                pl.BlockSpec((block, rows, lon), lambda i, *_: (i, 0, 0))
                for rows in pieces
                for _ in range(count)
            ],
            scratch_shapes=[f32(tall, lat), f32(tall, lat), f32(2, tall, lat)]
            + [
                f32(tall, lat), f32(tall, lat),
                f32(span, lat), f32(span, lat), f32(span, lat),
                f32(lat, lon),
            ] * lanes,
        ),
        out_shape=[
            jax.ShapeDtypeStruct((made, rows, lon), jnp.float32)
            for rows in pieces
            for _ in range(count)
        ],
        cost_estimate=pl.CostEstimate(
            flops=0, bytes_accessed=12 * made * lat * lon * 4, transcendentals=0
        ),
        name="advance",
    )(*tables, spectrum, *strips, *strips, turned_sea, inverse)


def couple(place, assignment, arrived, sea_rows, winds, per_kind, blocks, count, comps_dev, part):
    comps = assignment.shape[0]
    lon = sea_rows.shape[1]
    bands, band, _ = blocks[0].shape
    flat = [a for group, _ in arrived for a in group]
    sizes = [group[0].shape[0] for group, _ in arrived]
    unroll = 8 if all(size % 8 == 0 for size in sizes) else 6

    def kernel(place_ref, kinds_ref, *rest):
        ins, rest = rest[: len(flat)], rest[len(flat) :]
        sea_ref, wind_ref, weight_ref, east_ref, north_ref, decay_ref, high_ref, low_ref = rest[:8]
        outs, (sorted_ref,) = rest[8:-1], rest[-1:]
        me = place_ref[0]
        for k in range(count):
            for g in range(len(arrived)):
                first = (me ^ k) * comps_dev + sum(sizes[:g])
                source = ins[g * count + k]

                def put(i, carry, source=source, first=first):
                    rows = [i * unroll + u for u in range(unroll)]
                    kinds = [kinds_ref[first + c] for c in rows]
                    values = [source[c] for c in rows]
                    for kind, value in zip(kinds, values):
                        sorted_ref[pl.ds(kind, ROWS, stride=comps), :] = value
                    return carry

                lax.fori_loop(0, sizes[g] // unroll, put, 0)

        def pair(p, carry):
            starts = [pl.multiple_of((2 * p + q) * comps, 8) for q in range(2)]
            loads, us, vs, seas = [], [], [], []
            for q in range(2):
                j = 2 * p + q
                total = jnp.sum(
                    weight_ref[...] * sorted_ref[pl.ds(starts[q], comps), :], axis=0, keepdims=True
                )
                loading = total / comps
                loads.append(loading / (1.0 + loading))
                us.append(wind_ref[0, pl.ds(j, 1), :])
                vs.append(wind_ref[1, pl.ds(j, 1), :])
                seas.append(sea_ref[pl.ds(j, 1), :])
            for n in range(bands):
                kinds = slice(n * band, (n + 1) * band)
                spots = [pl.ds(pl.multiple_of(starts[q] + n * band, 8), band) for q in range(2)]
                energy = [sorted_ref[spots[q], :] for q in range(2)]
                both = jnp.concatenate(energy, axis=1)
                high = both.astype(jnp.bfloat16)
                low = (both - high.astype(jnp.float32)).astype(jnp.bfloat16)
                dot = lambda a, b: jnp.dot(a, b, preferred_element_type=jnp.float32)
                mixed = dot(high_ref[n], high) + (dot(high_ref[n], low) + dot(low_ref[n], high))
                for q in range(2):
                    drive = east_ref[kinds, :] * us[q] + north_ref[kinds, :] * vs[q]
                    exponent = jnp.maximum(drive, 0.0) - decay_ref[kinds, :] * loads[q]
                    sorted_ref[spots[q], :] = seas[q] * (
                        energy[q] * jnp.exp(exponent) + mixed[:, q * lon : (q + 1) * lon]
                    )
            return carry

        lax.fori_loop(0, ROWS // 2, pair, 0)
        step = 8 if comps_dev % 8 == 0 else 6
        for k in range(count):

            def take(i, carry, k=k):
                rows = [i * step + u for u in range(step)]
                kinds = [kinds_ref[(me ^ k) * comps_dev + c] for c in rows]
                values = [sorted_ref[pl.ds(kind, ROWS, stride=comps), :] for kind in kinds]
                for c, value in zip(rows, values):
                    outs[k][c] = value
                return carry

            lax.fori_loop(0, comps_dev // step, take, 0)

    vmem = pl.BlockSpec(memory_space=pltpu.VMEM)
    pieces = [
        pl.BlockSpec((a.shape[0], ROWS, lon), lambda *_, at=at: (0, at, 0))
        for group, at in arrived
        for a in group
    ]
    rows = pl.BlockSpec((ROWS, lon), lambda *_: (part, 0))
    wind_rows = pl.BlockSpec((2, ROWS, lon), lambda *_: (0, part, 0))
    return pl.pallas_call(
        kernel,
        grid_spec=pltpu.PrefetchScalarGridSpec(
            num_scalar_prefetch=2,
            grid=(1,),
            in_specs=pieces + [rows, wind_rows] + [vmem] * 6,
            out_specs=[vmem] * count,
            scratch_shapes=[pltpu.VMEM((ROWS * comps, lon), jnp.float32)],
        ),
        out_shape=[jax.ShapeDtypeStruct((comps_dev, ROWS, lon), jnp.float32)] * count,
        cost_estimate=pl.CostEstimate(
            flops=0, bytes_accessed=8 * comps * ROWS * lon * 4, transcendentals=0
        ),
        name="couple",
    )(place, assignment, *flat, sea_rows, winds, *per_kind, *blocks)


def settle(place, returned, ks, part, rows_dev, lat, partial):
    comps_dev, _, lon = returned[0].shape
    amount = len(ks)

    def kernel(place_ref, *rest):
        ins, out_ref, (held, in_sem, out_sem) = rest[:amount], rest[-4], rest[-3:]
        me = place_ref[0]
        into = [
            pltpu.make_async_copy(ins[n], held.at[n], in_sem.at[n]) for n in range(amount)
        ]
        for copy in into:
            copy.start()
        out = []
        for n, k in enumerate(ks):
            row = pl.multiple_of((me ^ k) * rows_dev + part * ROWS, ROWS)
            into[n].wait()
            out.append(
                pltpu.make_async_copy(
                    held.at[n], out_ref.at[:, pl.ds(row, ROWS), :], out_sem.at[n]
                )
            )
            out[n].start()
        for copy in out:
            copy.wait()

    anywhere = pl.BlockSpec(memory_space=pl.ANY)
    extra = [] if partial is None else [partial]
    return pl.pallas_call(
        kernel,
        grid_spec=pltpu.PrefetchScalarGridSpec(
            num_scalar_prefetch=1,
            grid=(),
            in_specs=[anywhere] * (amount + len(extra)),
            out_specs=anywhere,
            scratch_shapes=[
                pltpu.VMEM((amount, comps_dev, ROWS, lon), jnp.float32),
                pltpu.SemaphoreType.DMA((amount,)),
                pltpu.SemaphoreType.DMA((amount,)),
            ],
        ),
        out_shape=jax.ShapeDtypeStruct((comps_dev, lat, lon), jnp.float32),
        input_output_aliases={1 + amount: 0} if extra else {},
        cost_estimate=pl.CostEstimate(
            flops=0, bytes_accessed=2 * amount * comps_dev * ROWS * lon * 4, transcendentals=0
        ),
        name="settle",
    )(place, *[returned[k] for k in ks], *extra)


def order_of(count):
    return sorted(range(1, count), key=lambda k: (k == 1, k & 1, k))


def swap(pieces, count):
    made = [pieces[0]] + [None] * (count - 1)
    for k in order_of(count):
        made[k] = lax.ppermute(pieces[k], "group", [(i, i ^ k) for i in range(count)])
    return made


def exchange(near, far):
    count = lax.axis_size("sector")
    pairs = [(i, i ^ 1) for i in range(count)]
    near = lax.ppermute(near, "sector", pairs)
    pairs = [(i, (i + 1) % count if i % 2 else (i - 1) % count) for i in range(count)]
    far = lax.ppermute(far, "sector", pairs)
    return near, far


def local(spectrum, land_mask, wind_field, assignment, courant, growth, whitecap, weights, spread):
    member = lax.axis_index("group").astype(jnp.int32)
    count = lax.axis_size("group")
    comps_dev, lat, lon = spectrum.shape
    comps = assignment.shape[0]
    rows_dev = wind_field.shape[1]
    parts = rows_dev // ROWS
    unit = comps_dev // UNITS
    parity = lax.axis_index("sector").astype(jnp.int32) % 2
    place = jnp.stack((member, parity))

    angles = (jnp.arange(DIRS).astype(jnp.float32) + 0.5) * (2.0 * math.pi / DIRS)
    cosine, sine = jnp.cos(angles), jnp.sin(angles)
    latitude = (jnp.arange(lat).astype(jnp.float32) + 0.5 - lat / 2) * (math.pi / 2160.0)
    inverse = (1.0 / jnp.cos(latitude))[None, :]
    sea_mask = land_mask.astype(jnp.float32)
    turned = sea_mask.T
    tables = (place, assignment, courant, cosine, sine)

    arrived = [[] for _ in range(parts)]
    base = 0
    for c, units in enumerate(CHUNKS):
        made = units * unit
        near, far = edge_strips(
            place, spectrum, turned, base, made, comps_dev // STRIP_BLOCKS
        )
        strips = exchange(near, far)
        pieces = [ROWS] * parts if c == len(CHUNKS) - 1 else [rows_dev]
        sent = advance(tables, spectrum, strips, turned, inverse, base, made, unit, count, pieces)
        for p in range(len(pieces)):
            group = swap(sent[p * count : (p + 1) * count], count)
            for part in range(parts):
                if len(pieces) == 1:
                    arrived[part].append((group, part))
                elif p == part:
                    arrived[part].append((group, 0))
        base += made

    def spread_out(values):
        return jnp.broadcast_to(values[:, None], (comps, lon))

    fast = jnp.repeat(growth, DIRS)
    per_kind = (
        spread_out(jnp.repeat(weights, DIRS)),
        spread_out(fast * jnp.tile(cosine, FREQ)),
        spread_out(fast * jnp.tile(sine, FREQ)),
        spread_out(jnp.repeat(whitecap, DIRS)),
    )
    halves = (0.5 * spread).reshape(FREQ // BAND, BAND, DIRS, 1, DIRS)
    same = jnp.eye(BAND, dtype=jnp.float32)[None, :, None, :, None]
    whole = (halves * same).reshape(FREQ // BAND, BAND * DIRS, BAND * DIRS)
    high = lax.reduce_precision(whole, 8, 7)
    blocks = (high.astype(jnp.bfloat16), (whole - high).astype(jnp.bfloat16))
    sea_rows = lax.dynamic_slice_in_dim(sea_mask, member * rows_dev, rows_dev, 0)

    returned = []
    for part in range(parts):
        made = couple(
            place, assignment, arrived[part], sea_rows, wind_field, per_kind, blocks,
            count, comps_dev, part,
        )
        returned.append(swap(made, count))
    order = [0] + order_of(count)
    out = None
    for part in range(parts):
        cut = count if part < parts - 1 else (3 * count) // 4
        for ks in (order[:cut], order[cut:]):
            if ks:
                out = settle(place, returned[part], ks, part, rows_dev, lat, out)
    return out


def solution(mesh):
    in_specs = (
        P("group", None, "sector"),
        P(None, "sector"),
        P(None, "group", "sector"),
        P(),
        P(),
        P(),
        P(),
        P(),
        P(),
    )
    out_specs = P("group", None, "sector")
    return jax.shard_map(local, mesh=mesh, in_specs=in_specs, out_specs=out_specs, check_vma=False)
```

time: 503 us -> 337 us (0.67); the launches traced: 495 us -> 336 us
  Pallas kernels: 0 us -> 120 us
  blocking collectives: 108 us -> 0 us
  local copies, waits for them, and re-layouts: 112 us -> 13.6 us
  other arithmetic: 93.6 us -> 6.86 us
  matrix products: 54.6 us -> 0 us
  waiting for transfers between devices: 95.8 us -> 138 us
  starting transfers between devices: 30.3 us -> 57.3 us
    ppermute x12 -> x48, waiting for transfers between devices: 0.03 us -> 138 us  [the longest x42 131 us: swap(): lax.ppermute(pieces[k], 'group', [(i, i ^ k) for i in range(count)])]
    pallas_call x0 -> x11, Pallas kernels: none -> 120 us  [the longest x3 57.3 us: advance(): pl.pallas_call(kernel, grid_spec=pltpu.PrefetchScalarGridSpec(num_scalar_...]
    all_to_all x1 -> x0, blocking collectives: 108 us -> none  [local(): lax.all_to_all(renewed.reshape(all_comps, rows_dev, lon_local), 'group',...]
    all_to_all x1 -> x0, waiting for transfers between devices: 95.8 us -> none  [local(): lax.all_to_all(propagate(spectrum, flow_x, flow_y, sea_mask), 'group', sp...]
    mul x7 -> x2, other arithmetic: 85.5 us -> 1.38 us  [the longest x1 1.33 us: local(): fast * jnp.tile(sine, FREQ)]
    slice x13 -> x0, local copies, waits for them, and re-layouts: 77.5 us -> none  [the longest x6 73.7 us: combine(): from_south = jnp.pad(centre[:, :-1], ((0, 0), (1, 0), (0, 0)))]
    dot_general x5 -> x0, matrix products: 54.6 us -> none  [the longest x1 46.4 us: local(): mixed = jnp.dot(coupling, energy, precision=lax.Precision.HIGHEST)]
    ppermute x12 -> x48, starting transfers between devices: 24.6 us -> 57.3 us  [the longest x42 46.8 us: swap(): lax.ppermute(pieces[k], 'group', [(i, i ^ k) for i in range(count)])]
  transfers between devices with their start and end apart: 13 -> 48, of which waited for: 1 -> 16; matrix products, arithmetic and copies ran while one was open for 17% -> 5% of each run, Pallas kernels for 0% -> 34%
where the time goes in v1:
time: 337 us; the launch traced here: 336 us
  waiting for transfers between devices  138 us (41%)
  Pallas kernels  120 us (36%)
  starting transfers between devices  57.3 us (17%)
  local copies, waits for them, and re-layouts  13.6 us (4%)
  other arithmetic  6.86 us (2%)
    ppermute x42, waiting for transfers between devices, swap(): lax.ppermute(pieces[k], 'group', [(i, i ^ k) for i in range(count)])  131 us
    pallas_call x3, Pallas kernels, advance(): pl.pallas_call(kernel, grid_spec=pltpu.PrefetchScalarGridSpec(num_scalar_...  57.3 us
    ppermute x42, starting transfers between devices, swap(): lax.ppermute(pieces[k], 'group', [(i, i ^ k) for i in range(count)])  46.8 us
    pallas_call x2, Pallas kernels, couple(): pl.pallas_call(kernel, grid_spec=pltpu.PrefetchScalarGridSpec(num_scalar_...  39.6 us
    pallas_call x3, Pallas kernels, edge_strips(): pl.pallas_call(kernel, grid_spec=pltpu.PrefetchScalarGridSpec(num_scalar_...  12.3 us
    pallas_call x3, Pallas kernels, settle(): pl.pallas_call(kernel, grid_spec=pltpu.PrefetchScalarGridSpec(num_scalar_...  11.2 us
  transfers between devices with their start and end apart: 48, of which 16 were waited for; matrix products, arithmetic and copies ran while one was open for 5% of the time, Pallas kernels for 34%

profile of v1, /device:TPU:0, one launch (start us, length us, event | category | flops | bytes accessed | tf_op | source)
XLA Modules:
  0.0 336.1 jit_solution(14334326520999197730)
XLA Ops:
  0.0 1.5 fusion.4
  2.7 3.4 %edge_strips.3 = (f32[37,8,128]{2,1,0:T(8,128)}, f32[37,8,128]{2,1,0:T(8,128)}) custom-call(s32[2]{0:T(128)} %pad_add_fusion.place_ref, f32[144,128,128]{2,1,0:T(8,128)} %wave_ref.11, f32[128,128]{1,0:T(8,128)} %copy.12.sea_ref), custom_call_target="tpu_custom_call" | custom-call | bytes 4718592 | tf_op jit(solution)/shard_map/edge_strips/pallas_call | solution.py:43
  6.2 3.1 collective-permute-start
  9.2 2.5 collective-permute-start.1
  11.7 5.3 %edge_strips.5 = (f32[73,8,128]{2,1,0:T(8,128)}, f32[73,8,128]{2,1,0:T(8,128)}) custom-call(s32[2]{0:T(128)} %pad_add_fusion.place_ref, f32[144,128,128]{2,1,0:T(8,128)} %wave_ref.11, f32[128,128]{1,0:T(8,128)} %copy.12.sea_ref), custom_call_target="tpu_custom_call" | custom-call | bytes 9437184 | tf_op jit(solution)/shard_map/edge_strips/pallas_call | solution.py:43
  17.6 0.9 collective-permute-start.19
  20.5 14.8 %advance.3 = (f32[36,16,128]{2,1,0:T(8,128)}, f32[36,16,128]{2,1,0:T(8,128)}, f32[36,16,128]{2,1,0:T(8,128)}, f32[36,16,128]{2,1,0:T(8,128)}, f32[36,16,128]{2,1...) custom-call(s32[2]{0:T(128)} %pad_add_fusion.place_ref, s32[1152]{0:T(1024)} %kinds_ref.9, ...), custom_call_target="tpu_custom_call" | custom-call | bytes 28311552 | tf_op jit(solution)/shard_map/advance/pallas_call | solution.py:152
  35.4 3.6 %edge_strips.4 = (f32[37,8,128]{2,1,0:T(8,128)}, f32[37,8,128]{2,1,0:T(8,128)}) custom-call(s32[2]{0:T(128)} %pad_add_fusion.place_ref, f32[144,128,128]{2,1,0:T(8,128)} %wave_ref.11, f32[128,128]{1,0:T(8,128)} %copy.12.sea_ref), custom_call_target="tpu_custom_call" | custom-call | bytes 4718592 | tf_op jit(solution)/shard_map/edge_strips/pallas_call | solution.py:43
  39.0 0.9 collective-permute-start.9
  39.9 2.5 collective-permute-start.10
  42.4 3.0 collective-permute-done.9.near_ref.near_sea_ref
  45.4 1.5 collective-permute-start.3
  46.9 3.2 collective-permute-done.10.far_ref.far_sea_ref
  50.7 1.6 collective-permute-start.5
  52.3 0.9 collective-permute-start.6
  53.2 1.6 collective-permute-start.7
  54.8 14.8 %advance.4 = (f32[36,16,128]{2,1,0:T(8,128)}, f32[36,16,128]{2,1,0:T(8,128)}, f32[36,16,128]{2,1,0:T(8,128)}, f32[36,16,128]{2,1,0:T(8,128)}, f32[36,16,128]{2,1...) custom-call(s32[2]{0:T(128)} %pad_add_fusion.place_ref, s32[1152]{0:T(1024)} %kinds_ref.9, ...), custom_call_target="tpu_custom_call" | custom-call | bytes 28311552 | tf_op jit(solution)/shard_map/advance/pallas_call | solution.py:152
  69.7 0.8 collective-permute-start.8
  70.5 0.8 collective-permute-start.11
  71.9 1.4 collective-permute-done.6.rest_5_
  73.3 7.9 %collective-permute-start.14 = (f32[36,16,128]{2,1,0:T(8,128)}, f32[36,16,128]{2,1,0:T(8,128)S(1)}, u32[]{:S(2)}, u32[]{:S(2)}) collective-permute-start(f32[36,16,128]{2,1,0:T(8,128)} %get-tuple-element.75), channel_id=1, source_target_pairs={{0,4},{1,5},{2,6},{3,7},{4,0},{5,1},{6,2},{7,3},{8,12},{9,13},{10,... | collective-permute-start | bytes 884744 | tf_op jit(solution)/shard_map/ppermute | solution.py:343
  81.3 27.7 %advance.5 = (f32[72,8,128]{2,1,0:T(8,128)}, f32[72,8,128]{2,1,0:T(8,128)}, f32[72,8,128]{2,1,0:T(8,128)}, f32[72,8,128]{2,1,0:T(8,128)}, f32[72,8,128]{2,1,0:T(...) custom-call(s32[2]{0:T(128)} %pad_add_fusion.place_ref, ...), custom_call_target="tpu_custom_call" | custom-call | bytes 56623104 | tf_op jit(solution)/shard_map/advance/pallas_call | solution.py:152
  109.1 2.9 collective-permute-start.16
  112.7 1.3 broadcast_multiply_fusion.1
  114.0 17.2 %collective-permute-done.15.rest_13_ = f32[36,16,128]{2,1,0:T(8,128)S(1)} collective-permute-done((f32[36,16,128]{2,1,0:T(8,128)}, f32[36,16,128]{2,1,0:T(8,128)S(1)}, u32[]{:S(2)}, u32[]{:S(2)}) %collective-permute-start.15) | collective-permute-done | bytes 294944 | tf_op jit(solution)/shard_map/ppermute | solution.py:343
  131.2 1.4 collective-permute-start.35
  132.7 2.0 collective-permute-start.38
  134.7 1.2 collective-permute-start.39
  135.9 1.3 constant_dynamic-slice_fusion.rest_24_
  137.2 4.2 %collective-permute-done.35.rest_18_ = f32[72,8,128]{2,1,0:T(8,128)} collective-permute-done((f32[72,8,128]{2,1,0:T(8,128)}, f32[72,8,128]{2,1,0:T(8,128)}, u32[]{:S(2)}, u32[]{:S(2)}) %collective-permute-start.35) | collective-permute-done | bytes 294944 | tf_op jit(solution)/shard_map/ppermute | solution.py:343
  141.4 1.4 collective-permute-start.21
  142.8 3.8 %collective-permute-done.36.rest_19_ = f32[72,8,128]{2,1,0:T(8,128)} collective-permute-done((f32[72,8,128]{2,1,0:T(8,128)}, f32[72,8,128]{2,1,0:T(8,128)}, u32[]{:S(2)}, u32[]{:S(2)}) %collective-permute-start.36) | collective-permute-done | bytes 294944 | tf_op jit(solution)/shard_map/ppermute | solution.py:343
  146.6 2.2 collective-permute-start.22
  148.8 6.1 %collective-permute-done.38.rest_21_ = f32[72,8,128]{2,1,0:T(8,128)} collective-permute-done((f32[72,8,128]{2,1,0:T(8,128)}, f32[72,8,128]{2,1,0:T(8,128)}, u32[]{:S(2)}, u32[]{:S(2)}) %collective-permute-start.38) | collective-permute-done | bytes 294944 | tf_op jit(solution)/shard_map/ppermute | solution.py:343
  155.2 2.2 collective-permute-start.40
  158.4 1.4 mul.103
  159.8 1.4 mul.101
  161.4 0.8 mul.110
  163.0 1.0 mul.108
  164.0 2.2 fusion
  166.3 4.9 %collective-permute-done.40.rest_23_ = f32[72,8,128]{2,1,0:T(8,128)} collective-permute-done((f32[72,8,128]{2,1,0:T(8,128)}, f32[72,8,128]{2,1,0:T(8,128)}, u32[]{:S(2)}, u32[]{:S(2)}) %collective-permute-start.40) | collective-permute-done | bytes 294944 | tf_op jit(solution)/shard_map/ppermute | solution.py:343
  171.2 2.7 collective-permute-start.25
  173.9 1.0 broadcast_in_dim.41.rest_27_
  174.9 1.0 broadcast_in_dim.42.rest_28_
  176.0 1.0 broadcast_in_dim.39.rest_26_
  177.0 1.0 broadcast_in_dim.45.rest_29_
  178.0 19.9 %couple.3 = (f32[144,8,128]{2,1,0:T(8,128)}, f32[144,8,128]{2,1,0:T(8,128)}, f32[144,8,128]{2,1,0:T(8,128)}, f32[144,8,128]{2,1,0:T(8,128)}, f32[144,8,128]{2,1,...) custom-call(s32[2]{0:T(128)} %pad_add_fusion.place_ref, s32[1152]{0:T(1024)} %kinds_ref.9, ...), custom_call_target="tpu_custom_call" | custom-call | bytes 37748736 | tf_op jit(solution)/shard_map/couple/pallas_call | solution.py:270
  198.9 2.7 collective-permute-start.43
  201.6 1.6 collective-permute-start.26
  203.2 41.1 %collective-permute-done.26.rest_23_ = f32[72,8,128]{2,1,0:T(8,128)S(1)} collective-permute-done((f32[72,8,128]{2,1,0:T(8,128)S(1)}, f32[72,8,128]{2,1,0:T(8,128)S(1)}, u32[]{:S(2)}, u32[]{:S(2)}) %collective-permute-start.26) | collective-permute-done | bytes 294944 | tf_op jit(solution)/shard_map/ppermute | solution.py:343
  244.2 2.0 collective-permute-start.45
  246.3 19.7 %couple.2 = (f32[144,8,128]{2,1,0:T(8,128)}, f32[144,8,128]{2,1,0:T(8,128)}, f32[144,8,128]{2,1,0:T(8,128)}, f32[144,8,128]{2,1,0:T(8,128)}, f32[144,8,128]{2,1,...) custom-call(s32[2]{0:T(128)} %pad_add_fusion.place_ref, s32[1152]{0:T(1024)} %kinds_ref.9, ...), custom_call_target="tpu_custom_call" | custom-call | bytes 37748736 | tf_op jit(solution)/shard_map/couple/pallas_call | solution.py:270
  266.0 0.8 collective-permute-start.46
  266.9 1.4 collective-permute-start.29
  268.3 1.4 collective-permute-start.30
  270.4 12.3 %collective-permute-done.46.rest_6_ = f32[144,8,128]{2,1,0:T(8,128)S(1)} collective-permute-done((f32[144,8,128]{2,1,0:T(8,128)}, f32[144,8,128]{2,1,0:T(8,128)S(1)}, u32[]{:S(2)}, u32[]{:S(2)}) %collective-permute-start.46) | collective-permute-done | bytes 589856 | tf_op jit(solution)/shard_map/ppermute | solution.py:343
  283.6 11.7 %collective-permute-done.29.rest_1_ = f32[144,8,128]{2,1,0:T(8,128)S(1)} collective-permute-done((f32[144,8,128]{2,1,0:T(8,128)}, f32[144,8,128]{2,1,0:T(8,128)S(1)}, u32[]{:S(2)}, u32[]{:S(2)}) %collective-permute-start.29) | collective-permute-done | bytes 589856 | tf_op jit(solution)/shard_map/ppermute | solution.py:343
  296.6 4.8 %settle.3.rest_6_ = f32[144,128,128]{2,1,0:T(8,128)} custom-call(s32[2]{0:T(128)} %pad_add_fusion.place_ref, f32[144,8,128]{2,1,0:T(8,128)} %get-tuple-element.105.rest_0_, f32[144,8,128]{2,1,0:T(8,128)} %copy-done.20, f32[144,8,128]{2,1,0:T(8,128)} %copy-done.21, f32[144,8,128]{2,1,0:T(8,128)} %copy-done.22, f32[144,8,128]{2,1,0:T(8,128)} %copy-done.23, ...), custom_call_target="tpu_custom_call" | custom-call | bytes 9437184 | tf_op jit(solution)/shard_map/settle/pallas_call | solution.py:314
  301.4 7.1 %collective-permute-done.31.rest_3_ = f32[144,8,128]{2,1,0:T(8,128)} collective-permute-done((f32[144,8,128]{2,1,0:T(8,128)}, f32[144,8,128]{2,1,0:T(8,128)}, u32[]{:S(2)}, u32[]{:S(2)}) %collective-permute-start.31) | collective-permute-done | bytes 589856 | tf_op jit(solution)/shard_map/ppermute | solution.py:343
  308.5 10.9 %collective-permute-done.32.rest_4_ = f32[144,8,128]{2,1,0:T(8,128)} collective-permute-done((f32[144,8,128]{2,1,0:T(8,128)}, f32[144,8,128]{2,1,0:T(8,128)}, u32[]{:S(2)}, u32[]{:S(2)}) %collective-permute-start.32) | collective-permute-done | bytes 589856 | tf_op jit(solution)/shard_map/ppermute | solution.py:343
  319.4 1.4 collective-permute-done.33.rest_5_
  320.8 3.6 %settle.4.rest_2_ = f32[144,128,128]{2,1,0:T(8,128)} custom-call(s32[2]{0:T(128)} %pad_add_fusion.place_ref, f32[144,8,128]{2,1,0:T(8,128)} %get-tuple-element.91.rest_0_, f32[144,8,128]{2,1,0:T(8,128)} %copy-done.25, f32[144,8,128]{2,1,0:T(8,128)} %collective-permute-done.30.rest_2_, ...), custom_call_target="tpu_custom_call", output_to_operand_aliasing={{}: (7, {})} | custom-call | bytes 7077888 | tf_op jit(solution)/shard_map/settle/pallas_call | solution.py:314
  324.4 8.9 %collective-permute-done.27.rest_0_ = f32[144,8,128]{2,1,0:T(8,128)} collective-permute-done((f32[144,8,128]{2,1,0:T(8,128)}, f32[144,8,128]{2,1,0:T(8,128)}, u32[]{:S(2)}, u32[]{:S(2)}) %collective-permute-start.27) | collective-permute-done | bytes 589856 | tf_op jit(solution)/shard_map/ppermute | solution.py:343
  333.4 2.8 settle.5
  (152 shorter events, 12.2 us)
Async XLA Ops:
  6.2 13.6 %collective-permute-start = (f32[37,8,128]{2,1,0:T(8,128)}, f32[37,8,128]{2,1,0:T(8,128)S(1)}, u32[]{:S(2)}, u32[]{:S(2)}) collective-permute-start(f32[37,8,128]{2,1,0:T(8,128)} %get-tuple-element.59), channel_id=1, source_target_pairs={{0,8},{8,0},{16,24},{24,16},{1,9},{9,1},{17,25},{25,17},{2,10},{10... | collective-permute-start | bytes 454664 | tf_op jit(solution)/shard_map/ppermute | solution.py:350
  9.2 10.5 %collective-permute-start.1 = (f32[37,8,128]{2,1,0:T(8,128)}, f32[37,8,128]{2,1,0:T(8,128)S(1)}, u32[]{:S(2)}, u32[]{:S(2)}) collective-permute-start(f32[37,8,128]{2,1,0:T(8,128)} %get-tuple-element.60), channel_id=1, source_target_pairs={{0,24},{8,16},{16,8},{24,0},{1,25},{9,17},{17,9},{25,1},{2,26},{10... | collective-permute-start | bytes 454664 | tf_op jit(solution)/shard_map/ppermute | solution.py:352
  17.0 33.7 %collective-permute-start.18 = (f32[73,8,128]{2,1,0:T(8,128)}, f32[73,8,128]{2,1,0:T(8,128)S(1)}, u32[]{:S(2)}, u32[]{:S(2)}) collective-permute-start(f32[73,8,128]{2,1,0:T(8,128)} %get-tuple-element.79), channel_id=1, source_target_pairs={{0,8},{8,0},{16,24},{24,16},{1,9},{9,1},{17,25},{25,17},{2,10},{10... | collective-permute-start | bytes 897032 | tf_op jit(solution)/shard_map/ppermute | solution.py:350
  17.6 34.7 %collective-permute-start.19 = (f32[73,8,128]{2,1,0:T(8,128)}, f32[73,8,128]{2,1,0:T(8,128)S(1)}, u32[]{:S(2)}, u32[]{:S(2)}) collective-permute-start(f32[73,8,128]{2,1,0:T(8,128)} %get-tuple-element.80), channel_id=1, source_target_pairs={{0,24},{8,16},{16,8},{24,0},{1,25},{9,17},{17,9},{25,1},{2,26},{10... | collective-permute-start | bytes 897032 | tf_op jit(solution)/shard_map/ppermute | solution.py:352
  35.4 17.9 %collective-permute-start.2 = (f32[36,16,128]{2,1,0:T(8,128)}, f32[36,16,128]{2,1,0:T(8,128)S(1)}, u32[]{:S(2)}, u32[]{:S(2)}) collective-permute-start(f32[36,16,128]{2,1,0:T(8,128)} %get-tuple-element.62), channel_id=1, source_target_pairs={{0,1},{1,0},{2,3},{3,2},{4,5},{5,4},{6,7},{7,6},{8,9},{9,8},{10,11... | collective-permute-start | bytes 884744 | tf_op jit(solution)/shard_map/ppermute | solution.py:343
  39.0 6.4 %collective-permute-start.9 = (f32[37,8,128]{2,1,0:T(8,128)}, f32[37,8,128]{2,1,0:T(8,128)S(1)}, u32[]{:S(2)}, u32[]{:S(2)}) collective-permute-start(f32[37,8,128]{2,1,0:T(8,128)} %get-tuple-element.69), channel_id=1, source_target_pairs={{0,8},{8,0},{16,24},{24,16},{1,9},{9,1},{17,25},{25,17},{2,10},{10... | collective-permute-start | bytes 454664 | tf_op jit(solution)/shard_map/ppermute | solution.py:350
  39.9 10.2 %collective-permute-start.10 = (f32[37,8,128]{2,1,0:T(8,128)}, f32[37,8,128]{2,1,0:T(8,128)S(1)}, u32[]{:S(2)}, u32[]{:S(2)}) collective-permute-start(f32[37,8,128]{2,1,0:T(8,128)} %get-tuple-element.70), channel_id=1, source_target_pairs={{0,24},{8,16},{16,8},{24,0},{1,25},{9,17},{17,9},{25,1},{2,26},{10... | collective-permute-start | bytes 454664 | tf_op jit(solution)/shard_map/ppermute | solution.py:352
  45.4 24.3 %collective-permute-start.3 = (f32[36,16,128]{2,1,0:T(8,128)}, f32[36,16,128]{2,1,0:T(8,128)S(1)}, u32[]{:S(2)}, u32[]{:S(2)}) collective-permute-start(f32[36,16,128]{2,1,0:T(8,128)} %get-tuple-element.63), channel_id=1, source_target_pairs={{0,2},{1,3},{2,0},{3,1},{4,6},{5,7},{6,4},{7,5},{8,10},{9,11},{10,... | collective-permute-start | bytes 884744 | tf_op jit(solution)/shard_map/ppermute | solution.py:343
  50.1 20.4 %collective-permute-start.4 = (f32[36,16,128]{2,1,0:T(8,128)}, f32[36,16,128]{2,1,0:T(8,128)S(1)}, u32[]{:S(2)}, u32[]{:S(2)}) collective-permute-start(f32[36,16,128]{2,1,0:T(8,128)} %get-tuple-element.64), channel_id=1, source_target_pairs={{0,3},{1,2},{2,1},{3,0},{4,7},{5,6},{6,5},{7,4},{8,11},{9,10},{10,... | collective-permute-start | bytes 884744 | tf_op jit(solution)/shard_map/ppermute | solution.py:343
  50.7 20.7 %collective-permute-start.5 = (f32[36,16,128]{2,1,0:T(8,128)S(1)}, f32[36,16,128]{2,1,0:T(8,128)S(1)}, u32[]{:S(2)}, u32[]{:S(2)}) collective-permute-start(f32[36,16,128]{2,1,0:T(8,128)S(1)} %copy-done.41), channel_id=1, source_target_pairs={{0,4},{1,5},{2,6},{3,7},{4,0},{5,1},{6,2},{7,3},{8,12},{9,13},{10,... | collective-permute-start | bytes 884744 | tf_op jit(solution)/shard_map/ppermute | solution.py:343
  52.3 20.9 %collective-permute-start.6 = (f32[36,16,128]{2,1,0:T(8,128)S(1)}, f32[36,16,128]{2,1,0:T(8,128)S(1)}, u32[]{:S(2)}, u32[]{:S(2)}) collective-permute-start(f32[36,16,128]{2,1,0:T(8,128)S(1)} %copy-done.40), channel_id=1, source_target_pairs={{0,5},{1,4},{2,7},{3,6},{4,1},{5,0},{6,3},{7,2},{8,13},{9,12},{10,... | collective-permute-start | bytes 884744 | tf_op jit(solution)/shard_map/ppermute | solution.py:343
  53.2 20.1 %collective-permute-start.7 = (f32[36,16,128]{2,1,0:T(8,128)S(1)}, f32[36,16,128]{2,1,0:T(8,128)S(1)}, u32[]{:S(2)}, u32[]{:S(2)}) collective-permute-start(f32[36,16,128]{2,1,0:T(8,128)S(1)} %copy-done.39), channel_id=1, source_target_pairs={{0,6},{1,7},{2,4},{3,5},{4,2},{5,3},{6,0},{7,1},{8,14},{9,15},{10,... | collective-permute-start | bytes 884744 | tf_op jit(solution)/shard_map/ppermute | solution.py:343
  69.7 39.2 %copy-start.3 = (f32[36,16,128]{2,1,0:T(8,128)}, f32[36,16,128]{2,1,0:T(8,128)S(1)}, u32[]{:S(2)}) copy-start(f32[36,16,128]{2,1,0:T(8,128)S(1)} %collective-permute-done.3.rest_2_) | copy-start | bytes 884740
  69.7 39.3 %collective-permute-start.8 = (f32[36,16,128]{2,1,0:T(8,128)}, f32[36,16,128]{2,1,0:T(8,128)S(1)}, u32[]{:S(2)}, u32[]{:S(2)}) collective-permute-start(f32[36,16,128]{2,1,0:T(8,128)} %get-tuple-element.68), channel_id=1, source_target_pairs={{0,7},{1,6},{2,5},{3,4},{4,3},{5,2},{6,1},{7,0},{8,15},{9,14},{10,... | collective-permute-start | bytes 884744 | tf_op jit(solution)/shard_map/ppermute | solution.py:343
  70.5 38.4 %copy-start.4 = (f32[36,16,128]{2,1,0:T(8,128)}, f32[36,16,128]{2,1,0:T(8,128)S(1)}, u32[]{:S(2)}) copy-start(f32[36,16,128]{2,1,0:T(8,128)S(1)} %collective-permute-done.4.rest_3_) | copy-start | bytes 884740
  70.5 38.6 %collective-permute-start.11 = (f32[36,16,128]{2,1,0:T(8,128)}, f32[36,16,128]{2,1,0:T(8,128)S(1)}, u32[]{:S(2)}, u32[]{:S(2)}) collective-permute-start(f32[36,16,128]{2,1,0:T(8,128)} %get-tuple-element.72), channel_id=1, source_target_pairs={{0,1},{1,0},{2,3},{3,2},{4,5},{5,4},{6,7},{7,6},{8,9},{9,8},{10,11... | collective-permute-start | bytes 884744 | tf_op jit(solution)/shard_map/ppermute | solution.py:343
  71.4 37.6 %copy-start.5 = (f32[36,16,128]{2,1,0:T(8,128)}, f32[36,16,128]{2,1,0:T(8,128)S(1)}, u32[]{:S(2)}) copy-start(f32[36,16,128]{2,1,0:T(8,128)S(1)} %collective-permute-done.5.rest_4_) | copy-start | bytes 884740
  71.4 40.7 %collective-permute-start.12 = (f32[36,16,128]{2,1,0:T(8,128)}, f32[36,16,128]{2,1,0:T(8,128)S(1)}, u32[]{:S(2)}, u32[]{:S(2)}) collective-permute-start(f32[36,16,128]{2,1,0:T(8,128)} %get-tuple-element.73), channel_id=1, source_target_pairs={{0,2},{1,3},{2,0},{3,1},{4,6},{5,7},{6,4},{7,5},{8,10},{9,11},{10,... | collective-permute-start | bytes 884744 | tf_op jit(solution)/shard_map/ppermute | solution.py:343
  73.3 35.7 %copy-start.6 = (f32[36,16,128]{2,1,0:T(8,128)}, f32[36,16,128]{2,1,0:T(8,128)S(1)}, u32[]{:S(2)}) copy-start(f32[36,16,128]{2,1,0:T(8,128)S(1)} %collective-permute-done.6.rest_5_) | copy-start | bytes 884740
  73.3 38.8 %collective-permute-start.13 = (f32[36,16,128]{2,1,0:T(8,128)}, f32[36,16,128]{2,1,0:T(8,128)S(1)}, u32[]{:S(2)}, u32[]{:S(2)}) collective-permute-start(f32[36,16,128]{2,1,0:T(8,128)} %get-tuple-element.74), channel_id=1, source_target_pairs={{0,3},{1,2},{2,1},{3,0},{4,7},{5,6},{6,5},{7,4},{8,11},{9,10},{10,... | collective-permute-start | bytes 884744 | tf_op jit(solution)/shard_map/ppermute | solution.py:343
  73.3 35.7 %copy-start.7 = (f32[36,16,128]{2,1,0:T(8,128)}, f32[36,16,128]{2,1,0:T(8,128)S(1)}, u32[]{:S(2)}) copy-start(f32[36,16,128]{2,1,0:T(8,128)S(1)} %collective-permute-done.7.rest_6_) | copy-start | bytes 884740
  73.3 39.3 %copy-start.35 = (f32[36]{0:T(128)S(1)}, f32[36]{0:T(128)}, u32[]{:S(2)}) copy-start(f32[36]{0:T(128)} %get-tuple-element.119.sin_ref) | copy-start | bytes 436
  73.3 39.3 %copy-start.36 = (f32[36]{0:T(128)S(1)}, f32[36]{0:T(128)}, u32[]{:S(2)}) copy-start(f32[36]{0:T(128)} %get-tuple-element.120.cos_ref) | copy-start | bytes 436
  73.3 63.9 %copy-start.28 = (f32[32,36,36]{2,0,1:T(8,128)S(1)}, f32[32,36,36]{2,0,1:T(8,128)}, u32[]{:S(2)}) copy-start(f32[32,36,36]{2,0,1:T(8,128)} %param.17) | copy-start | bytes 497668
  73.3 38.9 %collective-permute-start.14 = (f32[36,16,128]{2,1,0:T(8,128)}, f32[36,16,128]{2,1,0:T(8,128)S(1)}, u32[]{:S(2)}, u32[]{:S(2)}) collective-permute-start(f32[36,16,128]{2,1,0:T(8,128)} %get-tuple-element.75), channel_id=1, source_target_pairs={{0,4},{1,5},{2,6},{3,7},{4,0},{5,1},{6,2},{7,3},{8,12},{9,13},{10,... | collective-permute-start | bytes 884744 | tf_op jit(solution)/shard_map/ppermute | solution.py:343
  109.0 48.4 %copy-start.37 = (f32[32]{0:T(128)S(1)}, f32[32]{0:T(128)}, u32[]{:S(2)}) copy-start(f32[32]{0:T(128)} %param.15) | copy-start | bytes 388
  109.0 22.2 %collective-permute-start.15 = (f32[36,16,128]{2,1,0:T(8,128)}, f32[36,16,128]{2,1,0:T(8,128)S(1)}, u32[]{:S(2)}, u32[]{:S(2)}) collective-permute-start(f32[36,16,128]{2,1,0:T(8,128)} %get-tuple-element.76), channel_id=1, source_target_pairs={{0,5},{1,4},{2,7},{3,6},{4,1},{5,0},{6,3},{7,2},{8,13},{9,12},{10,... | collective-permute-start | bytes 884744 | tf_op jit(solution)/shard_map/ppermute | solution.py:343
  109.1 23.4 %collective-permute-start.16 = (f32[36,16,128]{2,1,0:T(8,128)}, f32[36,16,128]{2,1,0:T(8,128)S(1)}, u32[]{:S(2)}, u32[]{:S(2)}) collective-permute-start(f32[36,16,128]{2,1,0:T(8,128)} %get-tuple-element.77), channel_id=1, source_target_pairs={{0,6},{1,7},{2,4},{3,5},{4,2},{5,3},{6,0},{7,1},{8,14},{9,15},{10,... | collective-permute-start | bytes 884744 | tf_op jit(solution)/shard_map/ppermute | solution.py:343
  112.1 50.1 %copy-start.10 = (f32[36,16,128]{2,1,0:T(8,128)}, f32[36,16,128]{2,1,0:T(8,128)S(1)}, u32[]{:S(2)}) copy-start(f32[36,16,128]{2,1,0:T(8,128)S(1)} %collective-permute-done.12.rest_10_) | copy-start | bytes 884740
  112.1 20.6 %collective-permute-start.17 = (f32[36,16,128]{2,1,0:T(8,128)}, f32[36,16,128]{2,1,0:T(8,128)S(1)}, u32[]{:S(2)}, u32[]{:S(2)}) collective-permute-start(f32[36,16,128]{2,1,0:T(8,128)} %get-tuple-element.78), channel_id=1, source_target_pairs={{0,7},{1,6},{2,5},{3,4},{4,3},{5,2},{6,1},{7,0},{8,15},{9,14},{10,... | collective-permute-start | bytes 884744 | tf_op jit(solution)/shard_map/ppermute | solution.py:343
  112.1 50.5 %copy-start.11 = (f32[36,16,128]{2,1,0:T(8,128)}, f32[36,16,128]{2,1,0:T(8,128)S(1)}, u32[]{:S(2)}) copy-start(f32[36,16,128]{2,1,0:T(8,128)S(1)} %collective-permute-done.13.rest_11_) | copy-start | bytes 884740
  112.1 20.6 %collective-permute-start.20 = (f32[72,8,128]{2,1,0:T(8,128)}, f32[72,8,128]{2,1,0:T(8,128)S(1)}, u32[]{:S(2)}, u32[]{:S(2)}) collective-permute-start(f32[72,8,128]{2,1,0:T(8,128)} %get-tuple-element.82), channel_id=1, source_target_pairs={{0,1},{1,0},{2,3},{3,2},{4,5},{5,4},{6,7},{7,6},{8,9},{9,8},{10,11... | collective-permute-start | bytes 884744 | tf_op jit(solution)/shard_map/ppermute | solution.py:343
  112.3 50.3 %copy-start.12 = (f32[36,16,128]{2,1,0:T(8,128)}, f32[36,16,128]{2,1,0:T(8,128)S(1)}, u32[]{:S(2)}) copy-start(f32[36,16,128]{2,1,0:T(8,128)S(1)} %collective-permute-done.14.rest_12_) | copy-start | bytes 884740
  112.3 22.5 %collective-permute-start.34 = (f32[72,8,128]{2,1,0:T(8,128)}, f32[72,8,128]{2,1,0:T(8,128)S(1)}, u32[]{:S(2)}, u32[]{:S(2)}) collective-permute-start(f32[72,8,128]{2,1,0:T(8,128)} %get-tuple-element.98), channel_id=1, source_target_pairs={{0,1},{1,0},{2,3},{3,2},{4,5},{5,4},{6,7},{7,6},{8,9},{9,8},{10,11... | collective-permute-start | bytes 884744 | tf_op jit(solution)/shard_map/ppermute | solution.py:343
  131.2 31.0 %copy-start.13 = (f32[36,16,128]{2,1,0:T(8,128)}, f32[36,16,128]{2,1,0:T(8,128)S(1)}, u32[]{:S(2)}) copy-start(f32[36,16,128]{2,1,0:T(8,128)S(1)} %collective-permute-done.15.rest_13_) | copy-start | bytes 884740
  131.2 10.2 %collective-permute-start.35 = (f32[72,8,128]{2,1,0:T(8,128)}, f32[72,8,128]{2,1,0:T(8,128)}, u32[]{:S(2)}, u32[]{:S(2)}) collective-permute-start(f32[72,8,128]{2,1,0:T(8,128)} %get-tuple-element.99), channel_id=1, source_target_pairs={{0,2},{1,3},{2,0},{3,1},{4,6},{5,7},{6,4},{7,5},{8,10},{9,11},{10,... | collective-permute-start | bytes 884744 | tf_op jit(solution)/shard_map/ppermute | solution.py:343
  132.6 14.0 %collective-permute-start.36 = (f32[72,8,128]{2,1,0:T(8,128)}, f32[72,8,128]{2,1,0:T(8,128)}, u32[]{:S(2)}, u32[]{:S(2)}) collective-permute-start(f32[72,8,128]{2,1,0:T(8,128)} %get-tuple-element.100), channel_id=1, source_target_pairs={{0,3},{1,2},{2,1},{3,0},{4,7},{5,6},{6,5},{7,4},{8,11},{9,10},{10,... | collective-permute-start | bytes 884744 | tf_op jit(solution)/shard_map/ppermute | solution.py:343
  132.7 16.1 %collective-permute-start.37 = (f32[72,8,128]{2,1,0:T(8,128)}, f32[72,8,128]{2,1,0:T(8,128)}, u32[]{:S(2)}, u32[]{:S(2)}) collective-permute-start(f32[72,8,128]{2,1,0:T(8,128)} %get-tuple-element.101), channel_id=1, source_target_pairs={{0,4},{1,5},{2,6},{3,7},{4,0},{5,1},{6,2},{7,3},{8,12},{9,13},{10,... | collective-permute-start | bytes 884744 | tf_op jit(solution)/shard_map/ppermute | solution.py:343
  132.7 22.3 %collective-permute-start.38 = (f32[72,8,128]{2,1,0:T(8,128)}, f32[72,8,128]{2,1,0:T(8,128)}, u32[]{:S(2)}, u32[]{:S(2)}) collective-permute-start(f32[72,8,128]{2,1,0:T(8,128)} %get-tuple-element.102), channel_id=1, source_target_pairs={{0,5},{1,4},{2,7},{3,6},{4,1},{5,0},{6,3},{7,2},{8,13},{9,12},{10,... | collective-permute-start | bytes 884744 | tf_op jit(solution)/shard_map/ppermute | solution.py:343
  134.7 20.5 %collective-permute-start.39 = (f32[72,8,128]{2,1,0:T(8,128)}, f32[72,8,128]{2,1,0:T(8,128)}, u32[]{:S(2)}, u32[]{:S(2)}) collective-permute-start(f32[72,8,128]{2,1,0:T(8,128)} %get-tuple-element.103), channel_id=1, source_target_pairs={{0,6},{1,7},{2,4},{3,5},{4,2},{5,3},{6,0},{7,1},{8,14},{9,15},{10,... | collective-permute-start | bytes 884744 | tf_op jit(solution)/shard_map/ppermute | solution.py:343
  141.4 56.5 %collective-permute-start.21 = (f32[72,8,128]{2,1,0:T(8,128)}, f32[72,8,128]{2,1,0:T(8,128)}, u32[]{:S(2)}, u32[]{:S(2)}) collective-permute-start(f32[72,8,128]{2,1,0:T(8,128)} %get-tuple-element.83), channel_id=1, source_target_pairs={{0,2},{1,3},{2,0},{3,1},{4,6},{5,7},{6,4},{7,5},{8,10},{9,11},{10,... | collective-permute-start | bytes 884744 | tf_op jit(solution)/shard_map/ppermute | solution.py:343
  146.6 51.9 %collective-permute-start.22 = (f32[72,8,128]{2,1,0:T(8,128)}, f32[72,8,128]{2,1,0:T(8,128)}, u32[]{:S(2)}, u32[]{:S(2)}) collective-permute-start(f32[72,8,128]{2,1,0:T(8,128)} %get-tuple-element.84), channel_id=1, source_target_pairs={{0,3},{1,2},{2,1},{3,0},{4,7},{5,6},{6,5},{7,4},{8,11},{9,10},{10,... | collective-permute-start | bytes 884744 | tf_op jit(solution)/shard_map/ppermute | solution.py:343
  148.8 50.0 %collective-permute-start.23 = (f32[72,8,128]{2,1,0:T(8,128)}, f32[72,8,128]{2,1,0:T(8,128)}, u32[]{:S(2)}, u32[]{:S(2)}) collective-permute-start(f32[72,8,128]{2,1,0:T(8,128)} %get-tuple-element.85), channel_id=1, source_target_pairs={{0,4},{1,5},{2,6},{3,7},{4,0},{5,1},{6,2},{7,3},{8,12},{9,13},{10,... | collective-permute-start | bytes 884744 | tf_op jit(solution)/shard_map/ppermute | solution.py:343
  155.0 46.6 %collective-permute-start.24 = (f32[72,8,128]{2,1,0:T(8,128)}, f32[72,8,128]{2,1,0:T(8,128)}, u32[]{:S(2)}, u32[]{:S(2)}) collective-permute-start(f32[72,8,128]{2,1,0:T(8,128)} %get-tuple-element.86), channel_id=1, source_target_pairs={{0,5},{1,4},{2,7},{3,6},{4,1},{5,0},{6,3},{7,2},{8,13},{9,12},{10,... | collective-permute-start | bytes 884744 | tf_op jit(solution)/shard_map/ppermute | solution.py:343
  155.2 16.0 %collective-permute-start.40 = (f32[72,8,128]{2,1,0:T(8,128)}, f32[72,8,128]{2,1,0:T(8,128)}, u32[]{:S(2)}, u32[]{:S(2)}) collective-permute-start(f32[72,8,128]{2,1,0:T(8,128)} %get-tuple-element.104), channel_id=1, source_target_pairs={{0,7},{1,6},{2,5},{3,4},{4,3},{5,2},{6,1},{7,0},{8,15},{9,14},{10,... | collective-permute-start | bytes 884744 | tf_op jit(solution)/shard_map/ppermute | solution.py:343
  171.2 30.3 %collective-permute-start.25 = (f32[72,8,128]{2,1,0:T(8,128)}, f32[72,8,128]{2,1,0:T(8,128)S(1)}, u32[]{:S(2)}, u32[]{:S(2)}) collective-permute-start(f32[72,8,128]{2,1,0:T(8,128)} %get-tuple-element.87), channel_id=1, source_target_pairs={{0,6},{1,7},{2,4},{3,5},{4,2},{5,3},{6,0},{7,1},{8,14},{9,15},{10,... | collective-permute-start | bytes 884744 | tf_op jit(solution)/shard_map/ppermute | solution.py:343
  198.0 68.0 %collective-permute-start.41 = (f32[144,8,128]{2,1,0:T(8,128)}, f32[144,8,128]{2,1,0:T(8,128)S(1)}, u32[]{:S(2)}, u32[]{:S(2)}) collective-permute-start(f32[144,8,128]{2,1,0:T(8,128)} %get-tuple-element.106), channel_id=1, source_target_pairs={{0,2},{1,3},{2,0},{3,1},{4,6},{5,7},{6,4},{7,5},{8,10},{9,11},{10,... | collective-permute-start | bytes 1769480 | tf_op jit(solution)/shard_map/ppermute | solution.py:343
  198.5 68.3 %collective-permute-start.42 = (f32[144,8,128]{2,1,0:T(8,128)}, f32[144,8,128]{2,1,0:T(8,128)S(1)}, u32[]{:S(2)}, u32[]{:S(2)}) collective-permute-start(f32[144,8,128]{2,1,0:T(8,128)} %get-tuple-element.107), channel_id=1, source_target_pairs={{0,4},{1,5},{2,6},{3,7},{4,0},{5,1},{6,2},{7,3},{8,12},{9,13},{10,... | collective-permute-start | bytes 1769480 | tf_op jit(solution)/shard_map/ppermute | solution.py:343
  198.9 68.1 %collective-permute-start.43 = (f32[144,8,128]{2,1,0:T(8,128)}, f32[144,8,128]{2,1,0:T(8,128)S(1)}, u32[]{:S(2)}, u32[]{:S(2)}) collective-permute-start(f32[144,8,128]{2,1,0:T(8,128)} %get-tuple-element.108), channel_id=1, source_target_pairs={{0,6},{1,7},{2,4},{3,5},{4,2},{5,3},{6,0},{7,1},{8,14},{9,15},{10,... | collective-permute-start | bytes 1769480 | tf_op jit(solution)/shard_map/ppermute | solution.py:343
  201.5 66.8 %collective-permute-start.44 = (f32[144,8,128]{2,1,0:T(8,128)}, f32[144,8,128]{2,1,0:T(8,128)S(1)}, u32[]{:S(2)}, u32[]{:S(2)}) collective-permute-start(f32[144,8,128]{2,1,0:T(8,128)} %get-tuple-element.109), channel_id=1, source_target_pairs={{0,3},{1,2},{2,1},{3,0},{4,7},{5,6},{6,5},{7,4},{8,11},{9,10},{10,... | collective-permute-start | bytes 1769480 | tf_op jit(solution)/shard_map/ppermute | solution.py:343
  201.5 44.7 %copy-start.31 = (f32[72,8,128]{2,1,0:T(8,128)}, f32[72,8,128]{2,1,0:T(8,128)S(1)}, u32[]{:S(2)}) copy-start(f32[72,8,128]{2,1,0:T(8,128)S(1)} %collective-permute-done.25.rest_22_) | copy-start | bytes 884740
  201.6 42.7 %collective-permute-start.26 = (f32[72,8,128]{2,1,0:T(8,128)S(1)}, f32[72,8,128]{2,1,0:T(8,128)S(1)}, u32[]{:S(2)}, u32[]{:S(2)}) collective-permute-start(f32[72,8,128]{2,1,0:T(8,128)S(1)} %copy-done.38), channel_id=1, source_target_pairs={{0,7},{1,6},{2,5},{3,4},{4,3},{5,2},{6,1},{7,0},{8,15},{9,14},{10,... | collective-permute-start | bytes 884744 | tf_op jit(solution)/shard_map/ppermute | solution.py:343
  244.2 25.4 %collective-permute-start.45 = (f32[144,8,128]{2,1,0:T(8,128)}, f32[144,8,128]{2,1,0:T(8,128)S(1)}, u32[]{:S(2)}, u32[]{:S(2)}) collective-permute-start(f32[144,8,128]{2,1,0:T(8,128)} %get-tuple-element.110), channel_id=1, source_target_pairs={{0,5},{1,4},{2,7},{3,6},{4,1},{5,0},{6,3},{7,2},{8,13},{9,12},{10,... | collective-permute-start | bytes 1769480 | tf_op jit(solution)/shard_map/ppermute | solution.py:343
  266.0 30.6 %copy-start.20 = (f32[144,8,128]{2,1,0:T(8,128)}, f32[144,8,128]{2,1,0:T(8,128)S(1)}, u32[]{:S(2)}) copy-start(f32[144,8,128]{2,1,0:T(8,128)S(1)} %collective-permute-done.41.rest_1_) | copy-start | bytes 1769476
  266.0 16.7 %collective-permute-start.46 = (f32[144,8,128]{2,1,0:T(8,128)}, f32[144,8,128]{2,1,0:T(8,128)S(1)}, u32[]{:S(2)}, u32[]{:S(2)}) collective-permute-start(f32[144,8,128]{2,1,0:T(8,128)} %get-tuple-element.111), channel_id=1, source_target_pairs={{0,7},{1,6},{2,5},{3,4},{4,3},{5,2},{6,1},{7,0},{8,15},{9,14},{10,... | collective-permute-start | bytes 1769480 | tf_op jit(solution)/shard_map/ppermute | solution.py:343
  266.8 29.8 %copy-start.21 = (f32[144,8,128]{2,1,0:T(8,128)}, f32[144,8,128]{2,1,0:T(8,128)S(1)}, u32[]{:S(2)}) copy-start(f32[144,8,128]{2,1,0:T(8,128)S(1)} %collective-permute-done.42.rest_2_) | copy-start | bytes 1769476
  266.8 16.4 %collective-permute-start.47 = (f32[144,8,128]{2,1,0:T(8,128)}, f32[144,8,128]{2,1,0:T(8,128)S(1)}, u32[]{:S(2)}, u32[]{:S(2)}) collective-permute-start(f32[144,8,128]{2,1,0:T(8,128)} %get-tuple-element.112), channel_id=1, source_target_pairs={{0,1},{1,0},{2,3},{3,2},{4,5},{5,4},{6,7},{7,6},{8,9},{9,8},{10,11... | collective-permute-start | bytes 1769480 | tf_op jit(solution)/shard_map/ppermute | solution.py:343
  266.9 28.4 %collective-permute-start.29 = (f32[144,8,128]{2,1,0:T(8,128)}, f32[144,8,128]{2,1,0:T(8,128)S(1)}, u32[]{:S(2)}, u32[]{:S(2)}) collective-permute-start(f32[144,8,128]{2,1,0:T(8,128)} %get-tuple-element.92), channel_id=1, source_target_pairs={{0,2},{1,3},{2,0},{3,1},{4,6},{5,7},{6,4},{7,5},{8,10},{9,11},{10,... | collective-permute-start | bytes 1769480 | tf_op jit(solution)/shard_map/ppermute | solution.py:343
  268.3 27.5 %collective-permute-start.30 = (f32[144,8,128]{2,1,0:T(8,128)}, f32[144,8,128]{2,1,0:T(8,128)}, u32[]{:S(2)}, u32[]{:S(2)}) collective-permute-start(f32[144,8,128]{2,1,0:T(8,128)} %get-tuple-element.93), channel_id=1, source_target_pairs={{0,4},{1,5},{2,6},{3,7},{4,0},{5,1},{6,2},{7,3},{8,12},{9,13},{10,... | collective-permute-start | bytes 1769480 | tf_op jit(solution)/shard_map/ppermute | solution.py:343
  269.7 38.8 %collective-permute-start.31 = (f32[144,8,128]{2,1,0:T(8,128)}, f32[144,8,128]{2,1,0:T(8,128)}, u32[]{:S(2)}, u32[]{:S(2)}) collective-permute-start(f32[144,8,128]{2,1,0:T(8,128)} %get-tuple-element.94), channel_id=1, source_target_pairs={{0,6},{1,7},{2,4},{3,5},{4,2},{5,3},{6,0},{7,1},{8,14},{9,15},{10,... | collective-permute-start | bytes 1769480 | tf_op jit(solution)/shard_map/ppermute | solution.py:343
  282.7 36.7 %collective-permute-start.32 = (f32[144,8,128]{2,1,0:T(8,128)}, f32[144,8,128]{2,1,0:T(8,128)}, u32[]{:S(2)}, u32[]{:S(2)}) collective-permute-start(f32[144,8,128]{2,1,0:T(8,128)} %get-tuple-element.95), channel_id=1, source_target_pairs={{0,3},{1,2},{2,1},{3,0},{4,7},{5,6},{6,5},{7,4},{8,11},{9,10},{10,... | collective-permute-start | bytes 1769480 | tf_op jit(solution)/shard_map/ppermute | solution.py:343
  283.2 37.6 %collective-permute-start.33 = (f32[144,8,128]{2,1,0:T(8,128)}, f32[144,8,128]{2,1,0:T(8,128)}, u32[]{:S(2)}, u32[]{:S(2)}) collective-permute-start(f32[144,8,128]{2,1,0:T(8,128)} %get-tuple-element.96), channel_id=1, source_target_pairs={{0,5},{1,4},{2,7},{3,6},{4,1},{5,0},{6,3},{7,2},{8,13},{9,12},{10,... | collective-permute-start | bytes 1769480 | tf_op jit(solution)/shard_map/ppermute | solution.py:343
  295.3 38.0 %collective-permute-start.27 = (f32[144,8,128]{2,1,0:T(8,128)}, f32[144,8,128]{2,1,0:T(8,128)}, u32[]{:S(2)}, u32[]{:S(2)}) collective-permute-start(f32[144,8,128]{2,1,0:T(8,128)} %get-tuple-element.89), channel_id=1, source_target_pairs={{0,7},{1,6},{2,5},{3,4},{4,3},{5,2},{6,1},{7,0},{8,15},{9,14},{10,... | collective-permute-start | bytes 1769480 | tf_op jit(solution)/shard_map/ppermute | solution.py:343
  295.8 37.5 %collective-permute-start.28 = (f32[144,8,128]{2,1,0:T(8,128)}, f32[144,8,128]{2,1,0:T(8,128)}, u32[]{:S(2)}, u32[]{:S(2)}) collective-permute-start(f32[144,8,128]{2,1,0:T(8,128)} %get-tuple-element.90), channel_id=1, source_target_pairs={{0,1},{1,0},{2,3},{3,2},{4,5},{5,4},{6,7},{7,6},{8,9},{9,8},{10,11... | collective-permute-start | bytes 1769480 | tf_op jit(solution)/shard_map/ppermute | solution.py:343
  (26 other events, 447.9 us)

commit v2 on v1

v2 whole, which is shorter than its diff:
```python
import math

import jax
import jax.numpy as jnp
import numpy as np
from jax import lax
from jax.experimental import pallas as pl
from jax.experimental.pallas import tpu as pltpu
from jax.sharding import PartitionSpec as P


DIRS = 36
FREQ = 32
SUBSTEPS = 6
EDGE = 8
ROWS = 8
UNITS = 24
CHUNKS = (6, 8, 10)
STRIP_BLOCKS = 12
STREAMS = 3
BAND = 4
PAD = 8
LANES = 3


def edge_strips(spectrum, land_mask, base, made, block):
    _, lat, lon = spectrum.shape
    part = block // STREAMS

    def kernel(*rest):
        waves, (land_ref, near_ref, far_ref, turned) = rest[:STREAMS], rest[STREAMS:]
        step = pl.program_id(0)
        even = lax.rem(lax.axis_index("sector"), 2) == 0
        near = pl.multiple_of(jnp.where(even, lon - EDGE, 0), EDGE)
        far = pl.multiple_of(jnp.where(even, 0, lon - EDGE), EDGE)
        for b in range(block):
            turned[b] = waves[b // part][b % part].T
            near_ref[step * block + b] = turned[b, pl.ds(near, EDGE)]
            far_ref[step * block + b] = turned[b, pl.ds(far, EDGE)]

        @pl.when(step == 0)
        def _():
            turned[0] = land_ref[...].astype(jnp.float32).T
            near_ref[made] = turned[0, pl.ds(near, EDGE)]
            far_ref[made] = turned[0, pl.ds(far, EDGE)]

    strip = pl.BlockSpec((made + 1, EDGE, lat), lambda i, *_: (0, 0, 0))
    shape = jax.ShapeDtypeStruct((made + 1, EDGE, lat), jnp.float32)
    first = base // part
    streams = [
        pl.BlockSpec((part, lat, lon), lambda i, *_, n=n: (first + i * STREAMS + n, 0, 0))
        for n in range(STREAMS)
    ]
    return pl.pallas_call(
        kernel,
        grid=(made // block,),
        in_specs=streams + [pl.BlockSpec((lat, lon), lambda i: (0, 0))],
        out_specs=[strip, strip],
        scratch_shapes=[pltpu.VMEM((block, lon, lat), jnp.float32)],
        out_shape=[shape, shape],
        cost_estimate=pl.CostEstimate(
            flops=0, bytes_accessed=8 * made * lat * lon, transcendentals=0
        ),
        name="edge_strips",
    )(*[spectrum] * STREAMS, land_mask)


def advance(tables, spectrum, strips, land_mask, inverse, base, made, block, count, pieces):
    comps_dev, lat, lon = spectrum.shape
    rows_dev = sum(pieces)
    span = lon + EDGE
    lanes = LANES if block % LANES == 0 else 3 if block % 3 == 0 else 1

    def kernel(
        kinds_ref, courant_ref, cos_ref, sin_ref,
        wave_ref, near_ref, far_ref, near_sea_ref, far_sea_ref, land_ref, inverse_ref,
        *rest,
    ):
        outs, rest = rest[: len(pieces) * count], rest[len(pieces) * count :]
        sea, slope, side = rest[:3]
        sets = [rest[3 + 6 * q : 9 + 6 * q] for q in range(lanes)]
        step = pl.program_id(0)
        me = lax.axis_index("group")
        even = lax.rem(lax.axis_index("sector"), 2) == 0

        @pl.when(step == 0)
        def _():
            for ping, pong, *_ in sets:
                ping[...] = jnp.zeros_like(ping)
                pong[...] = jnp.zeros_like(pong)
            own = land_ref[...].astype(jnp.float32).T
            sea[0, EDGE:] = own
            sea[1, :lon] = own
            sea[0, :EDGE] = jnp.where(even, far_sea_ref[0], near_sea_ref[0])
            sea[1, lon:] = jnp.where(even, near_sea_ref[0], far_sea_ref[0])
            lane = lax.broadcasted_iota(jnp.int32, (span, lat), 1)
            for way in range(2):
                slope[way] = sea[way] * inverse_ref[...]
                side[way] = jnp.where(lane == 0, 0.0, sea[way])
                side[2 + way] = jnp.where(lane == lat - 1, 0.0, sea[way])

        def some(i, carry):
            easts, turns = [], []
            for q, (ping, pong, keep, cross, along, result) in enumerate(sets):
                b = i * lanes + q
                kind = kinds_ref[me * comps_dev + base + step * block + b]
                speed = courant_ref[lax.div(kind, DIRS)]
                flow_x = speed * cos_ref[lax.rem(kind, DIRS)]
                flow_y = speed * sin_ref[lax.rem(kind, DIRS)]
                eastward = flow_x > 0.0
                northward = flow_y > 0.0
                way = jnp.where(eastward, 0, 1)
                easts.append(jnp.full((EDGE, lat), way) == 0)
                turns.append(jnp.where(northward, 1, lat - 1))
                rate_x, rate_y = jnp.abs(flow_x), jnp.abs(flow_y)
                ratio = rate_x * slope[way]
                cross[...] = ratio
                along[...] = rate_y * side[jnp.where(northward, way, 2 + way)]
                keep[...] = (1.0 - rate_y) * sea[way] - ratio
                own = pl.multiple_of(jnp.where(eastward, 2 * EDGE, EDGE), EDGE)
                upwind = pl.multiple_of(jnp.where(eastward, EDGE, EDGE + lon), EDGE)
                ping[pl.ds(own, lon)] = wave_ref[b].T
                ping[pl.ds(upwind, EDGE)] = jnp.where(eastward == even, far_ref[b], near_ref[b])
            for substep in range(SUBSTEPS):
                for row in range(0, span, EDGE):
                    for q, (ping, pong, keep, cross, along, result) in enumerate(sets):
                        now, then = (ping, pong) if substep % 2 == 0 else (pong, ping)
                        spot = slice(row, row + EDGE)
                        here = now[row + EDGE : row + 2 * EDGE]
                        upwind = jnp.where(
                            easts[q],
                            now[row + EDGE - 1 : row + 2 * EDGE - 1],
                            now[row + EDGE + 1 : row + 2 * EDGE + 1],
                        )
                        then[row + EDGE : row + 2 * EDGE] = (
                            keep[spot] * here
                            + cross[spot] * upwind
                            + along[spot] * pltpu.roll(here, turns[q], 1)
                        )
            for q, (ping, pong, keep, cross, along, result) in enumerate(sets):
                b = i * lanes + q
                last = ping if SUBSTEPS % 2 == 0 else pong
                kind = kinds_ref[me * comps_dev + base + step * block + b]
                eastward = cos_ref[lax.rem(kind, DIRS)] > 0.0
                own = pl.multiple_of(jnp.where(eastward, 2 * EDGE, EDGE), EDGE)
                result[...] = last[pl.ds(own, lon)].T
                offset = 0
                for p, rows in enumerate(pieces):
                    for k in range(count):
                        row = pl.multiple_of((me ^ k) * rows_dev + offset, ROWS)
                        outs[p * count + k][b] = result[pl.ds(row, rows)]
                    offset += rows
            return carry

        lax.fori_loop(0, block // lanes, some, 0)

    strip = pl.BlockSpec((block, EDGE, lat), lambda i, *_: (i, 0, 0))
    strip_of_sea = pl.BlockSpec((1, EDGE, lat), lambda i, *_: (made, 0, 0))
    fixed = lambda shape: pl.BlockSpec(shape, lambda i, *_: (0,) * len(shape))
    first_block = base // block
    f32 = lambda *shape: pltpu.VMEM(shape, jnp.float32)
    return pl.pallas_call(
        kernel,
        grid_spec=pltpu.PrefetchScalarGridSpec(
            num_scalar_prefetch=4,
            grid=(made // block,),
            in_specs=[
                pl.BlockSpec((block, lat, lon), lambda i, *_: (first_block + i, 0, 0)),
                strip,
                strip,
                strip_of_sea,
                strip_of_sea,
                fixed((lat, lon)),
                fixed((1, lat)),
            ],
            out_specs=[
                pl.BlockSpec((block, rows, lon), lambda i, *_: (i, 0, 0))
                for rows in pieces
                for _ in range(count)
            ],
            scratch_shapes=[f32(2, span, lat), f32(2, span, lat), f32(4, span, lat)]
            + [
                f32(span + 2 * EDGE, lat), f32(span + 2 * EDGE, lat),
                f32(span, lat), f32(span, lat), f32(span, lat),
                f32(lat, lon),
            ] * lanes,
        ),
        out_shape=[
            jax.ShapeDtypeStruct((made, rows, lon), jnp.float32)
            for rows in pieces
            for _ in range(count)
        ],
        cost_estimate=pl.CostEstimate(
            flops=0, bytes_accessed=12 * made * lat * lon * 4, transcendentals=0
        ),
        name="advance",
    )(*tables, spectrum, *strips, *strips, land_mask, inverse)


def couple(assignment, arrived, sea_rows, winds, per_kind, blocks, count, comps_dev, part):
    comps = assignment.shape[0]
    lon = sea_rows.shape[1]
    bands, band, _ = blocks[0].shape
    flat = [a for group, _ in arrived for a in group]
    sizes = [group[0].shape[0] for group, _ in arrived]
    pitch = comps + PAD
    unroll = 8 if all(size % 8 == 0 for size in sizes) else 6

    def kernel(kinds_ref, *rest):
        ins, rest = rest[: len(flat)], rest[len(flat) :]
        sea_ref, wind_ref, weight_ref, east_ref, north_ref, decay_ref, high_ref, low_ref = rest[:8]
        outs, (sorted_ref,) = rest[8:-1], rest[-1:]
        me = lax.axis_index("group")
        for k in range(count):
            for g in range(len(arrived)):
                first = (me ^ k) * comps_dev + sum(sizes[:g])
                source = ins[g * count + k]

                def put(i, carry, source=source, first=first):
                    rows = [i * unroll + u for u in range(unroll)]
                    kinds = [kinds_ref[first + c] for c in rows]
                    values = [source[c] for c in rows]
                    for kind, value in zip(kinds, values):
                        sorted_ref[pl.ds(kind, ROWS, stride=pitch), :] = value
                    return carry

                lax.fori_loop(0, sizes[g] // unroll, put, 0)

        def pair(p, carry):
            starts = [pl.multiple_of((2 * p + q) * pitch, 8) for q in range(2)]
            loads, us, vs, seas = [], [], [], []
            for q in range(2):
                j = 2 * p + q
                total = jnp.sum(
                    weight_ref[...] * sorted_ref[pl.ds(starts[q], comps), :], axis=0, keepdims=True
                )
                loading = total / comps
                loads.append(loading / (1.0 + loading))
                us.append(wind_ref[0, pl.ds(j, 1), :])
                vs.append(wind_ref[1, pl.ds(j, 1), :])
                seas.append(sea_ref[pl.ds(j, 1), :])
            for n in range(bands):
                kinds = slice(n * band, (n + 1) * band)
                spots = [pl.ds(pl.multiple_of(starts[q] + n * band, 8), band) for q in range(2)]
                energy = [sorted_ref[spots[q], :] for q in range(2)]
                both = jnp.concatenate(energy, axis=1)
                high = both.astype(jnp.bfloat16)
                low = (both - high.astype(jnp.float32)).astype(jnp.bfloat16)
                dot = lambda a, b: jnp.dot(a, b, preferred_element_type=jnp.float32)
                mixed = dot(high_ref[n], high) + (dot(high_ref[n], low) + dot(low_ref[n], high))
                for q in range(2):
                    drive = east_ref[kinds, :] * us[q] + north_ref[kinds, :] * vs[q]
                    exponent = jnp.maximum(drive, 0.0) - decay_ref[kinds, :] * loads[q]
                    sorted_ref[spots[q], :] = seas[q] * (
                        energy[q] * jnp.exp(exponent) + mixed[:, q * lon : (q + 1) * lon]
                    )
            return carry

        lax.fori_loop(0, ROWS // 2, pair, 0)
        step = 8 if comps_dev % 8 == 0 else 6
        for k in range(count):

            def take(i, carry, k=k):
                rows = [i * step + u for u in range(step)]
                kinds = [kinds_ref[(me ^ k) * comps_dev + c] for c in rows]
                values = [sorted_ref[pl.ds(kind, ROWS, stride=pitch), :] for kind in kinds]
                for c, value in zip(rows, values):
                    outs[k][c] = value
                return carry

            lax.fori_loop(0, comps_dev // step, take, 0)

    vmem = pl.BlockSpec(memory_space=pltpu.VMEM)
    pieces = [
        pl.BlockSpec((a.shape[0], ROWS, lon), lambda *_, at=at: (0, at, 0))
        for group, at in arrived
        for a in group
    ]
    rows = pl.BlockSpec((ROWS, lon), lambda *_: (part, 0))
    wind_rows = pl.BlockSpec((2, ROWS, lon), lambda *_: (0, part, 0))
    return pl.pallas_call(
        kernel,
        grid_spec=pltpu.PrefetchScalarGridSpec(
            num_scalar_prefetch=1,
            grid=(1,),
            in_specs=pieces + [rows, wind_rows] + [vmem] * 6,
            out_specs=[vmem] * count,
            scratch_shapes=[pltpu.VMEM((ROWS * pitch, lon), jnp.float32)],
        ),
        out_shape=[jax.ShapeDtypeStruct((comps_dev, ROWS, lon), jnp.float32)] * count,
        cost_estimate=pl.CostEstimate(
            flops=0, bytes_accessed=8 * comps * ROWS * lon * 4, transcendentals=0
        ),
        name="couple",
    )(assignment, *flat, sea_rows, winds, *per_kind, *blocks)


def settle(returned, ks, part, rows_dev, lat, partial):
    comps_dev, _, lon = returned[0].shape
    cuts = 4 if len(ks) <= 2 else 2
    cut = comps_dev // cuts
    jobs = [(n, k, c) for n, k in enumerate(ks) for c in range(cuts)]
    amount = len(jobs)

    def kernel(*rest):
        ins, out_ref, (held, in_sem, out_sem) = rest[: len(ks)], rest[-4], rest[-3:]
        me = lax.axis_index("group")
        into, out = [], []
        for job, (n, k, c) in enumerate(jobs):
            row = pl.multiple_of((me ^ k) * rows_dev + part * ROWS, ROWS)
            some = pl.ds(c * cut, cut)
            into.append(pltpu.make_async_copy(ins[n].at[some], held.at[job], in_sem.at[job]))
            target = out_ref.at[some, pl.ds(row, ROWS), :]
            out.append(pltpu.make_async_copy(held.at[job], target, out_sem.at[job]))
        for copy in into:
            copy.start()
        for job in range(amount):
            into[job].wait()
            out[job].start()
        for copy in out:
            copy.wait()

    anywhere = pl.BlockSpec(memory_space=pl.ANY)
    extra = [] if partial is None else [partial]
    return pl.pallas_call(
        kernel,
        in_specs=[anywhere] * (len(ks) + len(extra)),
        out_specs=anywhere,
        scratch_shapes=[
            pltpu.VMEM((amount, cut, ROWS, lon), jnp.float32),
            pltpu.SemaphoreType.DMA((amount,)),
            pltpu.SemaphoreType.DMA((amount,)),
        ],
        out_shape=jax.ShapeDtypeStruct((comps_dev, lat, lon), jnp.float32),
        input_output_aliases={len(ks): 0} if extra else {},
        cost_estimate=pl.CostEstimate(
            flops=0, bytes_accessed=2 * len(ks) * comps_dev * ROWS * lon * 4, transcendentals=0
        ),
        name="settle",
    )(*[returned[k] for k in ks], *extra)


def order_of(count):
    return [k for k in (*range(2, count, 2), *range(3, count, 2))] + [1]


def stages_of(count):
    order = order_of(count)
    return [[0, 1] + order[: count - 5], order[count - 5 : count - 3], order[count - 3 : count - 2]]


def swap(pieces, count):
    made = [pieces[0]] + [None] * (count - 1)
    for k in order_of(count):
        made[k] = lax.ppermute(pieces[k], "group", [(i, i ^ k) for i in range(count)])
    return made


def exchange(near, far):
    count = lax.axis_size("sector")
    pairs = [(i, i ^ 1) for i in range(count)]
    near = lax.ppermute(near, "sector", pairs)
    pairs = [(i, (i + 1) % count if i % 2 else (i - 1) % count) for i in range(count)]
    far = lax.ppermute(far, "sector", pairs)
    return near, far


def local(spectrum, land_mask, wind_field, assignment, courant, growth, whitecap, weights, spread):
    member = lax.axis_index("group").astype(jnp.int32)
    count = lax.axis_size("group")
    comps_dev, lat, lon = spectrum.shape
    comps = assignment.shape[0]
    rows_dev = wind_field.shape[1]
    parts = rows_dev // ROWS
    unit = comps_dev // UNITS

    angles = (np.arange(DIRS) + 0.5) * (2.0 * math.pi / DIRS)
    cosine = jnp.asarray(np.cos(angles), jnp.float32)
    sine = jnp.asarray(np.sin(angles), jnp.float32)
    latitude = (np.arange(lat) + 0.5 - lat / 2) * (math.pi / 2160.0)
    inverse = jnp.asarray(1.0 / np.cos(latitude), jnp.float32)[None, :]
    sea_mask = land_mask.astype(jnp.float32)
    tables = (assignment, courant, cosine, sine)

    arrived = [[] for _ in range(parts)]
    base = 0
    for c, units in enumerate(CHUNKS):
        made = units * unit
        near, far = edge_strips(
            spectrum, land_mask, base, made, comps_dev // STRIP_BLOCKS
        )
        strips = exchange(near, far)
        pieces = [ROWS] * parts if c == len(CHUNKS) - 1 else [rows_dev]
        sent = advance(
            tables, spectrum, strips, land_mask, inverse, base, made, unit, count, pieces
        )
        for p in range(len(pieces)):
            group = swap(sent[p * count : (p + 1) * count], count)
            for part in range(parts):
                if len(pieces) == 1:
                    arrived[part].append((group, part))
                elif p == part:
                    arrived[part].append((group, 0))
        base += made

    def spread_out(values):
        return jnp.broadcast_to(values[:, None], (comps, lon))

    fast = jnp.repeat(growth, DIRS)
    per_kind = (
        spread_out(jnp.repeat(weights, DIRS)),
        spread_out(fast * jnp.tile(cosine, FREQ)),
        spread_out(fast * jnp.tile(sine, FREQ)),
        spread_out(jnp.repeat(whitecap, DIRS)),
    )
    halves = (0.5 * spread).reshape(FREQ // BAND, BAND, DIRS, 1, DIRS)
    same = jnp.eye(BAND, dtype=jnp.float32)[None, :, None, :, None]
    whole = (halves * same).reshape(FREQ // BAND, BAND * DIRS, BAND * DIRS)
    high = lax.reduce_precision(whole, 8, 7)
    blocks = (high.astype(jnp.bfloat16), (whole - high).astype(jnp.bfloat16))
    sea_rows = lax.dynamic_slice_in_dim(sea_mask, member * rows_dev, rows_dev, 0)

    returned = []
    for part in range(parts):
        made = couple(
            assignment, arrived[part], sea_rows, wind_field, per_kind, blocks,
            count, comps_dev, part,
        )
        returned.append(swap(made, count))
    order = order_of(count)
    out = None
    for part in range(parts):
        stages = [[0] + order] if part < parts - 1 else stages_of(count)
        for ks in stages:
            out = settle(returned[part], ks, part, rows_dev, lat, out)
    return out


def solution(mesh):
    in_specs = (
        P("group", None, "sector"),
        P(None, "sector"),
        P(None, "group", "sector"),
        P(),
        P(),
        P(),
        P(),
        P(),
        P(),
    )
    out_specs = P("group", None, "sector")
    return jax.shard_map(local, mesh=mesh, in_specs=in_specs, out_specs=out_specs, check_vma=False)
```

time: 337 us -> 319 us (0.947)
  Pallas kernels: 120 us -> 99.9 us
  waiting for transfers between devices: 138 us -> 156 us
  starting transfers between devices: 57.3 us -> 47.9 us
    ppermute x42, waiting for transfers between devices: 131 us -> 145 us  [swap(): lax.ppermute(pieces[k], 'group', [(i, i ^ k) for i in range(count)])]
    pallas_call x2, Pallas kernels: 39.6 us -> 28.7 us  [couple(): pl.pallas_call(kernel, grid_spec=pltpu.PrefetchScalarGridSpec(num_scalar_...]
    pallas_call x3, Pallas kernels: 57.3 us -> 47.2 us  [advance(): pl.pallas_call(kernel, grid_spec=pltpu.PrefetchScalarGridSpec(num_scalar_...]
    ppermute x42, starting transfers between devices: 46.8 us -> 37.6 us  [swap(): lax.ppermute(pieces[k], 'group', [(i, i ^ k) for i in range(count)])]
    ppermute x3, waiting for transfers between devices: 3.19 us -> 7.7 us  [exchange(): far = lax.ppermute(far, 'sector', pairs)]
    pallas_call x6 -> x7, Pallas kernels: 23.4 us -> 23.9 us  [the longest x3 12.8 us: edge_strips(): pl.pallas_call(kernel, grid=(made // block,), in_specs=streams + [pl.Bloc...]
  transfers between devices with their start and end apart: 48 -> 48, of which waited for: 16 -> 14; matrix products, arithmetic and copies ran while one was open for 5% -> 3% of each run, Pallas kernels for 34% -> 30%
where the time goes in v2:
time: 319 us
  waiting for transfers between devices  156 us (49%)
  Pallas kernels  99.9 us (31%)
  starting transfers between devices  47.9 us (15%)
  local copies, waits for them, and re-layouts  10.4 us (3%)
  other arithmetic  3.7 us (1%)
    ppermute x42, waiting for transfers between devices, swap(): lax.ppermute(pieces[k], 'group', [(i, i ^ k) for i in range(count)])  145 us
    pallas_call x3, Pallas kernels, advance(): pl.pallas_call(kernel, grid_spec=pltpu.PrefetchScalarGridSpec(num_scalar_...  47.2 us
    ppermute x42, starting transfers between devices, swap(): lax.ppermute(pieces[k], 'group', [(i, i ^ k) for i in range(count)])  37.6 us
    pallas_call x2, Pallas kernels, couple(): pl.pallas_call(kernel, grid_spec=pltpu.PrefetchScalarGridSpec(num_scalar_...  28.7 us
    pallas_call x3, Pallas kernels, edge_strips(): pl.pallas_call(kernel, grid=(made // block,), in_specs=streams + [pl.Bloc...  12.8 us
    pallas_call x4, Pallas kernels, settle(): pl.pallas_call(kernel, in_specs=[anywhere] * (len(ks) + len(extra)), out_...  11.1 us
    ppermute x3, waiting for transfers between devices, exchange(): far = lax.ppermute(far, 'sector', pairs)  7.7 us
    ppermute x3, starting transfers between devices, exchange(): far = lax.ppermute(far, 'sector', pairs)  6.61 us
  transfers between devices with their start and end apart: 48, of which 14 were waited for; matrix products, arithmetic and copies ran while one was open for 3% of the time, Pallas kernels for 30%

profile of v2, /device:TPU:0, one launch (start us, length us, event | category | flops | bytes accessed | tf_op | source)
XLA Modules:
  0.0 318.8 jit_solution(10307784629711938171)
XLA Ops:
  0.0 3.6 %edge_strips.3 = (f32[37,8,128]{2,1,0:T(8,128)}, f32[37,8,128]{2,1,0:T(8,128)}) custom-call(f32[144,128,128]{2,1,0:T(8,128)} %wave_ref.5, f32[144,128,128]{2,1,0:T(8,128)} %wave_ref.5, f32[144,128,128]{2,1,0:T(8,128)} %wave_ref.5, s32[128,128]{1,0:T(8,128)} %land_ref.5), custom_call_target="tpu_custom_call" | custom-call | bytes 4718592 | tf_op jit(solution)/shard_map/edge_strips/pallas_call | solution.py:54
  3.6 3.1 collective-permute-start
  6.6 2.5 collective-permute-start.1
  9.1 4.0 %edge_strips.4 = (f32[49,8,128]{2,1,0:T(8,128)}, f32[49,8,128]{2,1,0:T(8,128)}) custom-call(f32[144,128,128]{2,1,0:T(8,128)} %wave_ref.5, f32[144,128,128]{2,1,0:T(8,128)} %wave_ref.5, f32[144,128,128]{2,1,0:T(8,128)} %wave_ref.5, s32[128,128]{1,0:T(8,128)} %land_ref.5), custom_call_target="tpu_custom_call" | custom-call | bytes 6291456 | tf_op jit(solution)/shard_map/edge_strips/pallas_call | solution.py:54
  13.1 0.7 collective-permute-start.9
  13.8 0.9 collective-permute-start.10
  14.7 2.7 collective-permute-done.1.far_ref.far_sea_ref
  18.1 12.3 %advance.3 = (f32[36,16,128]{2,1,0:T(8,128)}, f32[36,16,128]{2,1,0:T(8,128)}, f32[36,16,128]{2,1,0:T(8,128)}, f32[36,16,128]{2,1,0:T(8,128)}, f32[36,16,128]{2,1...) custom-call(s32[1152]{0:T(1024)} %kinds_ref.9, f32[32]{0:T(128)} %courant_ref.5, ...), custom_call_target="tpu_custom_call" | custom-call | bytes 28311552 | tf_op jit(solution)/shard_map/advance/pallas_call | solution.py:162
  30.5 5.2 %edge_strips.5 = (f32[61,8,128]{2,1,0:T(8,128)}, f32[61,8,128]{2,1,0:T(8,128)}) custom-call(f32[144,128,128]{2,1,0:T(8,128)} %wave_ref.5, f32[144,128,128]{2,1,0:T(8,128)} %wave_ref.5, f32[144,128,128]{2,1,0:T(8,128)} %wave_ref.5, s32[128,128]{1,0:T(8,128)} %land_ref.5), custom_call_target="tpu_custom_call" | custom-call | bytes 7864320 | tf_op jit(solution)/shard_map/edge_strips/pallas_call | solution.py:54
  35.7 3.2 %collective-permute-start.19 = (f32[61,8,128]{2,1,0:T(8,128)}, f32[61,8,128]{2,1,0:T(8,128)S(1)}, u32[]{:S(2)}, u32[]{:S(2)}) collective-permute-start(f32[61,8,128]{2,1,0:T(8,128)} %get-tuple-element.80), channel_id=1, source_target_pairs={{0,24},{8,16},{16,8},{24,0},{1,25},{9,17},{17,9},{25,1},{2,26},{10... | collective-permute-start | bytes 749576 | tf_op jit(solution)/shard_map/ppermute | solution.py:364
  38.9 1.6 collective-permute-start.3
  40.5 3.7 %collective-permute-done.18.near_ref.near_sea_ref = f32[61,8,128]{2,1,0:T(8,128)S(1)} collective-permute-done((f32[61,8,128]{2,1,0:T(8,128)}, f32[61,8,128]{2,1,0:T(8,128)S(1)}, u32[]{:S(2)}, u32[]{:S(2)}) %collective-permute-start.18) | collective-permute-done | bytes 249888 | tf_op jit(solution)/shard_map/ppermute | solution.py:362
  44.2 1.5 collective-permute-start.5
  45.8 5.0 %collective-permute-done.19.far_ref.far_sea_ref = f32[61,8,128]{2,1,0:T(8,128)S(1)} collective-permute-done((f32[61,8,128]{2,1,0:T(8,128)}, f32[61,8,128]{2,1,0:T(8,128)S(1)}, u32[]{:S(2)}, u32[]{:S(2)}) %collective-permute-start.19) | collective-permute-done | bytes 249888 | tf_op jit(solution)/shard_map/ppermute | solution.py:364
  50.8 0.7 collective-permute-start.6
  51.5 1.9 collective-permute-start.7
  53.4 1.4 collective-permute-start.8
  54.8 19.3 %advance.5 = (f32[60,8,128]{2,1,0:T(8,128)}, f32[60,8,128]{2,1,0:T(8,128)}, f32[60,8,128]{2,1,0:T(8,128)}, f32[60,8,128]{2,1,0:T(8,128)}, f32[60,8,128]{2,1,0:T(...) custom-call(s32[1152]{0:T(1024)} %kinds_ref.9, ...), custom_call_target="tpu_custom_call" | custom-call | bytes 47185920 | tf_op jit(solution)/shard_map/advance/pallas_call | solution.py:162
  74.3 1.6 collective-permute-start.35
  76.7 15.6 %advance.4 = (f32[48,16,128]{2,1,0:T(8,128)}, f32[48,16,128]{2,1,0:T(8,128)}, f32[48,16,128]{2,1,0:T(8,128)}, f32[48,16,128]{2,1,0:T(8,128)}, f32[48,16,128]{2,1...) custom-call(s32[1152]{0:T(1024)} %kinds_ref.9, f32[32]{0:T(128)} %courant_ref.5, ...), custom_call_target="tpu_custom_call" | custom-call | bytes 37748736 | tf_op jit(solution)/shard_map/advance/pallas_call | solution.py:162
  92.6 1.6 collective-permute-start.12
  94.2 1.1 collective-permute-start.38
  95.7 2.2 collective-permute-start.40
  98.0 4.5 %collective-permute-done.38.rest_21_ = f32[60,8,128]{2,1,0:T(8,128)S(1)} collective-permute-done((f32[60,8,128]{2,1,0:T(8,128)}, f32[60,8,128]{2,1,0:T(8,128)S(1)}, u32[]{:S(2)}, u32[]{:S(2)}) %collective-permute-start.38) | collective-permute-done | bytes 245792 | tf_op jit(solution)/shard_map/ppermute | solution.py:355
  102.9 8.0 %collective-permute-done.39.rest_22_ = f32[60,8,128]{2,1,0:T(8,128)S(1)} collective-permute-done((f32[60,8,128]{2,1,0:T(8,128)}, f32[60,8,128]{2,1,0:T(8,128)S(1)}, u32[]{:S(2)}, u32[]{:S(2)}) %collective-permute-start.39) | collective-permute-done | bytes 245792 | tf_op jit(solution)/shard_map/ppermute | solution.py:355
  111.5 3.6 %collective-permute-done.40.rest_23_ = f32[60,8,128]{2,1,0:T(8,128)S(1)} collective-permute-done((f32[60,8,128]{2,1,0:T(8,128)}, f32[60,8,128]{2,1,0:T(8,128)S(1)}, u32[]{:S(2)}, u32[]{:S(2)}) %collective-permute-start.40) | collective-permute-done | bytes 245792 | tf_op jit(solution)/shard_map/ppermute | solution.py:355
  115.1 1.1 collective-permute-start.15
  116.3 2.4 collective-permute-start.16
  118.8 0.8 mul.62
  120.5 1.0 mul.60
  121.5 2.3 fusion
  123.8 0.7 collective-permute-start.20
  124.8 1.5 collective-permute-start.21
  126.3 23.0 %collective-permute-done.15.rest_13_ = f32[48,16,128]{2,1,0:T(8,128)} collective-permute-done((f32[48,16,128]{2,1,0:T(8,128)}, f32[48,16,128]{2,1,0:T(8,128)}, u32[]{:S(2)}, u32[]{:S(2)}) %collective-permute-start.15) | collective-permute-done | bytes 393248 | tf_op jit(solution)/shard_map/ppermute | solution.py:355
  149.3 1.3 collective-permute-start.22
  151.1 1.3 collective-permute-start.24
  153.0 1.3 dynamic-slice_convert_fusion.rest_24_
  154.3 1.0 broadcast_in_dim.44.rest_27_
  155.3 1.0 broadcast_in_dim.45.rest_28_
  156.4 1.0 broadcast_in_dim.42.rest_26_
  157.4 1.1 broadcast_in_dim.48.rest_29_
  158.5 14.4 %couple.3 = (f32[144,8,128]{2,1,0:T(8,128)}, f32[144,8,128]{2,1,0:T(8,128)}, f32[144,8,128]{2,1,0:T(8,128)}, f32[144,8,128]{2,1,0:T(8,128)}, f32[144,8,128]{2,1,...) custom-call(s32[1152]{0:T(1024)} %kinds_ref.9, ...), custom_call_target="tpu_custom_call" | custom-call | bytes 37748736 | tf_op jit(solution)/shard_map/couple/pallas_call | solution.py:281
  174.0 0.7 copy-done.27
  174.7 2.5 collective-permute-start.43
  177.2 0.7 copy-done.29
  177.9 1.1 collective-permute-start.25
  179.0 40.4 %collective-permute-done.25.rest_22_ = f32[60,8,128]{2,1,0:T(8,128)S(1)} collective-permute-done((f32[60,8,128]{2,1,0:T(8,128)}, f32[60,8,128]{2,1,0:T(8,128)S(1)}, u32[]{:S(2)}, u32[]{:S(2)}) %collective-permute-start.25) | collective-permute-done | bytes 245792 | tf_op jit(solution)/shard_map/ppermute | solution.py:355
  219.9 8.5 %collective-permute-done.26.rest_23_ = f32[60,8,128]{2,1,0:T(8,128)S(1)} collective-permute-done((f32[60,8,128]{2,1,0:T(8,128)}, f32[60,8,128]{2,1,0:T(8,128)S(1)}, u32[]{:S(2)}, u32[]{:S(2)}) %collective-permute-start.26) | collective-permute-done | bytes 245792 | tf_op jit(solution)/shard_map/ppermute | solution.py:355
  228.4 0.7 copy-done.32
  229.1 0.9 collective-permute-start.45
  230.0 14.3 %couple.2 = (f32[144,8,128]{2,1,0:T(8,128)}, f32[144,8,128]{2,1,0:T(8,128)}, f32[144,8,128]{2,1,0:T(8,128)}, f32[144,8,128]{2,1,0:T(8,128)}, f32[144,8,128]{2,1,...) custom-call(s32[1152]{0:T(1024)} %kinds_ref.9, ...), custom_call_target="tpu_custom_call" | custom-call | bytes 37748736 | tf_op jit(solution)/shard_map/couple/pallas_call | solution.py:281
  244.4 1.1 collective-permute-start.46
  246.0 1.3 collective-permute-start.31
  247.5 12.8 %collective-permute-done.46.rest_6_ = f32[144,8,128]{2,1,0:T(8,128)S(1)} collective-permute-done((f32[144,8,128]{2,1,0:T(8,128)}, f32[144,8,128]{2,1,0:T(8,128)S(1)}, u32[]{:S(2)}, u32[]{:S(2)}) %collective-permute-start.46) | collective-permute-done | bytes 589856 | tf_op jit(solution)/shard_map/ppermute | solution.py:355
  260.3 0.7 collective-permute-start.32
  261.0 1.3 collective-permute-start.33
  262.3 1.4 collective-permute-start.29
  263.7 10.2 %collective-permute-done.31.rest_2_ = f32[144,8,128]{2,1,0:T(8,128)} collective-permute-done((f32[144,8,128]{2,1,0:T(8,128)}, f32[144,8,128]{2,1,0:T(8,128)}, u32[]{:S(2)}, u32[]{:S(2)}) %collective-permute-start.31) | collective-permute-done | bytes 589856 | tf_op jit(solution)/shard_map/ppermute | solution.py:355
  273.9 4.4 %settle.4.rest_5_ = f32[144,128,128]{2,1,0:T(8,128)} custom-call(f32[144,8,128]{2,1,0:T(8,128)} %get-tuple-element.105.rest_0_, f32[144,8,128]{2,1,0:T(8,128)} %copy-done.12, f32[144,8,128]{2,1,0:T(8,128)} %copy-done.13, f32[144,8,128]{2,1,0:T(8,128)} %copy-done.14, f32[144,8,128]{2,1,0:T(8,128)} %copy-done.15, f32[144,8,128]{2,1,0:T(8,128)} %copy-done.16, ...), custom_call_target="tpu_custom_call" | custom-call | bytes 9437184 | tf_op jit(solution)/shard_map/settle/pallas_call | solution.py:325
  278.4 21.8 %collective-permute-done.33.rest_4_ = f32[144,8,128]{2,1,0:T(8,128)} collective-permute-done((f32[144,8,128]{2,1,0:T(8,128)}, f32[144,8,128]{2,1,0:T(8,128)}, u32[]{:S(2)}, u32[]{:S(2)}) %collective-permute-start.33) | collective-permute-done | bytes 589856 | tf_op jit(solution)/shard_map/ppermute | solution.py:355
  300.2 2.7 settle.5.rest_2_
  302.9 11.8 %collective-permute-done.29.rest_1_ = f32[144,8,128]{2,1,0:T(8,128)} collective-permute-done((f32[144,8,128]{2,1,0:T(8,128)}, f32[144,8,128]{2,1,0:T(8,128)}, u32[]{:S(2)}, u32[]{:S(2)}) %collective-permute-start.29) | collective-permute-done | bytes 589856 | tf_op jit(solution)/shard_map/ppermute | solution.py:355
  314.7 2.1 settle.6.rest_1_
  316.9 1.9 settle.7
  (156 shorter events, 8.3 us)
Async XLA Ops:
  3.6 11.1 %collective-permute-start = (f32[37,8,128]{2,1,0:T(8,128)}, f32[37,8,128]{2,1,0:T(8,128)S(1)}, u32[]{:S(2)}, u32[]{:S(2)}) collective-permute-start(f32[37,8,128]{2,1,0:T(8,128)} %get-tuple-element.59), channel_id=1, source_target_pairs={{0,8},{8,0},{16,24},{24,16},{1,9},{9,1},{17,25},{25,17},{2,10},{10... | collective-permute-start | bytes 454664 | tf_op jit(solution)/shard_map/ppermute | solution.py:362
  6.6 10.8 %collective-permute-start.1 = (f32[37,8,128]{2,1,0:T(8,128)}, f32[37,8,128]{2,1,0:T(8,128)S(1)}, u32[]{:S(2)}, u32[]{:S(2)}) collective-permute-start(f32[37,8,128]{2,1,0:T(8,128)} %get-tuple-element.60), channel_id=1, source_target_pairs={{0,24},{8,16},{16,8},{24,0},{1,25},{9,17},{17,9},{25,1},{2,26},{10... | collective-permute-start | bytes 454664 | tf_op jit(solution)/shard_map/ppermute | solution.py:364
  13.1 25.8 %collective-permute-start.9 = (f32[49,8,128]{2,1,0:T(8,128)}, f32[49,8,128]{2,1,0:T(8,128)S(1)}, u32[]{:S(2)}, u32[]{:S(2)}) collective-permute-start(f32[49,8,128]{2,1,0:T(8,128)} %get-tuple-element.69), channel_id=1, source_target_pairs={{0,8},{8,0},{16,24},{24,16},{1,9},{9,1},{17,25},{25,17},{2,10},{10... | collective-permute-start | bytes 602120 | tf_op jit(solution)/shard_map/ppermute | solution.py:362
  13.8 26.7 %collective-permute-start.10 = (f32[49,8,128]{2,1,0:T(8,128)}, f32[49,8,128]{2,1,0:T(8,128)S(1)}, u32[]{:S(2)}, u32[]{:S(2)}) collective-permute-start(f32[49,8,128]{2,1,0:T(8,128)} %get-tuple-element.70), channel_id=1, source_target_pairs={{0,24},{8,16},{16,8},{24,0},{1,25},{9,17},{17,9},{25,1},{2,26},{10... | collective-permute-start | bytes 602120 | tf_op jit(solution)/shard_map/ppermute | solution.py:364
  30.4 21.1 %collective-permute-start.2 = (f32[36,16,128]{2,1,0:T(8,128)}, f32[36,16,128]{2,1,0:T(8,128)S(1)}, u32[]{:S(2)}, u32[]{:S(2)}) collective-permute-start(f32[36,16,128]{2,1,0:T(8,128)} %get-tuple-element.62), channel_id=1, source_target_pairs={{0,1},{1,0},{2,3},{3,2},{4,5},{5,4},{6,7},{7,6},{8,9},{9,8},{10,11... | collective-permute-start | bytes 884744 | tf_op jit(solution)/shard_map/ppermute | solution.py:355
  35.7 8.6 %collective-permute-start.18 = (f32[61,8,128]{2,1,0:T(8,128)}, f32[61,8,128]{2,1,0:T(8,128)S(1)}, u32[]{:S(2)}, u32[]{:S(2)}) collective-permute-start(f32[61,8,128]{2,1,0:T(8,128)} %get-tuple-element.79), channel_id=1, source_target_pairs={{0,8},{8,0},{16,24},{24,16},{1,9},{9,1},{17,25},{25,17},{2,10},{10... | collective-permute-start | bytes 749576 | tf_op jit(solution)/shard_map/ppermute | solution.py:362
  35.7 15.1 %collective-permute-start.19 = (f32[61,8,128]{2,1,0:T(8,128)}, f32[61,8,128]{2,1,0:T(8,128)S(1)}, u32[]{:S(2)}, u32[]{:S(2)}) collective-permute-start(f32[61,8,128]{2,1,0:T(8,128)} %get-tuple-element.80), channel_id=1, source_target_pairs={{0,24},{8,16},{16,8},{24,0},{1,25},{9,17},{17,9},{25,1},{2,26},{10... | collective-permute-start | bytes 749576 | tf_op jit(solution)/shard_map/ppermute | solution.py:364
  38.9 37.7 %copy-start.8 = (f32[49,8,128]{2,1,0:T(8,128)}, f32[49,8,128]{2,1,0:T(8,128)S(1)}, u32[]{:S(2)}) copy-start(f32[49,8,128]{2,1,0:T(8,128)S(1)} %collective-permute-done.9.near_ref.near_sea_ref) | copy-start | bytes 602116
  38.9 14.5 %collective-permute-start.3 = (f32[36,16,128]{2,1,0:T(8,128)S(1)}, f32[36,16,128]{2,1,0:T(8,128)}, u32[]{:S(2)}, u32[]{:S(2)}) collective-permute-start(f32[36,16,128]{2,1,0:T(8,128)S(1)} %copy-done.41), channel_id=1, source_target_pairs={{0,2},{1,3},{2,0},{3,1},{4,6},{5,7},{6,4},{7,5},{8,10},{9,11},{10,... | collective-permute-start | bytes 884744 | tf_op jit(solution)/shard_map/ppermute | solution.py:355
  40.5 36.2 %copy-start.9 = (f32[49,8,128]{2,1,0:T(8,128)}, f32[49,8,128]{2,1,0:T(8,128)S(1)}, u32[]{:S(2)}) copy-start(f32[49,8,128]{2,1,0:T(8,128)S(1)} %collective-permute-done.10.far_ref.far_sea_ref) | copy-start | bytes 602116
  40.5 33.7 %collective-permute-start.4 = (f32[36,16,128]{2,1,0:T(8,128)}, f32[36,16,128]{2,1,0:T(8,128)S(1)}, u32[]{:S(2)}, u32[]{:S(2)}) collective-permute-start(f32[36,16,128]{2,1,0:T(8,128)} %get-tuple-element.64), channel_id=1, source_target_pairs={{0,3},{1,2},{2,1},{3,0},{4,7},{5,6},{6,5},{7,4},{8,11},{9,10},{10,... | collective-permute-start | bytes 884744 | tf_op jit(solution)/shard_map/ppermute | solution.py:355
  44.2 30.0 %collective-permute-start.5 = (f32[36,16,128]{2,1,0:T(8,128)S(1)}, f32[36,16,128]{2,1,0:T(8,128)S(1)}, u32[]{:S(2)}, u32[]{:S(2)}) collective-permute-start(f32[36,16,128]{2,1,0:T(8,128)S(1)} %copy-done.40), channel_id=1, source_target_pairs={{0,4},{1,5},{2,6},{3,7},{4,0},{5,1},{6,2},{7,3},{8,12},{9,13},{10,... | collective-permute-start | bytes 884744 | tf_op jit(solution)/shard_map/ppermute | solution.py:355
  50.8 25.0 %collective-permute-start.6 = (f32[36,16,128]{2,1,0:T(8,128)S(1)}, f32[36,16,128]{2,1,0:T(8,128)S(1)}, u32[]{:S(2)}, u32[]{:S(2)}) collective-permute-start(f32[36,16,128]{2,1,0:T(8,128)S(1)} %copy-done.39), channel_id=1, source_target_pairs={{0,5},{1,4},{2,7},{3,6},{4,1},{5,0},{6,3},{7,2},{8,13},{9,12},{10,... | collective-permute-start | bytes 884744 | tf_op jit(solution)/shard_map/ppermute | solution.py:355
  51.5 24.6 %collective-permute-start.7 = (f32[36,16,128]{2,1,0:T(8,128)S(1)}, f32[36,16,128]{2,1,0:T(8,128)S(1)}, u32[]{:S(2)}, u32[]{:S(2)}) collective-permute-start(f32[36,16,128]{2,1,0:T(8,128)S(1)} %copy-done.38), channel_id=1, source_target_pairs={{0,6},{1,7},{2,4},{3,5},{4,2},{5,3},{6,0},{7,1},{8,14},{9,15},{10,... | collective-permute-start | bytes 884744 | tf_op jit(solution)/shard_map/ppermute | solution.py:355
  53.4 38.9 %collective-permute-start.8 = (f32[36,16,128]{2,1,0:T(8,128)}, f32[36,16,128]{2,1,0:T(8,128)S(1)}, u32[]{:S(2)}, u32[]{:S(2)}) collective-permute-start(f32[36,16,128]{2,1,0:T(8,128)} %get-tuple-element.68), channel_id=1, source_target_pairs={{0,7},{1,6},{2,5},{3,4},{4,3},{5,2},{6,1},{7,0},{8,15},{9,14},{10,... | collective-permute-start | bytes 884744 | tf_op jit(solution)/shard_map/ppermute | solution.py:355
  74.2 18.4 %collective-permute-start.34 = (f32[60,8,128]{2,1,0:T(8,128)}, f32[60,8,128]{2,1,0:T(8,128)S(1)}, u32[]{:S(2)}, u32[]{:S(2)}) collective-permute-start(f32[60,8,128]{2,1,0:T(8,128)} %get-tuple-element.98), channel_id=1, source_target_pairs={{0,1},{1,0},{2,3},{3,2},{4,5},{5,4},{6,7},{7,6},{8,9},{9,8},{10,11... | collective-permute-start | bytes 737288 | tf_op jit(solution)/shard_map/ppermute | solution.py:355
  74.3 19.9 %collective-permute-start.35 = (f32[60,8,128]{2,1,0:T(8,128)}, f32[60,8,128]{2,1,0:T(8,128)S(1)}, u32[]{:S(2)}, u32[]{:S(2)}) collective-permute-start(f32[60,8,128]{2,1,0:T(8,128)} %get-tuple-element.99), channel_id=1, source_target_pairs={{0,2},{1,3},{2,0},{3,1},{4,6},{5,7},{6,4},{7,5},{8,10},{9,11},{10,... | collective-permute-start | bytes 737288 | tf_op jit(solution)/shard_map/ppermute | solution.py:355
  75.8 19.4 %collective-permute-start.36 = (f32[60,8,128]{2,1,0:T(8,128)}, f32[60,8,128]{2,1,0:T(8,128)S(1)}, u32[]{:S(2)}, u32[]{:S(2)}) collective-permute-start(f32[60,8,128]{2,1,0:T(8,128)} %get-tuple-element.100), channel_id=1, source_target_pairs={{0,3},{1,2},{2,1},{3,0},{4,7},{5,6},{6,5},{7,4},{8,11},{9,10},{10,... | collective-permute-start | bytes 737288 | tf_op jit(solution)/shard_map/ppermute | solution.py:355
  76.1 19.6 %collective-permute-start.37 = (f32[60,8,128]{2,1,0:T(8,128)}, f32[60,8,128]{2,1,0:T(8,128)S(1)}, u32[]{:S(2)}, u32[]{:S(2)}) collective-permute-start(f32[60,8,128]{2,1,0:T(8,128)} %get-tuple-element.101), channel_id=1, source_target_pairs={{0,4},{1,5},{2,6},{3,7},{4,0},{5,1},{6,2},{7,3},{8,12},{9,13},{10,... | collective-permute-start | bytes 737288 | tf_op jit(solution)/shard_map/ppermute | solution.py:355
  92.3 23.9 %collective-permute-start.11 = (f32[48,16,128]{2,1,0:T(8,128)}, f32[48,16,128]{2,1,0:T(8,128)}, u32[]{:S(2)}, u32[]{:S(2)}) collective-permute-start(f32[48,16,128]{2,1,0:T(8,128)} %get-tuple-element.72), channel_id=1, source_target_pairs={{0,1},{1,0},{2,3},{3,2},{4,5},{5,4},{6,7},{7,6},{8,9},{9,8},{10,11... | collective-permute-start | bytes 1179656 | tf_op jit(solution)/shard_map/ppermute | solution.py:355
  92.6 26.0 %collective-permute-start.12 = (f32[48,16,128]{2,1,0:T(8,128)}, f32[48,16,128]{2,1,0:T(8,128)}, u32[]{:S(2)}, u32[]{:S(2)}) collective-permute-start(f32[48,16,128]{2,1,0:T(8,128)} %get-tuple-element.73), channel_id=1, source_target_pairs={{0,2},{1,3},{2,0},{3,1},{4,6},{5,7},{6,4},{7,5},{8,10},{9,11},{10,... | collective-permute-start | bytes 1179656 | tf_op jit(solution)/shard_map/ppermute | solution.py:355
  94.2 8.3 %collective-permute-start.38 = (f32[60,8,128]{2,1,0:T(8,128)}, f32[60,8,128]{2,1,0:T(8,128)S(1)}, u32[]{:S(2)}, u32[]{:S(2)}) collective-permute-start(f32[60,8,128]{2,1,0:T(8,128)} %get-tuple-element.102), channel_id=1, source_target_pairs={{0,5},{1,4},{2,7},{3,6},{4,1},{5,0},{6,3},{7,2},{8,13},{9,12},{10,... | collective-permute-start | bytes 737288 | tf_op jit(solution)/shard_map/ppermute | solution.py:355
  95.3 15.6 %collective-permute-start.39 = (f32[60,8,128]{2,1,0:T(8,128)}, f32[60,8,128]{2,1,0:T(8,128)S(1)}, u32[]{:S(2)}, u32[]{:S(2)}) collective-permute-start(f32[60,8,128]{2,1,0:T(8,128)} %get-tuple-element.103), channel_id=1, source_target_pairs={{0,6},{1,7},{2,4},{3,5},{4,2},{5,3},{6,0},{7,1},{8,14},{9,15},{10,... | collective-permute-start | bytes 737288 | tf_op jit(solution)/shard_map/ppermute | solution.py:355
  95.7 19.4 %collective-permute-start.40 = (f32[60,8,128]{2,1,0:T(8,128)}, f32[60,8,128]{2,1,0:T(8,128)S(1)}, u32[]{:S(2)}, u32[]{:S(2)}) collective-permute-start(f32[60,8,128]{2,1,0:T(8,128)} %get-tuple-element.104), channel_id=1, source_target_pairs={{0,7},{1,6},{2,5},{3,4},{4,3},{5,2},{6,1},{7,0},{8,15},{9,14},{10,... | collective-permute-start | bytes 737288 | tf_op jit(solution)/shard_map/ppermute | solution.py:355
  102.5 21.3 %collective-permute-start.13 = (f32[48,16,128]{2,1,0:T(8,128)}, f32[48,16,128]{2,1,0:T(8,128)}, u32[]{:S(2)}, u32[]{:S(2)}) collective-permute-start(f32[48,16,128]{2,1,0:T(8,128)} %get-tuple-element.74), channel_id=1, source_target_pairs={{0,3},{1,2},{2,1},{3,0},{4,7},{5,6},{6,5},{7,4},{8,11},{9,10},{10,... | collective-permute-start | bytes 1179656 | tf_op jit(solution)/shard_map/ppermute | solution.py:355
  110.9 13.9 %collective-permute-start.14 = (f32[48,16,128]{2,1,0:T(8,128)}, f32[48,16,128]{2,1,0:T(8,128)}, u32[]{:S(2)}, u32[]{:S(2)}) collective-permute-start(f32[48,16,128]{2,1,0:T(8,128)} %get-tuple-element.75), channel_id=1, source_target_pairs={{0,4},{1,5},{2,6},{3,7},{4,0},{5,1},{6,2},{7,3},{8,12},{9,13},{10,... | collective-permute-start | bytes 1179656 | tf_op jit(solution)/shard_map/ppermute | solution.py:355
  115.1 34.2 %collective-permute-start.15 = (f32[48,16,128]{2,1,0:T(8,128)}, f32[48,16,128]{2,1,0:T(8,128)}, u32[]{:S(2)}, u32[]{:S(2)}) collective-permute-start(f32[48,16,128]{2,1,0:T(8,128)} %get-tuple-element.76), channel_id=1, source_target_pairs={{0,5},{1,4},{2,7},{3,6},{4,1},{5,0},{6,3},{7,2},{8,13},{9,12},{10,... | collective-permute-start | bytes 1179656 | tf_op jit(solution)/shard_map/ppermute | solution.py:355
  116.3 34.3 %collective-permute-start.16 = (f32[48,16,128]{2,1,0:T(8,128)}, f32[48,16,128]{2,1,0:T(8,128)}, u32[]{:S(2)}, u32[]{:S(2)}) collective-permute-start(f32[48,16,128]{2,1,0:T(8,128)} %get-tuple-element.77), channel_id=1, source_target_pairs={{0,6},{1,7},{2,4},{3,5},{4,2},{5,3},{6,0},{7,1},{8,14},{9,15},{10,... | collective-permute-start | bytes 1179656 | tf_op jit(solution)/shard_map/ppermute | solution.py:355
  118.6 32.4 %collective-permute-start.17 = (f32[48,16,128]{2,1,0:T(8,128)}, f32[48,16,128]{2,1,0:T(8,128)}, u32[]{:S(2)}, u32[]{:S(2)}) collective-permute-start(f32[48,16,128]{2,1,0:T(8,128)} %get-tuple-element.78), channel_id=1, source_target_pairs={{0,7},{1,6},{2,5},{3,4},{4,3},{5,2},{6,1},{7,0},{8,15},{9,14},{10,... | collective-permute-start | bytes 1179656 | tf_op jit(solution)/shard_map/ppermute | solution.py:355
  120.4 31.9 %copy-start.33 = (f32[36]{0:T(128)S(1)}, f32[36]{0:T(128)}, u32[]{:S(2)}) copy-start(f32[36]{0:T(128)} %constant.19.clone.sin_ref) | copy-start | bytes 436
  120.4 31.9 %copy-start.34 = (f32[36]{0:T(128)S(1)}, f32[36]{0:T(128)}, u32[]{:S(2)}) copy-start(f32[36]{0:T(128)} %constant.18.clone.cos_ref) | copy-start | bytes 436
  120.4 31.9 %copy-start.35 = (f32[32]{0:T(128)S(1)}, f32[32]{0:T(128)}, u32[]{:S(2)}) copy-start(f32[32]{0:T(128)} %param.17) | copy-start | bytes 388
  120.4 32.0 %copy-start.36 = (f32[32]{0:T(128)S(1)}, f32[32]{0:T(128)}, u32[]{:S(2)}) copy-start(f32[32]{0:T(128)} %param.18) | copy-start | bytes 388
  121.5 27.8 %copy-start.43 = (f32[60,8,128]{2,1,0:T(8,128)S(1)}, f32[60,8,128]{2,1,0:T(8,128)}, u32[]{:S(2)}) copy-start(f32[60,8,128]{2,1,0:T(8,128)} %get-tuple-element.84) | copy-start | bytes 737284
  121.5 29.1 %copy-start.42 = (f32[60,8,128]{2,1,0:T(8,128)S(1)}, f32[60,8,128]{2,1,0:T(8,128)}, u32[]{:S(2)}) copy-start(f32[60,8,128]{2,1,0:T(8,128)} %get-tuple-element.85) | copy-start | bytes 737284
  121.5 31.1 %copy-start.37 = (f32[32]{0:T(128)S(1)}, f32[32]{0:T(128)}, u32[]{:S(2)}) copy-start(f32[32]{0:T(128)} %param.19) | copy-start | bytes 388
  123.8 49.1 %collective-permute-start.20 = (f32[60,8,128]{2,1,0:T(8,128)S(1)}, f32[60,8,128]{2,1,0:T(8,128)S(1)}, u32[]{:S(2)}, u32[]{:S(2)}) collective-permute-start(f32[60,8,128]{2,1,0:T(8,128)S(1)} %copy-done.45), channel_id=1, source_target_pairs={{0,1},{1,0},{2,3},{3,2},{4,5},{5,4},{6,7},{7,6},{8,9},{9,8},{10,11... | collective-permute-start | bytes 737288 | tf_op jit(solution)/shard_map/ppermute | solution.py:355
  124.8 48.7 %collective-permute-start.21 = (f32[60,8,128]{2,1,0:T(8,128)S(1)}, f32[60,8,128]{2,1,0:T(8,128)S(1)}, u32[]{:S(2)}, u32[]{:S(2)}) collective-permute-start(f32[60,8,128]{2,1,0:T(8,128)S(1)} %copy-done.44), channel_id=1, source_target_pairs={{0,2},{1,3},{2,0},{3,1},{4,6},{5,7},{6,4},{7,5},{8,10},{9,11},{10,... | collective-permute-start | bytes 737288 | tf_op jit(solution)/shard_map/ppermute | solution.py:355
  149.3 24.7 %collective-permute-start.22 = (f32[60,8,128]{2,1,0:T(8,128)S(1)}, f32[60,8,128]{2,1,0:T(8,128)S(1)}, u32[]{:S(2)}, u32[]{:S(2)}) collective-permute-start(f32[60,8,128]{2,1,0:T(8,128)S(1)} %copy-done.43), channel_id=1, source_target_pairs={{0,3},{1,2},{2,1},{3,0},{4,7},{5,6},{6,5},{7,4},{8,11},{9,10},{10,... | collective-permute-start | bytes 737288 | tf_op jit(solution)/shard_map/ppermute | solution.py:355
  150.6 26.6 %collective-permute-start.23 = (f32[60,8,128]{2,1,0:T(8,128)S(1)}, f32[60,8,128]{2,1,0:T(8,128)S(1)}, u32[]{:S(2)}, u32[]{:S(2)}) collective-permute-start(f32[60,8,128]{2,1,0:T(8,128)S(1)} %copy-done.42), channel_id=1, source_target_pairs={{0,4},{1,5},{2,6},{3,7},{4,0},{5,1},{6,2},{7,3},{8,12},{9,13},{10,... | collective-permute-start | bytes 737288 | tf_op jit(solution)/shard_map/ppermute | solution.py:355
  151.1 26.8 %collective-permute-start.24 = (f32[60,8,128]{2,1,0:T(8,128)}, f32[60,8,128]{2,1,0:T(8,128)S(1)}, u32[]{:S(2)}, u32[]{:S(2)}) collective-permute-start(f32[60,8,128]{2,1,0:T(8,128)} %get-tuple-element.86), channel_id=1, source_target_pairs={{0,5},{1,4},{2,7},{3,6},{4,1},{5,0},{6,3},{7,2},{8,13},{9,12},{10,... | collective-permute-start | bytes 737288 | tf_op jit(solution)/shard_map/ppermute | solution.py:355
  172.9 57.1 %copy-start.23 = (f32[60,8,128]{2,1,0:T(8,128)}, f32[60,8,128]{2,1,0:T(8,128)S(1)}, u32[]{:S(2)}) copy-start(f32[60,8,128]{2,1,0:T(8,128)S(1)} %collective-permute-done.20.rest_17_) | copy-start | bytes 737284
  172.9 71.4 %collective-permute-start.41 = (f32[144,8,128]{2,1,0:T(8,128)}, f32[144,8,128]{2,1,0:T(8,128)S(1)}, u32[]{:S(2)}, u32[]{:S(2)}) collective-permute-start(f32[144,8,128]{2,1,0:T(8,128)} %get-tuple-element.106), channel_id=1, source_target_pairs={{0,2},{1,3},{2,0},{3,1},{4,6},{5,7},{6,4},{7,5},{8,10},{9,11},{10,... | collective-permute-start | bytes 1769480 | tf_op jit(solution)/shard_map/ppermute | solution.py:355
  173.5 56.5 %copy-start.25 = (f32[60,8,128]{2,1,0:T(8,128)}, f32[60,8,128]{2,1,0:T(8,128)S(1)}, u32[]{:S(2)}) copy-start(f32[60,8,128]{2,1,0:T(8,128)S(1)} %collective-permute-done.21.rest_18_) | copy-start | bytes 737284
  173.5 72.0 %collective-permute-start.42 = (f32[144,8,128]{2,1,0:T(8,128)}, f32[144,8,128]{2,1,0:T(8,128)S(1)}, u32[]{:S(2)}, u32[]{:S(2)}) collective-permute-start(f32[144,8,128]{2,1,0:T(8,128)} %get-tuple-element.107), channel_id=1, source_target_pairs={{0,4},{1,5},{2,6},{3,7},{4,0},{5,1},{6,2},{7,3},{8,12},{9,13},{10,... | collective-permute-start | bytes 1769480 | tf_op jit(solution)/shard_map/ppermute | solution.py:355
  174.7 70.9 %collective-permute-start.43 = (f32[144,8,128]{2,1,0:T(8,128)}, f32[144,8,128]{2,1,0:T(8,128)S(1)}, u32[]{:S(2)}, u32[]{:S(2)}) collective-permute-start(f32[144,8,128]{2,1,0:T(8,128)} %get-tuple-element.108), channel_id=1, source_target_pairs={{0,6},{1,7},{2,4},{3,5},{4,2},{5,3},{6,0},{7,1},{8,14},{9,15},{10,... | collective-permute-start | bytes 1769480 | tf_op jit(solution)/shard_map/ppermute | solution.py:355
  177.9 68.2 %collective-permute-start.44 = (f32[144,8,128]{2,1,0:T(8,128)}, f32[144,8,128]{2,1,0:T(8,128)S(1)}, u32[]{:S(2)}, u32[]{:S(2)}) collective-permute-start(f32[144,8,128]{2,1,0:T(8,128)} %get-tuple-element.109), channel_id=1, source_target_pairs={{0,3},{1,2},{2,1},{3,0},{4,7},{5,6},{6,5},{7,4},{8,11},{9,10},{10,... | collective-permute-start | bytes 1769480 | tf_op jit(solution)/shard_map/ppermute | solution.py:355
  177.9 50.5 %copy-start.30 = (f32[60,8,128]{2,1,0:T(8,128)}, f32[60,8,128]{2,1,0:T(8,128)S(1)}, u32[]{:S(2)}) copy-start(f32[60,8,128]{2,1,0:T(8,128)S(1)} %collective-permute-done.24.rest_21_) | copy-start | bytes 737284
  177.9 41.4 %collective-permute-start.25 = (f32[60,8,128]{2,1,0:T(8,128)}, f32[60,8,128]{2,1,0:T(8,128)S(1)}, u32[]{:S(2)}, u32[]{:S(2)}) collective-permute-start(f32[60,8,128]{2,1,0:T(8,128)} %get-tuple-element.87), channel_id=1, source_target_pairs={{0,6},{1,7},{2,4},{3,5},{4,2},{5,3},{6,0},{7,1},{8,14},{9,15},{10,... | collective-permute-start | bytes 737288 | tf_op jit(solution)/shard_map/ppermute | solution.py:355
  219.3 9.1 %collective-permute-start.26 = (f32[60,8,128]{2,1,0:T(8,128)}, f32[60,8,128]{2,1,0:T(8,128)S(1)}, u32[]{:S(2)}, u32[]{:S(2)}) collective-permute-start(f32[60,8,128]{2,1,0:T(8,128)} %get-tuple-element.88), channel_id=1, source_target_pairs={{0,7},{1,6},{2,5},{3,4},{4,3},{5,2},{6,1},{7,0},{8,15},{9,14},{10,... | collective-permute-start | bytes 737288 | tf_op jit(solution)/shard_map/ppermute | solution.py:355
  229.1 18.2 %collective-permute-start.45 = (f32[144,8,128]{2,1,0:T(8,128)}, f32[144,8,128]{2,1,0:T(8,128)S(1)}, u32[]{:S(2)}, u32[]{:S(2)}) collective-permute-start(f32[144,8,128]{2,1,0:T(8,128)} %get-tuple-element.110), channel_id=1, source_target_pairs={{0,5},{1,4},{2,7},{3,6},{4,1},{5,0},{6,3},{7,2},{8,13},{9,12},{10,... | collective-permute-start | bytes 1769480 | tf_op jit(solution)/shard_map/ppermute | solution.py:355
  244.4 29.5 %copy-start.12 = (f32[144,8,128]{2,1,0:T(8,128)}, f32[144,8,128]{2,1,0:T(8,128)S(1)}, u32[]{:S(2)}) copy-start(f32[144,8,128]{2,1,0:T(8,128)S(1)} %collective-permute-done.41.rest_1_) | copy-start | bytes 1769476
  244.4 15.9 %collective-permute-start.46 = (f32[144,8,128]{2,1,0:T(8,128)}, f32[144,8,128]{2,1,0:T(8,128)S(1)}, u32[]{:S(2)}, u32[]{:S(2)}) collective-permute-start(f32[144,8,128]{2,1,0:T(8,128)} %get-tuple-element.111), channel_id=1, source_target_pairs={{0,7},{1,6},{2,5},{3,4},{4,3},{5,2},{6,1},{7,0},{8,15},{9,14},{10,... | collective-permute-start | bytes 1769480 | tf_op jit(solution)/shard_map/ppermute | solution.py:355
  245.5 28.4 %copy-start.13 = (f32[144,8,128]{2,1,0:T(8,128)}, f32[144,8,128]{2,1,0:T(8,128)S(1)}, u32[]{:S(2)}) copy-start(f32[144,8,128]{2,1,0:T(8,128)S(1)} %collective-permute-done.42.rest_2_) | copy-start | bytes 1769476
  245.5 15.5 %collective-permute-start.47 = (f32[144,8,128]{2,1,0:T(8,128)}, f32[144,8,128]{2,1,0:T(8,128)}, u32[]{:S(2)}, u32[]{:S(2)}) collective-permute-start(f32[144,8,128]{2,1,0:T(8,128)} %get-tuple-element.112), channel_id=1, source_target_pairs={{0,1},{1,0},{2,3},{3,2},{4,5},{5,4},{6,7},{7,6},{8,9},{9,8},{10,11... | collective-permute-start | bytes 1769480 | tf_op jit(solution)/shard_map/ppermute | solution.py:355
  245.6 28.3 %copy-start.14 = (f32[144,8,128]{2,1,0:T(8,128)}, f32[144,8,128]{2,1,0:T(8,128)S(1)}, u32[]{:S(2)}) copy-start(f32[144,8,128]{2,1,0:T(8,128)S(1)} %collective-permute-done.43.rest_3_) | copy-start | bytes 1769476
  245.6 16.7 %collective-permute-start.30 = (f32[144,8,128]{2,1,0:T(8,128)}, f32[144,8,128]{2,1,0:T(8,128)}, u32[]{:S(2)}, u32[]{:S(2)}) collective-permute-start(f32[144,8,128]{2,1,0:T(8,128)} %get-tuple-element.93), channel_id=1, source_target_pairs={{0,1},{1,0},{2,3},{3,2},{4,5},{5,4},{6,7},{7,6},{8,9},{9,8},{10,11... | collective-permute-start | bytes 1769480 | tf_op jit(solution)/shard_map/ppermute | solution.py:355
  246.0 27.9 %copy-start.15 = (f32[144,8,128]{2,1,0:T(8,128)}, f32[144,8,128]{2,1,0:T(8,128)S(1)}, u32[]{:S(2)}) copy-start(f32[144,8,128]{2,1,0:T(8,128)S(1)} %collective-permute-done.44.rest_4_) | copy-start | bytes 1769476
  246.0 27.9 %collective-permute-start.31 = (f32[144,8,128]{2,1,0:T(8,128)}, f32[144,8,128]{2,1,0:T(8,128)}, u32[]{:S(2)}, u32[]{:S(2)}) collective-permute-start(f32[144,8,128]{2,1,0:T(8,128)} %get-tuple-element.94), channel_id=1, source_target_pairs={{0,2},{1,3},{2,0},{3,1},{4,6},{5,7},{6,4},{7,5},{8,10},{9,11},{10,... | collective-permute-start | bytes 1769480 | tf_op jit(solution)/shard_map/ppermute | solution.py:355
  247.3 55.6 %collective-permute-start.28 = (f32[144,8,128]{2,1,0:T(8,128)}, f32[144,8,128]{2,1,0:T(8,128)}, u32[]{:S(2)}, u32[]{:S(2)}) collective-permute-start(f32[144,8,128]{2,1,0:T(8,128)} %get-tuple-element.90), channel_id=1, source_target_pairs={{0,3},{1,2},{2,1},{3,0},{4,7},{5,6},{6,5},{7,4},{8,11},{9,10},{10,... | collective-permute-start | bytes 1769480 | tf_op jit(solution)/shard_map/ppermute | solution.py:355
  260.3 18.0 %collective-permute-start.32 = (f32[144,8,128]{2,1,0:T(8,128)}, f32[144,8,128]{2,1,0:T(8,128)}, u32[]{:S(2)}, u32[]{:S(2)}) collective-permute-start(f32[144,8,128]{2,1,0:T(8,128)} %get-tuple-element.95), channel_id=1, source_target_pairs={{0,4},{1,5},{2,6},{3,7},{4,0},{5,1},{6,2},{7,3},{8,12},{9,13},{10,... | collective-permute-start | bytes 1769480 | tf_op jit(solution)/shard_map/ppermute | solution.py:355
  261.0 39.1 %collective-permute-start.33 = (f32[144,8,128]{2,1,0:T(8,128)}, f32[144,8,128]{2,1,0:T(8,128)}, u32[]{:S(2)}, u32[]{:S(2)}) collective-permute-start(f32[144,8,128]{2,1,0:T(8,128)} %get-tuple-element.96), channel_id=1, source_target_pairs={{0,6},{1,7},{2,4},{3,5},{4,2},{5,3},{6,0},{7,1},{8,14},{9,15},{10,... | collective-permute-start | bytes 1769480 | tf_op jit(solution)/shard_map/ppermute | solution.py:355
  262.3 52.4 %collective-permute-start.29 = (f32[144,8,128]{2,1,0:T(8,128)}, f32[144,8,128]{2,1,0:T(8,128)}, u32[]{:S(2)}, u32[]{:S(2)}) collective-permute-start(f32[144,8,128]{2,1,0:T(8,128)} %get-tuple-element.91), channel_id=1, source_target_pairs={{0,5},{1,4},{2,7},{3,6},{4,1},{5,0},{6,3},{7,2},{8,13},{9,12},{10,... | collective-permute-start | bytes 1769480 | tf_op jit(solution)/shard_map/ppermute | solution.py:355
  273.9 43.0 %collective-permute-start.27 = (f32[144,8,128]{2,1,0:T(8,128)}, f32[144,8,128]{2,1,0:T(8,128)}, u32[]{:S(2)}, u32[]{:S(2)}) collective-permute-start(f32[144,8,128]{2,1,0:T(8,128)} %get-tuple-element.89), channel_id=1, source_target_pairs={{0,7},{1,6},{2,5},{3,4},{4,3},{5,2},{6,1},{7,0},{8,15},{9,14},{10,... | collective-permute-start | bytes 1769480 | tf_op jit(solution)/shard_map/ppermute | solution.py:355
  (30 other events, 410.1 us)

commit v3 on v2

--- a/solution.py
+++ b/solution.py
@@ -10,25 +10,33 @@
 
 
 DIRS = 36
-FREQ = 32
 SUBSTEPS = 6
 EDGE = 8
 ROWS = 8
 UNITS = 24
-CHUNKS = (6, 8, 10)
-STRIP_BLOCKS = 12
+CHUNKS = (7, 7, 10)
+STRIP_BLOCKS = 10
 STREAMS = 3
 BAND = 4
 PAD = 8
 LANES = 3
 
 
-def edge_strips(spectrum, land_mask, base, made, block):
+def strip_blocks(base, made, most):
+    for block in range(most, 0, -1):
+        for streams in range(STREAMS, 0, -1):
+            part = block // streams
+            if made % block == 0 and block % streams == 0 and base % part == 0:
+                return block, streams
+
+
+def edge_strips(spectrum, land_mask, base, made, most):
     _, lat, lon = spectrum.shape
-    part = block // STREAMS
+    block, copies = strip_blocks(base, made, most)
+    part = block // copies
 
     def kernel(*rest):
-        waves, (land_ref, near_ref, far_ref, turned) = rest[:STREAMS], rest[STREAMS:]
+        waves, (land_ref, near_ref, far_ref, turned) = rest[:copies], rest[copies:]
         step = pl.program_id(0)
         even = lax.rem(lax.axis_index("sector"), 2) == 0
         near = pl.multiple_of(jnp.where(even, lon - EDGE, 0), EDGE)
@@ -48,8 +56,8 @@
     shape = jax.ShapeDtypeStruct((made + 1, EDGE, lat), jnp.float32)
     first = base // part
     streams = [
-        pl.BlockSpec((part, lat, lon), lambda i, *_, n=n: (first + i * STREAMS + n, 0, 0))
-        for n in range(STREAMS)
+        pl.BlockSpec((part, lat, lon), lambda i, *_, n=n: (first + i * copies + n, 0, 0))
+        for n in range(copies)
     ]
     return pl.pallas_call(
         kernel,
@@ -62,7 +70,7 @@
             flops=0, bytes_accessed=8 * made * lat * lon, transcendentals=0
         ),
         name="edge_strips",
-    )(*[spectrum] * STREAMS, land_mask)
+    )(*[spectrum] * copies, land_mask)
 
 
 def advance(tables, spectrum, strips, land_mask, inverse, base, made, block, count, pieces):
@@ -197,9 +205,52 @@
     )(*tables, spectrum, *strips, *strips, land_mask, inverse)
 
 
-def couple(assignment, arrived, sea_rows, winds, per_kind, blocks, count, comps_dev, part):
+def coupling_tables(growth, whitecap, weights, spread, cosine, sine, after, lon):
+    freqs, dirs, _ = spread.shape
+    comps = freqs * dirs
+    bands, band = freqs // BAND, BAND * dirs
+
+    def kernel(growth_ref, decay_ref, weight_ref, spread_ref, cos_ref, sin_ref, _, *rest):
+        weights_ref, east_ref, north_ref, decays_ref, high_ref, low_ref, whole = rest
+        one = jnp.ones((dirs, lon), jnp.float32)
+        for f in range(freqs):
+            rows = slice(f * dirs, (f + 1) * dirs)
+            weights_ref[rows] = weight_ref[f] * one
+            east_ref[rows] = growth_ref[f] * cos_ref[...]
+            north_ref[rows] = growth_ref[f] * sin_ref[...]
+            decays_ref[rows] = decay_ref[f] * one
+        whole[...] = jnp.zeros_like(whole)
+        for n in range(bands):
+            for q in range(BAND):
+                spot = slice(q * dirs, (q + 1) * dirs)
+                whole[spot, spot] = 0.5 * spread_ref[n * BAND + q]
+            high = whole[...].astype(jnp.bfloat16)
+            high_ref[n] = high
+            low_ref[n] = (whole[...] - high.astype(jnp.float32)).astype(jnp.bfloat16)
+
+    scalars = pl.BlockSpec(memory_space=pltpu.SMEM)
+    vmem = pl.BlockSpec(memory_space=pltpu.VMEM)
+    spread_out = lambda values: jnp.asarray(np.repeat(values[:, None], lon, axis=1))
+    rates = jax.ShapeDtypeStruct((comps, lon), jnp.float32)
+    part = jax.ShapeDtypeStruct((bands, band, band), jnp.bfloat16)
+    made = pl.pallas_call(
+        kernel,
+        in_specs=[scalars] * 3 + [vmem] * 3 + [pl.BlockSpec(memory_space=pl.ANY)],
+        out_specs=[vmem] * 6,
+        out_shape=[rates] * 4 + [part] * 2,
+        scratch_shapes=[pltpu.VMEM((band, band), jnp.float32)],
+        cost_estimate=pl.CostEstimate(
+            flops=0, bytes_accessed=20 * comps * lon, transcendentals=0
+        ),
+        name="coupling_tables",
+    )(growth, whitecap, weights, spread, spread_out(cosine), spread_out(sine), after)
+    return made[:4], made[4:]
+
+
+def couple(assignment, arrived, land_mask, winds, per_kind, blocks, count, comps_dev, part):
     comps = assignment.shape[0]
-    lon = sea_rows.shape[1]
+    lon = land_mask.shape[1]
+    rows_dev = winds.shape[1]
     bands, band, _ = blocks[0].shape
     flat = [a for group, _ in arrived for a in group]
     sizes = [group[0].shape[0] for group, _ in arrived]
@@ -208,7 +259,7 @@
 
     def kernel(kinds_ref, *rest):
         ins, rest = rest[: len(flat)], rest[len(flat) :]
-        sea_ref, wind_ref, weight_ref, east_ref, north_ref, decay_ref, high_ref, low_ref = rest[:8]
+        land_ref, wind_ref, weight_ref, east_ref, north_ref, decay_ref, high_ref, low_ref = rest[:8]
         outs, (sorted_ref,) = rest[8:-1], rest[-1:]
         me = lax.axis_index("group")
         for k in range(count):
@@ -238,7 +289,8 @@
                 loads.append(loading / (1.0 + loading))
                 us.append(wind_ref[0, pl.ds(j, 1), :])
                 vs.append(wind_ref[1, pl.ds(j, 1), :])
-                seas.append(sea_ref[pl.ds(j, 1), :])
+                sea_row = land_ref[pl.ds(me * rows_dev + part * ROWS + j, 1), :]
+                seas.append(sea_row.astype(jnp.float32))
             for n in range(bands):
                 kinds = slice(n * band, (n + 1) * band)
                 spots = [pl.ds(pl.multiple_of(starts[q] + n * band, 8), band) for q in range(2)]
@@ -276,14 +328,13 @@
         for group, at in arrived
         for a in group
     ]
-    rows = pl.BlockSpec((ROWS, lon), lambda *_: (part, 0))
     wind_rows = pl.BlockSpec((2, ROWS, lon), lambda *_: (0, part, 0))
     return pl.pallas_call(
         kernel,
         grid_spec=pltpu.PrefetchScalarGridSpec(
             num_scalar_prefetch=1,
             grid=(1,),
-            in_specs=pieces + [rows, wind_rows] + [vmem] * 6,
+            in_specs=pieces + [vmem, wind_rows] + [vmem] * 6,
             out_specs=[vmem] * count,
             scratch_shapes=[pltpu.VMEM((ROWS * pitch, lon), jnp.float32)],
         ),
@@ -292,7 +343,7 @@
             flops=0, bytes_accessed=8 * comps * ROWS * lon * 4, transcendentals=0
         ),
         name="couple",
-    )(assignment, *flat, sea_rows, winds, *per_kind, *blocks)
+    )(assignment, *flat, land_mask, winds, *per_kind, *blocks)
 
 
 def settle(returned, ks, part, rows_dev, lat, partial):
@@ -346,7 +397,7 @@
 
 def stages_of(count):
     order = order_of(count)
-    return [[0, 1] + order[: count - 5], order[count - 5 : count - 3], order[count - 3 : count - 2]]
+    return [[0, 1] + order[: count - 5], order[count - 5 : count - 4], order[count - 4 : count - 2]]
 
 
 def swap(pieces, count):
@@ -366,21 +417,17 @@
 
 
 def local(spectrum, land_mask, wind_field, assignment, courant, growth, whitecap, weights, spread):
-    member = lax.axis_index("group").astype(jnp.int32)
     count = lax.axis_size("group")
     comps_dev, lat, lon = spectrum.shape
-    comps = assignment.shape[0]
     rows_dev = wind_field.shape[1]
     parts = rows_dev // ROWS
     unit = comps_dev // UNITS
 
     angles = (np.arange(DIRS) + 0.5) * (2.0 * math.pi / DIRS)
-    cosine = jnp.asarray(np.cos(angles), jnp.float32)
-    sine = jnp.asarray(np.sin(angles), jnp.float32)
+    cosine, sine = np.float32(np.cos(angles)), np.float32(np.sin(angles))
     latitude = (np.arange(lat) + 0.5 - lat / 2) * (math.pi / 2160.0)
     inverse = jnp.asarray(1.0 / np.cos(latitude), jnp.float32)[None, :]
-    sea_mask = land_mask.astype(jnp.float32)
-    tables = (assignment, courant, cosine, sine)
+    tables = (assignment, courant, jnp.asarray(cosine), jnp.asarray(sine))
 
     arrived = [[] for _ in range(parts)]
     base = 0
@@ -403,27 +450,14 @@
                     arrived[part].append((group, 0))
         base += made
 
-    def spread_out(values):
-        return jnp.broadcast_to(values[:, None], (comps, lon))
-
-    fast = jnp.repeat(growth, DIRS)
-    per_kind = (
-        spread_out(jnp.repeat(weights, DIRS)),
-        spread_out(fast * jnp.tile(cosine, FREQ)),
-        spread_out(fast * jnp.tile(sine, FREQ)),
-        spread_out(jnp.repeat(whitecap, DIRS)),
+    per_kind, blocks = coupling_tables(
+        growth, whitecap, weights, spread, cosine, sine, sent[0], lon
     )
-    halves = (0.5 * spread).reshape(FREQ // BAND, BAND, DIRS, 1, DIRS)
-    same = jnp.eye(BAND, dtype=jnp.float32)[None, :, None, :, None]
-    whole = (halves * same).reshape(FREQ // BAND, BAND * DIRS, BAND * DIRS)
-    high = lax.reduce_precision(whole, 8, 7)
-    blocks = (high.astype(jnp.bfloat16), (whole - high).astype(jnp.bfloat16))
-    sea_rows = lax.dynamic_slice_in_dim(sea_mask, member * rows_dev, rows_dev, 0)
 
     returned = []
     for part in range(parts):
         made = couple(
-            assignment, arrived[part], sea_rows, wind_field, per_kind, blocks,
+            assignment, arrived[part], land_mask, wind_field, per_kind, blocks,
             count, comps_dev, part,
         )
         returned.append(swap(made, count))

time: 319 us -> 314 us (0.984)
  local copies, waits for them, and re-layouts: 10.4 us -> 3.78 us
  other arithmetic: 3.7 us -> 0 us
    ppermute x42, waiting for transfers between devices: 145 us -> 151 us  [swap(): lax.ppermute(pieces[k], 'group', [(i, i ^ k) for i in range(count)])]
    broadcast_in_dim x8 -> x0, local copies, waits for them, and re-layouts: 4.56 us -> none  [the longest x6 4.42 us: spread_out(): return jnp.broadcast_to(values[:, None], (comps, lon))]
    ppermute x3, waiting for transfers between devices: 3.75 us -> 0.01 us  [exchange(): near = lax.ppermute(near, 'sector', pairs)]
    convert_element_type x3 -> x0, other arithmetic: 3.58 us -> none  [the longest x1 2.28 us: local(): blocks = (high.astype(jnp.bfloat16), (whole - high).astype(jnp.bfloat16))]
  transfers between devices with their start and end apart: 48 -> 48, of which waited for: 14 -> 13; matrix products, arithmetic and copies ran while one was open for 3% -> 1% of each run, Pallas kernels for 30% -> 31%
where the time goes in v3:
time: 314 us; the launch traced here: 313 us
  waiting for transfers between devices  157 us (50%)
  Pallas kernels  103 us (33%)
  starting transfers between devices  48.9 us (16%)
  local copies, waits for them, and re-layouts  3.78 us (1%)
    ppermute x42, waiting for transfers between devices, swap(): lax.ppermute(pieces[k], 'group', [(i, i ^ k) for i in range(count)])  151 us
    pallas_call x3, Pallas kernels, advance(): pl.pallas_call(kernel, grid_spec=pltpu.PrefetchScalarGridSpec(num_scalar_...  47.2 us
    ppermute x42, starting transfers between devices, swap(): lax.ppermute(pieces[k], 'group', [(i, i ^ k) for i in range(count)])  39 us
    pallas_call x2, Pallas kernels, couple(): pl.pallas_call(kernel, grid_spec=pltpu.PrefetchScalarGridSpec(num_scalar_...  29 us
    pallas_call x3, Pallas kernels, edge_strips(): pl.pallas_call(kernel, grid=(made // block,), in_specs=streams + [pl.Bloc...  12.5 us
    pallas_call x4, Pallas kernels, settle(): pl.pallas_call(kernel, in_specs=[anywhere] * (len(ks) + len(extra)), out_...  11.1 us
  transfers between devices with their start and end apart: 48, of which 13 were waited for; matrix products, arithmetic and copies ran while one was open for 1% of the time, Pallas kernels for 31%

profile of v3, /device:TPU:0, one launch (start us, length us, event | category | flops | bytes accessed | tf_op | source)
XLA Modules:
  0.0 313.5 jit_solution(13098510301849170183)
XLA Ops:
  0.0 5.1 %edge_strips.5 = (f32[61,8,128]{2,1,0:T(8,128)}, f32[61,8,128]{2,1,0:T(8,128)}) custom-call(f32[144,128,128]{2,1,0:T(8,128)} %wave_ref.5, f32[144,128,128]{2,1,0:T(8,128)} %wave_ref.5, f32[144,128,128]{2,1,0:T(8,128)} %wave_ref.5, s32[128,128]{1,0:T(8,128)} %rest_24_.3), custom_call_target="tpu_custom_call" | custom-call | bytes 7864320 | tf_op jit(solution)/shard_map/edge_strips/pallas_call | solution.py:62
  5.1 3.1 collective-permute-start.18
  8.1 2.5 collective-permute-start.19
  10.6 3.7 %edge_strips.4 = (f32[43,8,128]{2,1,0:T(8,128)}, f32[43,8,128]{2,1,0:T(8,128)}) custom-call(f32[144,128,128]{2,1,0:T(8,128)} %wave_ref.5, f32[144,128,128]{2,1,0:T(8,128)} %wave_ref.5, s32[128,128]{1,0:T(8,128)} %rest_24_.3), custom_call_target="tpu_custom_call" | custom-call | bytes 5505024 | tf_op jit(solution)/shard_map/edge_strips/pallas_call | solution.py:62
  14.3 0.7 collective-permute-start.9
  15.0 0.9 collective-permute-start.10
  15.9 3.7 %edge_strips.3 = (f32[43,8,128]{2,1,0:T(8,128)}, f32[43,8,128]{2,1,0:T(8,128)}) custom-call(f32[144,128,128]{2,1,0:T(8,128)} %wave_ref.5, f32[144,128,128]{2,1,0:T(8,128)} %wave_ref.5, s32[128,128]{1,0:T(8,128)} %rest_24_.3), custom_call_target="tpu_custom_call" | custom-call | bytes 5505024 | tf_op jit(solution)/shard_map/edge_strips/pallas_call | solution.py:62
  19.6 0.9 collective-permute-start
  20.5 2.5 collective-permute-done.19.far_ref.far_sea_ref
  23.1 0.7 copy-done.11
  23.8 19.3 %advance.5 = (f32[60,8,128]{2,1,0:T(8,128)}, f32[60,8,128]{2,1,0:T(8,128)}, f32[60,8,128]{2,1,0:T(8,128)}, f32[60,8,128]{2,1,0:T(8,128)}, f32[60,8,128]{2,1,0:T(...) custom-call(s32[1152]{0:T(1024)} %kinds_ref.9, ...), custom_call_target="tpu_custom_call" | custom-call | bytes 47185920 | tf_op jit(solution)/shard_map/advance/pallas_call | solution.py:170
  43.2 1.9 collective-permute-start.1
  45.1 1.5 collective-permute-start.35
  46.6 1.6 collective-permute-start.37
  48.3 3.6 %collective-permute-done.1.far_ref.far_sea_ref = f32[43,8,128]{2,1,0:T(8,128)S(1)} collective-permute-done((f32[43,8,128]{2,1,0:T(8,128)S(1)}, f32[43,8,128]{2,1,0:T(8,128)S(1)}, u32[]{:S(2)}, u32[]{:S(2)}) %collective-permute-start.1) | collective-permute-done | bytes 176160 | tf_op jit(solution)/shard_map/ppermute | solution.py:415
  51.9 0.7 collective-permute-start.38
  52.6 1.9 collective-permute-start.39
  54.5 14.0 %advance.3 = (f32[42,16,128]{2,1,0:T(8,128)}, f32[42,16,128]{2,1,0:T(8,128)}, f32[42,16,128]{2,1,0:T(8,128)}, f32[42,16,128]{2,1,0:T(8,128)}, f32[42,16,128]{2,1...) custom-call(s32[1152]{0:T(1024)} %kinds_ref.9, f32[32]{0:T(128)} %courant_ref.5, ...), custom_call_target="tpu_custom_call" | custom-call | bytes 33030144 | tf_op jit(solution)/shard_map/advance/pallas_call | solution.py:170
  69.2 0.5 collective-permute-start.3
  69.9 0.9 collective-permute-start.4
  70.9 1.7 collective-permute-start.5
  72.6 0.5 collective-permute-start.40
  73.0 14.0 %advance.4 = (f32[42,16,128]{2,1,0:T(8,128)}, f32[42,16,128]{2,1,0:T(8,128)}, f32[42,16,128]{2,1,0:T(8,128)}, f32[42,16,128]{2,1,0:T(8,128)}, f32[42,16,128]{2,1...) custom-call(s32[1152]{0:T(1024)} %kinds_ref.9, f32[32]{0:T(128)} %courant_ref.5, ...), custom_call_target="tpu_custom_call" | custom-call | bytes 33030144 | tf_op jit(solution)/shard_map/advance/pallas_call | solution.py:170
  87.0 5.9 %collective-permute-done.40.rest_23_ = f32[60,8,128]{2,1,0:T(8,128)S(1)} collective-permute-done((f32[60,8,128]{2,1,0:T(8,128)S(1)}, f32[60,8,128]{2,1,0:T(8,128)S(1)}, u32[]{:S(2)}, u32[]{:S(2)}) %collective-permute-start.40) | collective-permute-done | bytes 245792 | tf_op jit(solution)/shard_map/ppermute | solution.py:406
  93.2 1.6 collective-permute-start.7
  94.8 0.8 collective-permute-start.8
  95.6 0.8 collective-permute-start.11
  96.4 0.5 collective-permute-start.12
  96.9 20.7 %collective-permute-done.6.rest_5_ = f32[42,16,128]{2,1,0:T(8,128)S(1)} collective-permute-done((f32[42,16,128]{2,1,0:T(8,128)S(1)}, f32[42,16,128]{2,1,0:T(8,128)S(1)}, u32[]{:S(2)}, u32[]{:S(2)}) %collective-permute-start.6) | collective-permute-done | bytes 344096 | tf_op jit(solution)/shard_map/ppermute | solution.py:406
  117.6 0.7 collective-permute-start.13
  118.4 1.2 collective-permute-start.15
  119.6 1.7 collective-permute-start.16
  121.3 1.3 collective-permute-start.17
  122.6 4.8 %collective-permute-done.13.rest_11_ = f32[42,16,128]{2,1,0:T(8,128)S(1)} collective-permute-done((f32[42,16,128]{2,1,0:T(8,128)}, f32[42,16,128]{2,1,0:T(8,128)S(1)}, u32[]{:S(2)}, u32[]{:S(2)}) %collective-permute-start.13) | collective-permute-done | bytes 344096 | tf_op jit(solution)/shard_map/ppermute | solution.py:406
  127.4 1.7 collective-permute-start.20
  129.1 15.1 %collective-permute-done.14.rest_12_ = f32[42,16,128]{2,1,0:T(8,128)} collective-permute-done((f32[42,16,128]{2,1,0:T(8,128)}, f32[42,16,128]{2,1,0:T(8,128)}, u32[]{:S(2)}, u32[]{:S(2)}) %collective-permute-start.14) | collective-permute-done | bytes 344096 | tf_op jit(solution)/shard_map/ppermute | solution.py:406
  144.2 1.5 collective-permute-start.21
  145.7 3.9 %collective-permute-done.15.rest_13_ = f32[42,16,128]{2,1,0:T(8,128)} collective-permute-done((f32[42,16,128]{2,1,0:T(8,128)}, f32[42,16,128]{2,1,0:T(8,128)}, u32[]{:S(2)}, u32[]{:S(2)}) %collective-permute-start.15) | collective-permute-done | bytes 344096 | tf_op jit(solution)/shard_map/ppermute | solution.py:406
  149.6 2.2 collective-permute-start.22
  152.1 0.5 collective-permute-start.24
  152.6 2.2 copy.18.spread_ref
  154.8 3.2 %coupling_tables.1 = (f32[1152,128]{1,0:T(8,128)}, f32[1152,128]{1,0:T(8,128)}, f32[1152,128]{1,0:T(8,128)}, f32[1152,128]{1,0:T(8,128)}, bf16[8,144,144]{2,1,0:T(8,128)(2,1)}, /*index=5*/bf16[8,144,144]{2,1,0:T(8,128)(2,1)}) custom-call(f32[32]{0:T(128)} %growth_ref.1, f32[32]{0:T(128)} %decay_ref.1, f32[32]{0:T(128)} %weight_ref.1, ...), custom_call_target="tpu_custom_call" | custom-call | bytes 2949120 | tf_op jit(solution)/shard_map/coupling_tables/pallas_call | solution.py:236
  158.1 14.5 %couple.3 = (f32[144,8,128]{2,1,0:T(8,128)}, f32[144,8,128]{2,1,0:T(8,128)}, f32[144,8,128]{2,1,0:T(8,128)}, f32[144,8,128]{2,1,0:T(8,128)}, f32[144,8,128]{2,1,...) custom-call(s32[1152]{0:T(1024)} %kinds_ref.9, ...), custom_call_target="tpu_custom_call" | custom-call | bytes 37748736 | tf_op jit(solution)/shard_map/couple/pallas_call | solution.py:332
  172.6 1.1 collective-permute-start.41
  173.7 0.8 collective-permute-start.42
  174.5 1.7 collective-permute-start.43
  176.2 0.7 collective-permute-start.44
  176.9 1.3 collective-permute-start.25
  178.2 41.7 %collective-permute-done.25.rest_22_ = f32[60,8,128]{2,1,0:T(8,128)S(1)} collective-permute-done((f32[60,8,128]{2,1,0:T(8,128)}, f32[60,8,128]{2,1,0:T(8,128)S(1)}, u32[]{:S(2)}, u32[]{:S(2)}) %collective-permute-start.25) | collective-permute-done | bytes 245792 | tf_op jit(solution)/shard_map/ppermute | solution.py:406
  219.8 1.3 collective-permute-start.26
  221.1 7.8 %collective-permute-done.26.rest_23_ = f32[60,8,128]{2,1,0:T(8,128)S(1)} collective-permute-done((f32[60,8,128]{2,1,0:T(8,128)}, f32[60,8,128]{2,1,0:T(8,128)S(1)}, u32[]{:S(2)}, u32[]{:S(2)}) %collective-permute-start.26) | collective-permute-done | bytes 245792 | tf_op jit(solution)/shard_map/ppermute | solution.py:406
  228.9 0.6 collective-permute-start.45
  229.6 14.5 %couple.2 = (f32[144,8,128]{2,1,0:T(8,128)}, f32[144,8,128]{2,1,0:T(8,128)}, f32[144,8,128]{2,1,0:T(8,128)}, f32[144,8,128]{2,1,0:T(8,128)}, f32[144,8,128]{2,1,...) custom-call(s32[1152]{0:T(1024)} %kinds_ref.9, ...), custom_call_target="tpu_custom_call" | custom-call | bytes 37748736 | tf_op jit(solution)/shard_map/couple/pallas_call | solution.py:332
  244.1 1.5 collective-permute-start.46
  246.1 1.1 collective-permute-start.31
  247.6 13.2 %collective-permute-done.46.rest_6_ = f32[144,8,128]{2,1,0:T(8,128)} collective-permute-done((f32[144,8,128]{2,1,0:T(8,128)}, f32[144,8,128]{2,1,0:T(8,128)}, u32[]{:S(2)}, u32[]{:S(2)}) %collective-permute-start.46) | collective-permute-done | bytes 589856 | tf_op jit(solution)/shard_map/ppermute | solution.py:406
  261.0 2.3 collective-permute-start.33
  263.7 10.1 %collective-permute-done.31.rest_2_ = f32[144,8,128]{2,1,0:T(8,128)} collective-permute-done((f32[144,8,128]{2,1,0:T(8,128)}, f32[144,8,128]{2,1,0:T(8,128)}, u32[]{:S(2)}, u32[]{:S(2)}) %collective-permute-start.31) | collective-permute-done | bytes 589856 | tf_op jit(solution)/shard_map/ppermute | solution.py:406
  274.2 4.4 %settle.4.rest_5_ = f32[144,128,128]{2,1,0:T(8,128)} custom-call(f32[144,8,128]{2,1,0:T(8,128)} %get-tuple-element.117.rest_0_, f32[144,8,128]{2,1,0:T(8,128)} %copy-done.16, f32[144,8,128]{2,1,0:T(8,128)} %copy-done.17, f32[144,8,128]{2,1,0:T(8,128)} %copy-done.18, f32[144,8,128]{2,1,0:T(8,128)} %copy-done.19, f32[144,8,128]{2,1,0:T(8,128)} %copy-done.20, ...), custom_call_target="tpu_custom_call" | custom-call | bytes 9437184 | tf_op jit(solution)/shard_map/settle/pallas_call | solution.py:376
  278.6 20.6 %collective-permute-done.32.rest_3_ = f32[144,8,128]{2,1,0:T(8,128)} collective-permute-done((f32[144,8,128]{2,1,0:T(8,128)}, f32[144,8,128]{2,1,0:T(8,128)}, u32[]{:S(2)}, u32[]{:S(2)}) %collective-permute-start.32) | collective-permute-done | bytes 589856 | tf_op jit(solution)/shard_map/ppermute | solution.py:406
  299.2 2.7 settle.5.rest_1_
  301.9 1.9 settle.6.rest_2_
  303.8 7.6 %collective-permute-done.28.rest_1_ = f32[144,8,128]{2,1,0:T(8,128)} collective-permute-done((f32[144,8,128]{2,1,0:T(8,128)}, f32[144,8,128]{2,1,0:T(8,128)}, u32[]{:S(2)}, u32[]{:S(2)}) %collective-permute-start.28) | collective-permute-done | bytes 589856 | tf_op jit(solution)/shard_map/ppermute | solution.py:406
  311.3 2.1 settle.7
  (114 shorter events, 3.9 us)
Async XLA Ops:
  5.1 15.5 %collective-permute-start.18 = (f32[61,8,128]{2,1,0:T(8,128)}, f32[61,8,128]{2,1,0:T(8,128)S(1)}, u32[]{:S(2)}, u32[]{:S(2)}) collective-permute-start(f32[61,8,128]{2,1,0:T(8,128)} %get-tuple-element.85), channel_id=1, source_target_pairs={{0,8},{8,0},{16,24},{24,16},{1,9},{9,1},{17,25},{25,17},{2,10},{10... | collective-permute-start | bytes 749576 | tf_op jit(solution)/shard_map/ppermute | solution.py:413
  8.1 15.0 %collective-permute-start.19 = (f32[61,8,128]{2,1,0:T(8,128)}, f32[61,8,128]{2,1,0:T(8,128)S(1)}, u32[]{:S(2)}, u32[]{:S(2)}) collective-permute-start(f32[61,8,128]{2,1,0:T(8,128)} %get-tuple-element.86), channel_id=1, source_target_pairs={{0,24},{8,16},{16,8},{24,0},{1,25},{9,17},{17,9},{25,1},{2,26},{10... | collective-permute-start | bytes 749576 | tf_op jit(solution)/shard_map/ppermute | solution.py:415
  14.3 30.8 %collective-permute-start.9 = (f32[43,8,128]{2,1,0:T(8,128)}, f32[43,8,128]{2,1,0:T(8,128)S(1)}, u32[]{:S(2)}, u32[]{:S(2)}) collective-permute-start(f32[43,8,128]{2,1,0:T(8,128)} %get-tuple-element.75), channel_id=1, source_target_pairs={{0,8},{8,0},{16,24},{24,16},{1,9},{9,1},{17,25},{25,17},{2,10},{10... | collective-permute-start | bytes 528392 | tf_op jit(solution)/shard_map/ppermute | solution.py:413
  15.0 31.6 %collective-permute-start.10 = (f32[43,8,128]{2,1,0:T(8,128)}, f32[43,8,128]{2,1,0:T(8,128)S(1)}, u32[]{:S(2)}, u32[]{:S(2)}) collective-permute-start(f32[43,8,128]{2,1,0:T(8,128)} %get-tuple-element.76), channel_id=1, source_target_pairs={{0,24},{8,16},{16,8},{24,0},{1,25},{9,17},{17,9},{25,1},{2,26},{10... | collective-permute-start | bytes 528392 | tf_op jit(solution)/shard_map/ppermute | solution.py:415
  19.6 27.0 %collective-permute-start = (f32[43,8,128]{2,1,0:T(8,128)}, f32[43,8,128]{2,1,0:T(8,128)S(1)}, u32[]{:S(2)}, u32[]{:S(2)}) collective-permute-start(f32[43,8,128]{2,1,0:T(8,128)} %get-tuple-element.65), channel_id=1, source_target_pairs={{0,8},{8,0},{16,24},{24,16},{1,9},{9,1},{17,25},{25,17},{2,10},{10... | collective-permute-start | bytes 528392 | tf_op jit(solution)/shard_map/ppermute | solution.py:413
  43.1 29.5 %copy-start.32 = (f32[60,8,128]{2,1,0:T(8,128)S(1)}, f32[60,8,128]{2,1,0:T(8,128)}, u32[]{:S(2)}) copy-start(f32[60,8,128]{2,1,0:T(8,128)} %get-tuple-element.116) | copy-start | bytes 737284
  43.1 9.5 %collective-permute-start.34 = (f32[60,8,128]{2,1,0:T(8,128)}, f32[60,8,128]{2,1,0:T(8,128)S(1)}, u32[]{:S(2)}, u32[]{:S(2)}) collective-permute-start(f32[60,8,128]{2,1,0:T(8,128)} %get-tuple-element.110), channel_id=1, source_target_pairs={{0,1},{1,0},{2,3},{3,2},{4,5},{5,4},{6,7},{7,6},{8,9},{9,8},{10,11... | collective-permute-start | bytes 737288 | tf_op jit(solution)/shard_map/ppermute | solution.py:406
  43.2 8.8 %collective-permute-start.1 = (f32[43,8,128]{2,1,0:T(8,128)S(1)}, f32[43,8,128]{2,1,0:T(8,128)S(1)}, u32[]{:S(2)}, u32[]{:S(2)}) collective-permute-start(f32[43,8,128]{2,1,0:T(8,128)S(1)} %copy-done.33), channel_id=1, source_target_pairs={{0,24},{8,16},{16,8},{24,0},{1,25},{9,17},{17,9},{25,1},{2,26},{10... | collective-permute-start | bytes 528392 | tf_op jit(solution)/shard_map/ppermute | solution.py:415
  45.1 27.9 %copy-start.12 = (f32[43,8,128]{2,1,0:T(8,128)}, f32[43,8,128]{2,1,0:T(8,128)S(1)}, u32[]{:S(2)}) copy-start(f32[43,8,128]{2,1,0:T(8,128)S(1)} %collective-permute-done.9.near_ref.near_sea_ref) | copy-start | bytes 528388
  45.1 23.4 %collective-permute-start.35 = (f32[60,8,128]{2,1,0:T(8,128)}, f32[60,8,128]{2,1,0:T(8,128)S(1)}, u32[]{:S(2)}, u32[]{:S(2)}) collective-permute-start(f32[60,8,128]{2,1,0:T(8,128)} %get-tuple-element.111), channel_id=1, source_target_pairs={{0,2},{1,3},{2,0},{3,1},{4,6},{5,7},{6,4},{7,5},{8,10},{9,11},{10,... | collective-permute-start | bytes 737288 | tf_op jit(solution)/shard_map/ppermute | solution.py:406
  46.6 22.2 %collective-permute-start.36 = (f32[60,8,128]{2,1,0:T(8,128)}, f32[60,8,128]{2,1,0:T(8,128)S(1)}, u32[]{:S(2)}, u32[]{:S(2)}) collective-permute-start(f32[60,8,128]{2,1,0:T(8,128)} %get-tuple-element.112), channel_id=1, source_target_pairs={{0,3},{1,2},{2,1},{3,0},{4,7},{5,6},{6,5},{7,4},{8,11},{9,10},{10,... | collective-permute-start | bytes 737288 | tf_op jit(solution)/shard_map/ppermute | solution.py:406
  46.6 23.1 %collective-permute-start.37 = (f32[60,8,128]{2,1,0:T(8,128)}, f32[60,8,128]{2,1,0:T(8,128)S(1)}, u32[]{:S(2)}, u32[]{:S(2)}) collective-permute-start(f32[60,8,128]{2,1,0:T(8,128)} %get-tuple-element.113), channel_id=1, source_target_pairs={{0,4},{1,5},{2,6},{3,7},{4,0},{5,1},{6,2},{7,3},{8,12},{9,13},{10,... | collective-permute-start | bytes 737288 | tf_op jit(solution)/shard_map/ppermute | solution.py:406
  51.9 18.9 %collective-permute-start.38 = (f32[60,8,128]{2,1,0:T(8,128)}, f32[60,8,128]{2,1,0:T(8,128)S(1)}, u32[]{:S(2)}, u32[]{:S(2)}) collective-permute-start(f32[60,8,128]{2,1,0:T(8,128)} %get-tuple-element.114), channel_id=1, source_target_pairs={{0,5},{1,4},{2,7},{3,6},{4,1},{5,0},{6,3},{7,2},{8,13},{9,12},{10,... | collective-permute-start | bytes 737288 | tf_op jit(solution)/shard_map/ppermute | solution.py:406
  52.6 19.9 %collective-permute-start.39 = (f32[60,8,128]{2,1,0:T(8,128)}, f32[60,8,128]{2,1,0:T(8,128)S(1)}, u32[]{:S(2)}, u32[]{:S(2)}) collective-permute-start(f32[60,8,128]{2,1,0:T(8,128)} %get-tuple-element.115), channel_id=1, source_target_pairs={{0,6},{1,7},{2,4},{3,5},{4,2},{5,3},{6,0},{7,1},{8,14},{9,15},{10,... | collective-permute-start | bytes 737288 | tf_op jit(solution)/shard_map/ppermute | solution.py:406
  68.5 24.6 %collective-permute-start.2 = (f32[42,16,128]{2,1,0:T(8,128)}, f32[42,16,128]{2,1,0:T(8,128)S(1)}, u32[]{:S(2)}, u32[]{:S(2)}) collective-permute-start(f32[42,16,128]{2,1,0:T(8,128)} %get-tuple-element.68), channel_id=1, source_target_pairs={{0,1},{1,0},{2,3},{3,2},{4,5},{5,4},{6,7},{7,6},{8,9},{9,8},{10,11... | collective-permute-start | bytes 1032200 | tf_op jit(solution)/shard_map/ppermute | solution.py:406
  69.2 25.6 %collective-permute-start.3 = (f32[42,16,128]{2,1,0:T(8,128)}, f32[42,16,128]{2,1,0:T(8,128)S(1)}, u32[]{:S(2)}, u32[]{:S(2)}) collective-permute-start(f32[42,16,128]{2,1,0:T(8,128)} %get-tuple-element.69), channel_id=1, source_target_pairs={{0,2},{1,3},{2,0},{3,1},{4,6},{5,7},{6,4},{7,5},{8,10},{9,11},{10,... | collective-permute-start | bytes 1032200 | tf_op jit(solution)/shard_map/ppermute | solution.py:406
  69.9 25.6 %collective-permute-start.4 = (f32[42,16,128]{2,1,0:T(8,128)}, f32[42,16,128]{2,1,0:T(8,128)S(1)}, u32[]{:S(2)}, u32[]{:S(2)}) collective-permute-start(f32[42,16,128]{2,1,0:T(8,128)} %get-tuple-element.70), channel_id=1, source_target_pairs={{0,3},{1,2},{2,1},{3,0},{4,7},{5,6},{6,5},{7,4},{8,11},{9,10},{10,... | collective-permute-start | bytes 1032200 | tf_op jit(solution)/shard_map/ppermute | solution.py:406
  70.9 25.5 %collective-permute-start.5 = (f32[42,16,128]{2,1,0:T(8,128)}, f32[42,16,128]{2,1,0:T(8,128)S(1)}, u32[]{:S(2)}, u32[]{:S(2)}) collective-permute-start(f32[42,16,128]{2,1,0:T(8,128)} %get-tuple-element.71), channel_id=1, source_target_pairs={{0,4},{1,5},{2,6},{3,7},{4,0},{5,1},{6,2},{7,3},{8,12},{9,13},{10,... | collective-permute-start | bytes 1032200 | tf_op jit(solution)/shard_map/ppermute | solution.py:406
  72.6 20.3 %collective-permute-start.40 = (f32[60,8,128]{2,1,0:T(8,128)S(1)}, f32[60,8,128]{2,1,0:T(8,128)S(1)}, u32[]{:S(2)}, u32[]{:S(2)}) collective-permute-start(f32[60,8,128]{2,1,0:T(8,128)S(1)} %copy-done.32), channel_id=1, source_target_pairs={{0,7},{1,6},{2,5},{3,4},{4,3},{5,2},{6,1},{7,0},{8,15},{9,14},{10,... | collective-permute-start | bytes 737288 | tf_op jit(solution)/shard_map/ppermute | solution.py:406
  92.9 24.7 %collective-permute-start.6 = (f32[42,16,128]{2,1,0:T(8,128)S(1)}, f32[42,16,128]{2,1,0:T(8,128)S(1)}, u32[]{:S(2)}, u32[]{:S(2)}) collective-permute-start(f32[42,16,128]{2,1,0:T(8,128)S(1)} %copy-done.31), channel_id=1, source_target_pairs={{0,5},{1,4},{2,7},{3,6},{4,1},{5,0},{6,3},{7,2},{8,13},{9,12},{10,... | collective-permute-start | bytes 1032200 | tf_op jit(solution)/shard_map/ppermute | solution.py:406
  93.2 64.8 %copy-start = (f32[42,16,128]{2,1,0:T(8,128)}, f32[42,16,128]{2,1,0:T(8,128)S(1)}, u32[]{:S(2)}) copy-start(f32[42,16,128]{2,1,0:T(8,128)S(1)} %collective-permute-done.2.rest_1_) | copy-start | bytes 1032196
  93.2 25.0 %collective-permute-start.7 = (f32[42,16,128]{2,1,0:T(8,128)}, f32[42,16,128]{2,1,0:T(8,128)S(1)}, u32[]{:S(2)}, u32[]{:S(2)}) collective-permute-start(f32[42,16,128]{2,1,0:T(8,128)} %get-tuple-element.73), channel_id=1, source_target_pairs={{0,6},{1,7},{2,4},{3,5},{4,2},{5,3},{6,0},{7,1},{8,14},{9,15},{10,... | collective-permute-start | bytes 1032200 | tf_op jit(solution)/shard_map/ppermute | solution.py:406
  94.8 63.2 %copy-start.1 = (f32[42,16,128]{2,1,0:T(8,128)}, f32[42,16,128]{2,1,0:T(8,128)S(1)}, u32[]{:S(2)}) copy-start(f32[42,16,128]{2,1,0:T(8,128)S(1)} %collective-permute-done.3.rest_2_) | copy-start | bytes 1032196
  94.8 23.6 %collective-permute-start.8 = (f32[42,16,128]{2,1,0:T(8,128)}, f32[42,16,128]{2,1,0:T(8,128)S(1)}, u32[]{:S(2)}, u32[]{:S(2)}) collective-permute-start(f32[42,16,128]{2,1,0:T(8,128)} %get-tuple-element.74), channel_id=1, source_target_pairs={{0,7},{1,6},{2,5},{3,4},{4,3},{5,2},{6,1},{7,0},{8,15},{9,14},{10,... | collective-permute-start | bytes 1032200 | tf_op jit(solution)/shard_map/ppermute | solution.py:406
  95.6 62.5 %copy-start.2 = (f32[42,16,128]{2,1,0:T(8,128)}, f32[42,16,128]{2,1,0:T(8,128)S(1)}, u32[]{:S(2)}) copy-start(f32[42,16,128]{2,1,0:T(8,128)S(1)} %collective-permute-done.4.rest_3_) | copy-start | bytes 1032196
  95.6 24.0 %collective-permute-start.11 = (f32[42,16,128]{2,1,0:T(8,128)}, f32[42,16,128]{2,1,0:T(8,128)S(1)}, u32[]{:S(2)}, u32[]{:S(2)}) collective-permute-start(f32[42,16,128]{2,1,0:T(8,128)} %get-tuple-element.78), channel_id=1, source_target_pairs={{0,1},{1,0},{2,3},{3,2},{4,5},{5,4},{6,7},{7,6},{8,9},{9,8},{10,11... | collective-permute-start | bytes 1032200 | tf_op jit(solution)/shard_map/ppermute | solution.py:406
  96.4 61.7 %copy-start.3 = (f32[42,16,128]{2,1,0:T(8,128)}, f32[42,16,128]{2,1,0:T(8,128)S(1)}, u32[]{:S(2)}) copy-start(f32[42,16,128]{2,1,0:T(8,128)S(1)} %collective-permute-done.5.rest_4_) | copy-start | bytes 1032196
  96.4 24.9 %collective-permute-start.12 = (f32[42,16,128]{2,1,0:T(8,128)}, f32[42,16,128]{2,1,0:T(8,128)S(1)}, u32[]{:S(2)}, u32[]{:S(2)}) collective-permute-start(f32[42,16,128]{2,1,0:T(8,128)} %get-tuple-element.79), channel_id=1, source_target_pairs={{0,2},{1,3},{2,0},{3,1},{4,6},{5,7},{6,4},{7,5},{8,10},{9,11},{10,... | collective-permute-start | bytes 1032200 | tf_op jit(solution)/shard_map/ppermute | solution.py:406
  117.6 40.5 %copy-start.4 = (f32[42,16,128]{2,1,0:T(8,128)}, f32[42,16,128]{2,1,0:T(8,128)S(1)}, u32[]{:S(2)}) copy-start(f32[42,16,128]{2,1,0:T(8,128)S(1)} %collective-permute-done.6.rest_5_) | copy-start | bytes 1032196
  117.6 9.8 %collective-permute-start.13 = (f32[42,16,128]{2,1,0:T(8,128)}, f32[42,16,128]{2,1,0:T(8,128)S(1)}, u32[]{:S(2)}, u32[]{:S(2)}) collective-permute-start(f32[42,16,128]{2,1,0:T(8,128)} %get-tuple-element.80), channel_id=1, source_target_pairs={{0,3},{1,2},{2,1},{3,0},{4,7},{5,6},{6,5},{7,4},{8,11},{9,10},{10,... | collective-permute-start | bytes 1032200 | tf_op jit(solution)/shard_map/ppermute | solution.py:406
  118.2 39.8 %copy-start.5 = (f32[42,16,128]{2,1,0:T(8,128)}, f32[42,16,128]{2,1,0:T(8,128)S(1)}, u32[]{:S(2)}) copy-start(f32[42,16,128]{2,1,0:T(8,128)S(1)} %collective-permute-done.7.rest_6_) | copy-start | bytes 1032196
  118.2 26.0 %collective-permute-start.14 = (f32[42,16,128]{2,1,0:T(8,128)}, f32[42,16,128]{2,1,0:T(8,128)}, u32[]{:S(2)}, u32[]{:S(2)}) collective-permute-start(f32[42,16,128]{2,1,0:T(8,128)} %get-tuple-element.81), channel_id=1, source_target_pairs={{0,4},{1,5},{2,6},{3,7},{4,0},{5,1},{6,2},{7,3},{8,12},{9,13},{10,... | collective-permute-start | bytes 1032200 | tf_op jit(solution)/shard_map/ppermute | solution.py:406
  118.4 39.7 %copy-start.6 = (f32[42,16,128]{2,1,0:T(8,128)}, f32[42,16,128]{2,1,0:T(8,128)S(1)}, u32[]{:S(2)}) copy-start(f32[42,16,128]{2,1,0:T(8,128)S(1)} %collective-permute-done.8.rest_7_) | copy-start | bytes 1032196
  118.4 31.2 %collective-permute-start.15 = (f32[42,16,128]{2,1,0:T(8,128)}, f32[42,16,128]{2,1,0:T(8,128)}, u32[]{:S(2)}, u32[]{:S(2)}) collective-permute-start(f32[42,16,128]{2,1,0:T(8,128)} %get-tuple-element.82), channel_id=1, source_target_pairs={{0,5},{1,4},{2,7},{3,6},{4,1},{5,0},{6,3},{7,2},{8,13},{9,12},{10,... | collective-permute-start | bytes 1032200 | tf_op jit(solution)/shard_map/ppermute | solution.py:406
  119.6 38.5 %copy-start.7 = (f32[42,16,128]{2,1,0:T(8,128)}, f32[42,16,128]{2,1,0:T(8,128)S(1)}, u32[]{:S(2)}) copy-start(f32[42,16,128]{2,1,0:T(8,128)S(1)} %collective-permute-done.11.rest_9_) | copy-start | bytes 1032196
  119.6 32.3 %collective-permute-start.16 = (f32[42,16,128]{2,1,0:T(8,128)}, f32[42,16,128]{2,1,0:T(8,128)}, u32[]{:S(2)}, u32[]{:S(2)}) collective-permute-start(f32[42,16,128]{2,1,0:T(8,128)} %get-tuple-element.83), channel_id=1, source_target_pairs={{0,6},{1,7},{2,4},{3,5},{4,2},{5,3},{6,0},{7,1},{8,14},{9,15},{10,... | collective-permute-start | bytes 1032200 | tf_op jit(solution)/shard_map/ppermute | solution.py:406
  121.3 36.8 %copy-start.8 = (f32[42,16,128]{2,1,0:T(8,128)}, f32[42,16,128]{2,1,0:T(8,128)S(1)}, u32[]{:S(2)}) copy-start(f32[42,16,128]{2,1,0:T(8,128)S(1)} %collective-permute-done.12.rest_10_) | copy-start | bytes 1032196
  121.3 30.8 %collective-permute-start.17 = (f32[42,16,128]{2,1,0:T(8,128)}, f32[42,16,128]{2,1,0:T(8,128)}, u32[]{:S(2)}, u32[]{:S(2)}) collective-permute-start(f32[42,16,128]{2,1,0:T(8,128)} %get-tuple-element.84), channel_id=1, source_target_pairs={{0,7},{1,6},{2,5},{3,4},{4,3},{5,2},{6,1},{7,0},{8,15},{9,14},{10,... | collective-permute-start | bytes 1032200 | tf_op jit(solution)/shard_map/ppermute | solution.py:406
  127.4 30.7 %copy-start.9 = (f32[42,16,128]{2,1,0:T(8,128)}, f32[42,16,128]{2,1,0:T(8,128)S(1)}, u32[]{:S(2)}) copy-start(f32[42,16,128]{2,1,0:T(8,128)S(1)} %collective-permute-done.13.rest_11_) | copy-start | bytes 1032196
  127.4 45.2 %collective-permute-start.20 = (f32[60,8,128]{2,1,0:T(8,128)}, f32[60,8,128]{2,1,0:T(8,128)}, u32[]{:S(2)}, u32[]{:S(2)}) collective-permute-start(f32[60,8,128]{2,1,0:T(8,128)} %get-tuple-element.88), channel_id=1, source_target_pairs={{0,1},{1,0},{2,3},{3,2},{4,5},{5,4},{6,7},{7,6},{8,9},{9,8},{10,11... | collective-permute-start | bytes 737288 | tf_op jit(solution)/shard_map/ppermute | solution.py:406
  144.2 29.5 %collective-permute-start.21 = (f32[60,8,128]{2,1,0:T(8,128)}, f32[60,8,128]{2,1,0:T(8,128)}, u32[]{:S(2)}, u32[]{:S(2)}) collective-permute-start(f32[60,8,128]{2,1,0:T(8,128)} %get-tuple-element.89), channel_id=1, source_target_pairs={{0,2},{1,3},{2,0},{3,1},{4,6},{5,7},{6,4},{7,5},{8,10},{9,11},{10,... | collective-permute-start | bytes 737288 | tf_op jit(solution)/shard_map/ppermute | solution.py:406
  149.6 24.9 %collective-permute-start.22 = (f32[60,8,128]{2,1,0:T(8,128)}, f32[60,8,128]{2,1,0:T(8,128)}, u32[]{:S(2)}, u32[]{:S(2)}) collective-permute-start(f32[60,8,128]{2,1,0:T(8,128)} %get-tuple-element.90), channel_id=1, source_target_pairs={{0,3},{1,2},{2,1},{3,0},{4,7},{5,6},{6,5},{7,4},{8,11},{9,10},{10,... | collective-permute-start | bytes 737288 | tf_op jit(solution)/shard_map/ppermute | solution.py:406
  151.8 24.3 %collective-permute-start.23 = (f32[60,8,128]{2,1,0:T(8,128)}, f32[60,8,128]{2,1,0:T(8,128)}, u32[]{:S(2)}, u32[]{:S(2)}) collective-permute-start(f32[60,8,128]{2,1,0:T(8,128)} %get-tuple-element.91), channel_id=1, source_target_pairs={{0,4},{1,5},{2,6},{3,7},{4,0},{5,1},{6,2},{7,3},{8,12},{9,13},{10,... | collective-permute-start | bytes 737288 | tf_op jit(solution)/shard_map/ppermute | solution.py:406
  152.1 24.7 %collective-permute-start.24 = (f32[60,8,128]{2,1,0:T(8,128)}, f32[60,8,128]{2,1,0:T(8,128)}, u32[]{:S(2)}, u32[]{:S(2)}) collective-permute-start(f32[60,8,128]{2,1,0:T(8,128)} %get-tuple-element.92), channel_id=1, source_target_pairs={{0,5},{1,4},{2,7},{3,6},{4,1},{5,0},{6,3},{7,2},{8,13},{9,12},{10,... | collective-permute-start | bytes 737288 | tf_op jit(solution)/shard_map/ppermute | solution.py:406
  172.6 71.5 %collective-permute-start.41 = (f32[144,8,128]{2,1,0:T(8,128)}, f32[144,8,128]{2,1,0:T(8,128)S(1)}, u32[]{:S(2)}, u32[]{:S(2)}) collective-permute-start(f32[144,8,128]{2,1,0:T(8,128)} %get-tuple-element.118), channel_id=1, source_target_pairs={{0,2},{1,3},{2,0},{3,1},{4,6},{5,7},{6,4},{7,5},{8,10},{9,11},{10,... | collective-permute-start | bytes 1769480 | tf_op jit(solution)/shard_map/ppermute | solution.py:406
  173.7 71.9 %collective-permute-start.42 = (f32[144,8,128]{2,1,0:T(8,128)}, f32[144,8,128]{2,1,0:T(8,128)S(1)}, u32[]{:S(2)}, u32[]{:S(2)}) collective-permute-start(f32[144,8,128]{2,1,0:T(8,128)} %get-tuple-element.119), channel_id=1, source_target_pairs={{0,4},{1,5},{2,6},{3,7},{4,0},{5,1},{6,2},{7,3},{8,12},{9,13},{10,... | collective-permute-start | bytes 1769480 | tf_op jit(solution)/shard_map/ppermute | solution.py:406
  174.5 71.5 %collective-permute-start.43 = (f32[144,8,128]{2,1,0:T(8,128)}, f32[144,8,128]{2,1,0:T(8,128)S(1)}, u32[]{:S(2)}, u32[]{:S(2)}) collective-permute-start(f32[144,8,128]{2,1,0:T(8,128)} %get-tuple-element.120), channel_id=1, source_target_pairs={{0,6},{1,7},{2,4},{3,5},{4,2},{5,3},{6,0},{7,1},{8,14},{9,15},{10,... | collective-permute-start | bytes 1769480 | tf_op jit(solution)/shard_map/ppermute | solution.py:406
  176.2 69.9 %collective-permute-start.44 = (f32[144,8,128]{2,1,0:T(8,128)}, f32[144,8,128]{2,1,0:T(8,128)S(1)}, u32[]{:S(2)}, u32[]{:S(2)}) collective-permute-start(f32[144,8,128]{2,1,0:T(8,128)} %get-tuple-element.121), channel_id=1, source_target_pairs={{0,3},{1,2},{2,1},{3,0},{4,7},{5,6},{6,5},{7,4},{8,11},{9,10},{10,... | collective-permute-start | bytes 1769480 | tf_op jit(solution)/shard_map/ppermute | solution.py:406
  176.9 43.0 %collective-permute-start.25 = (f32[60,8,128]{2,1,0:T(8,128)}, f32[60,8,128]{2,1,0:T(8,128)S(1)}, u32[]{:S(2)}, u32[]{:S(2)}) collective-permute-start(f32[60,8,128]{2,1,0:T(8,128)} %get-tuple-element.93), channel_id=1, source_target_pairs={{0,6},{1,7},{2,4},{3,5},{4,2},{5,3},{6,0},{7,1},{8,14},{9,15},{10,... | collective-permute-start | bytes 737288 | tf_op jit(solution)/shard_map/ppermute | solution.py:406
  219.8 9.1 %collective-permute-start.26 = (f32[60,8,128]{2,1,0:T(8,128)}, f32[60,8,128]{2,1,0:T(8,128)S(1)}, u32[]{:S(2)}, u32[]{:S(2)}) collective-permute-start(f32[60,8,128]{2,1,0:T(8,128)} %get-tuple-element.94), channel_id=1, source_target_pairs={{0,7},{1,6},{2,5},{3,4},{4,3},{5,2},{6,1},{7,0},{8,15},{9,14},{10,... | collective-permute-start | bytes 737288 | tf_op jit(solution)/shard_map/ppermute | solution.py:406
  228.9 18.3 %collective-permute-start.45 = (f32[144,8,128]{2,1,0:T(8,128)}, f32[144,8,128]{2,1,0:T(8,128)S(1)}, u32[]{:S(2)}, u32[]{:S(2)}) collective-permute-start(f32[144,8,128]{2,1,0:T(8,128)} %get-tuple-element.122), channel_id=1, source_target_pairs={{0,5},{1,4},{2,7},{3,6},{4,1},{5,0},{6,3},{7,2},{8,13},{9,12},{10,... | collective-permute-start | bytes 1769480 | tf_op jit(solution)/shard_map/ppermute | solution.py:406
  244.1 30.1 %copy-start.16 = (f32[144,8,128]{2,1,0:T(8,128)}, f32[144,8,128]{2,1,0:T(8,128)S(1)}, u32[]{:S(2)}) copy-start(f32[144,8,128]{2,1,0:T(8,128)S(1)} %collective-permute-done.41.rest_1_) | copy-start | bytes 1769476
  244.1 16.7 %collective-permute-start.46 = (f32[144,8,128]{2,1,0:T(8,128)}, f32[144,8,128]{2,1,0:T(8,128)}, u32[]{:S(2)}, u32[]{:S(2)}) collective-permute-start(f32[144,8,128]{2,1,0:T(8,128)} %get-tuple-element.123), channel_id=1, source_target_pairs={{0,7},{1,6},{2,5},{3,4},{4,3},{5,2},{6,1},{7,0},{8,15},{9,14},{10,... | collective-permute-start | bytes 1769480 | tf_op jit(solution)/shard_map/ppermute | solution.py:406
  245.6 28.5 %copy-start.17 = (f32[144,8,128]{2,1,0:T(8,128)}, f32[144,8,128]{2,1,0:T(8,128)S(1)}, u32[]{:S(2)}) copy-start(f32[144,8,128]{2,1,0:T(8,128)S(1)} %collective-permute-done.42.rest_2_) | copy-start | bytes 1769476
  245.6 15.4 %collective-permute-start.47 = (f32[144,8,128]{2,1,0:T(8,128)}, f32[144,8,128]{2,1,0:T(8,128)}, u32[]{:S(2)}, u32[]{:S(2)}) collective-permute-start(f32[144,8,128]{2,1,0:T(8,128)} %get-tuple-element.124), channel_id=1, source_target_pairs={{0,1},{1,0},{2,3},{3,2},{4,5},{5,4},{6,7},{7,6},{8,9},{9,8},{10,11... | collective-permute-start | bytes 1769480 | tf_op jit(solution)/shard_map/ppermute | solution.py:406
  246.0 28.1 %copy-start.18 = (f32[144,8,128]{2,1,0:T(8,128)}, f32[144,8,128]{2,1,0:T(8,128)S(1)}, u32[]{:S(2)}) copy-start(f32[144,8,128]{2,1,0:T(8,128)S(1)} %collective-permute-done.43.rest_3_) | copy-start | bytes 1769476
  246.0 17.3 %collective-permute-start.30 = (f32[144,8,128]{2,1,0:T(8,128)}, f32[144,8,128]{2,1,0:T(8,128)}, u32[]{:S(2)}, u32[]{:S(2)}) collective-permute-start(f32[144,8,128]{2,1,0:T(8,128)} %get-tuple-element.106), channel_id=1, source_target_pairs={{0,1},{1,0},{2,3},{3,2},{4,5},{5,4},{6,7},{7,6},{8,9},{9,8},{10,11... | collective-permute-start | bytes 1769480 | tf_op jit(solution)/shard_map/ppermute | solution.py:406
  246.1 28.0 %copy-start.19 = (f32[144,8,128]{2,1,0:T(8,128)}, f32[144,8,128]{2,1,0:T(8,128)S(1)}, u32[]{:S(2)}) copy-start(f32[144,8,128]{2,1,0:T(8,128)S(1)} %collective-permute-done.44.rest_4_) | copy-start | bytes 1769476
  246.1 27.7 %collective-permute-start.31 = (f32[144,8,128]{2,1,0:T(8,128)}, f32[144,8,128]{2,1,0:T(8,128)}, u32[]{:S(2)}, u32[]{:S(2)}) collective-permute-start(f32[144,8,128]{2,1,0:T(8,128)} %get-tuple-element.107), channel_id=1, source_target_pairs={{0,2},{1,3},{2,0},{3,1},{4,6},{5,7},{6,4},{7,5},{8,10},{9,11},{10,... | collective-permute-start | bytes 1769480 | tf_op jit(solution)/shard_map/ppermute | solution.py:406
  247.2 56.6 %collective-permute-start.27 = (f32[144,8,128]{2,1,0:T(8,128)}, f32[144,8,128]{2,1,0:T(8,128)S(1)}, u32[]{:S(2)}, u32[]{:S(2)}) collective-permute-start(f32[144,8,128]{2,1,0:T(8,128)} %get-tuple-element.102), channel_id=1, source_target_pairs={{0,5},{1,4},{2,7},{3,6},{4,1},{5,0},{6,3},{7,2},{8,13},{9,12},{10,... | collective-permute-start | bytes 1769480 | tf_op jit(solution)/shard_map/ppermute | solution.py:406
  260.8 38.4 %collective-permute-start.32 = (f32[144,8,128]{2,1,0:T(8,128)}, f32[144,8,128]{2,1,0:T(8,128)}, u32[]{:S(2)}, u32[]{:S(2)}) collective-permute-start(f32[144,8,128]{2,1,0:T(8,128)} %get-tuple-element.108), channel_id=1, source_target_pairs={{0,4},{1,5},{2,6},{3,7},{4,0},{5,1},{6,2},{7,3},{8,12},{9,13},{10,... | collective-permute-start | bytes 1769480 | tf_op jit(solution)/shard_map/ppermute | solution.py:406
  261.0 38.1 %collective-permute-start.33 = (f32[144,8,128]{2,1,0:T(8,128)}, f32[144,8,128]{2,1,0:T(8,128)}, u32[]{:S(2)}, u32[]{:S(2)}) collective-permute-start(f32[144,8,128]{2,1,0:T(8,128)} %get-tuple-element.109), channel_id=1, source_target_pairs={{0,6},{1,7},{2,4},{3,5},{4,2},{5,3},{6,0},{7,1},{8,14},{9,15},{10,... | collective-permute-start | bytes 1769480 | tf_op jit(solution)/shard_map/ppermute | solution.py:406
  263.3 38.6 %collective-permute-start.29 = (f32[144,8,128]{2,1,0:T(8,128)}, f32[144,8,128]{2,1,0:T(8,128)}, u32[]{:S(2)}, u32[]{:S(2)}) collective-permute-start(f32[144,8,128]{2,1,0:T(8,128)} %get-tuple-element.104), channel_id=1, source_target_pairs={{0,3},{1,2},{2,1},{3,0},{4,7},{5,6},{6,5},{7,4},{8,11},{9,10},{10,... | collective-permute-start | bytes 1769480 | tf_op jit(solution)/shard_map/ppermute | solution.py:406
  273.8 37.5 %collective-permute-start.28 = (f32[144,8,128]{2,1,0:T(8,128)}, f32[144,8,128]{2,1,0:T(8,128)}, u32[]{:S(2)}, u32[]{:S(2)}) collective-permute-start(f32[144,8,128]{2,1,0:T(8,128)} %get-tuple-element.103), channel_id=1, source_target_pairs={{0,7},{1,6},{2,5},{3,4},{4,3},{5,2},{6,1},{7,0},{8,15},{9,14},{10,... | collective-permute-start | bytes 1769480 | tf_op jit(solution)/shard_map/ppermute | solution.py:406
  (18 other events, 196.3 us)

commit v4 on v3

--- a/solution.py
+++ b/solution.py
@@ -15,11 +15,11 @@
 ROWS = 8
 UNITS = 24
 CHUNKS = (7, 7, 10)
-STRIP_BLOCKS = 10
-STREAMS = 3
+STRIP_BLOCKS = 4
+STREAMS = 5
 BAND = 4
 PAD = 8
-LANES = 3
+LANES = 6
 
 
 def strip_blocks(base, made, most):
@@ -39,21 +39,22 @@
         waves, (land_ref, near_ref, far_ref, turned) = rest[:copies], rest[copies:]
         step = pl.program_id(0)
         even = lax.rem(lax.axis_index("sector"), 2) == 0
-        near = pl.multiple_of(jnp.where(even, lon - EDGE, 0), EDGE)
-        far = pl.multiple_of(jnp.where(even, 0, lon - EDGE), EDGE)
+        near = jnp.where(even, lon - SUBSTEPS, 0)
+        far = jnp.where(even, 0, lon - SUBSTEPS)
         for b in range(block):
             turned[b] = waves[b // part][b % part].T
-            near_ref[step * block + b] = turned[b, pl.ds(near, EDGE)]
-            far_ref[step * block + b] = turned[b, pl.ds(far, EDGE)]
+            spot = pl.ds((step * block + b) * SUBSTEPS, SUBSTEPS)
+            near_ref[spot] = turned[b, pl.ds(near, SUBSTEPS)]
+            far_ref[spot] = turned[b, pl.ds(far, SUBSTEPS)]
 
         @pl.when(step == 0)
         def _():
             turned[0] = land_ref[...].astype(jnp.float32).T
-            near_ref[made] = turned[0, pl.ds(near, EDGE)]
-            far_ref[made] = turned[0, pl.ds(far, EDGE)]
-
-    strip = pl.BlockSpec((made + 1, EDGE, lat), lambda i, *_: (0, 0, 0))
-    shape = jax.ShapeDtypeStruct((made + 1, EDGE, lat), jnp.float32)
+            near_ref[made * SUBSTEPS :] = turned[0, pl.ds(near, SUBSTEPS)]
+            far_ref[made * SUBSTEPS :] = turned[0, pl.ds(far, SUBSTEPS)]
+
+    strip = pl.BlockSpec(((made + 1) * SUBSTEPS, lat), lambda i, *_: (0, 0))
+    shape = jax.ShapeDtypeStruct(((made + 1) * SUBSTEPS, lat), jnp.float32)
     first = base // part
     streams = [
         pl.BlockSpec((part, lat, lon), lambda i, *_, n=n: (first + i * copies + n, 0, 0))
@@ -81,7 +82,7 @@
 
     def kernel(
         kinds_ref, courant_ref, cos_ref, sin_ref,
-        wave_ref, near_ref, far_ref, near_sea_ref, far_sea_ref, land_ref, inverse_ref,
+        wave_ref, near_ref, far_ref, land_ref, inverse_ref,
         *rest,
     ):
         outs, rest = rest[: len(pieces) * count], rest[len(pieces) * count :]
@@ -99,8 +100,11 @@
             own = land_ref[...].astype(jnp.float32).T
             sea[0, EDGE:] = own
             sea[1, :lon] = own
-            sea[0, :EDGE] = jnp.where(even, far_sea_ref[0], near_sea_ref[0])
-            sea[1, lon:] = jnp.where(even, near_sea_ref[0], far_sea_ref[0])
+            sea[0, :EDGE] = jnp.zeros((EDGE, lat), jnp.float32)
+            sea[1, lon:] = jnp.zeros((EDGE, lat), jnp.float32)
+            near_sea, far_sea = near_ref[made * SUBSTEPS :], far_ref[made * SUBSTEPS :]
+            sea[0, EDGE - SUBSTEPS : EDGE] = jnp.where(even, far_sea, near_sea)
+            sea[1, lon : lon + SUBSTEPS] = jnp.where(even, near_sea, far_sea)
             lane = lax.broadcasted_iota(jnp.int32, (span, lat), 1)
             for way in range(2):
                 slope[way] = sea[way] * inverse_ref[...]
@@ -126,9 +130,12 @@
                 along[...] = rate_y * side[jnp.where(northward, way, 2 + way)]
                 keep[...] = (1.0 - rate_y) * sea[way] - ratio
                 own = pl.multiple_of(jnp.where(eastward, 2 * EDGE, EDGE), EDGE)
-                upwind = pl.multiple_of(jnp.where(eastward, EDGE, EDGE + lon), EDGE)
+                upwind = jnp.where(eastward, 2 * EDGE - SUBSTEPS, EDGE + lon)
                 ping[pl.ds(own, lon)] = wave_ref[b].T
-                ping[pl.ds(upwind, EDGE)] = jnp.where(eastward == even, far_ref[b], near_ref[b])
+                spot = pl.ds((step * block + b) * SUBSTEPS, SUBSTEPS)
+                ping[pl.ds(upwind, SUBSTEPS)] = jnp.where(
+                    eastward == even, far_ref[spot], near_ref[spot]
+                )
             for substep in range(SUBSTEPS):
                 for row in range(0, span, EDGE):
                     for q, (ping, pong, keep, cross, along, result) in enumerate(sets):
@@ -162,8 +169,6 @@
 
         lax.fori_loop(0, block // lanes, some, 0)
 
-    strip = pl.BlockSpec((block, EDGE, lat), lambda i, *_: (i, 0, 0))
-    strip_of_sea = pl.BlockSpec((1, EDGE, lat), lambda i, *_: (made, 0, 0))
     fixed = lambda shape: pl.BlockSpec(shape, lambda i, *_: (0,) * len(shape))
     first_block = base // block
     f32 = lambda *shape: pltpu.VMEM(shape, jnp.float32)
@@ -174,10 +179,8 @@
             grid=(made // block,),
             in_specs=[
                 pl.BlockSpec((block, lat, lon), lambda i, *_: (first_block + i, 0, 0)),
-                strip,
-                strip,
-                strip_of_sea,
-                strip_of_sea,
+                fixed(((made + 1) * SUBSTEPS, lat)),
+                fixed(((made + 1) * SUBSTEPS, lat)),
                 fixed((lat, lon)),
                 fixed((1, lat)),
             ],
@@ -202,7 +205,7 @@
             flops=0, bytes_accessed=12 * made * lat * lon * 4, transcendentals=0
         ),
         name="advance",
-    )(*tables, spectrum, *strips, *strips, land_mask, inverse)
+    )(*tables, spectrum, *strips, land_mask, inverse)
 
 
 def coupling_tables(growth, whitecap, weights, spread, cosine, sine, after, lon):

time: 314 us -> 314 us (level)
  Pallas kernels: 103 us -> 92.4 us
  waiting for transfers between devices: 157 us -> 163 us
    pallas_call x3, Pallas kernels: 47.2 us -> 39.5 us  [advance(): pl.pallas_call(kernel, grid_spec=pltpu.PrefetchScalarGridSpec(num_scalar_...]
    ppermute x3, waiting for transfers between devices: 0.01 us -> 5.6 us  [exchange(): near = lax.ppermute(near, 'sector', pairs)]
    unnamed x69 -> x71, local copies, waits for them, and re-layouts: 3.78 us -> 6.53 us
  transfers between devices with their start and end apart: 48 -> 48, of which waited for: 13 -> 16; matrix products, arithmetic and copies ran while one was open for 1% -> 1% of each run, Pallas kernels for 31% -> 23%
where the time goes in v4:
time: 314 us
  waiting for transfers between devices  163 us (52%)
  Pallas kernels  92.4 us (29%)
  starting transfers between devices  51.9 us (17%)
  local copies, waits for them, and re-layouts  6.53 us (2%)
    ppermute x42, waiting for transfers between devices, swap(): lax.ppermute(pieces[k], 'group', [(i, i ^ k) for i in range(count)])  149 us
    ppermute x42, starting transfers between devices, swap(): lax.ppermute(pieces[k], 'group', [(i, i ^ k) for i in range(count)])  41.4 us
    pallas_call x3, Pallas kernels, advance(): pl.pallas_call(kernel, grid_spec=pltpu.PrefetchScalarGridSpec(num_scalar_...  39.5 us
    pallas_call x2, Pallas kernels, couple(): pl.pallas_call(kernel, grid_spec=pltpu.PrefetchScalarGridSpec(num_scalar_...  29 us
    pallas_call x4, Pallas kernels, settle(): pl.pallas_call(kernel, in_specs=[anywhere] * (len(ks) + len(extra)), out_...  11.1 us
    pallas_call x3, Pallas kernels, edge_strips(): pl.pallas_call(kernel, grid=(made // block,), in_specs=streams + [pl.Bloc...  9.6 us
    ppermute x3, waiting for transfers between devices, exchange(): far = lax.ppermute(far, 'sector', pairs)  8.08 us
    ppermute x3, starting transfers between devices, exchange(): far = lax.ppermute(far, 'sector', pairs)  6.8 us
  transfers between devices with their start and end apart: 48, of which 16 were waited for; matrix products, arithmetic and copies ran while one was open for 1% of the time, Pallas kernels for 23%

profile of v4, /device:TPU:0, one launch (start us, length us, event | category | flops | bytes accessed | tf_op | source)
XLA Modules:
  0.0 313.7 jit_solution(14239020241412704450)
XLA Ops:
  0.0 3.7 %edge_strips.5 = (f32[366,128]{1,0:T(8,128)}, f32[366,128]{1,0:T(8,128)}) custom-call(f32[144,128,128]{2,1,0:T(8,128)} %wave_ref.5, f32[144,128,128]{2,1,0:T(8,128)} %wave_ref.5, f32[144,128,128]{2,1,0:T(8,128)} %wave_ref.5, f32[144,128,128]{2,1,0:T(8,128)} %wave_ref.5, f32[144,128,128]{2,1,0:T(8,128)} %wave_ref.5, s32[128,128]{1,0:T(8,128)} %rest_24_.3), custom_call_target="tpu_custom_call" | custom-call | bytes 7864320 | tf_op jit(solution)/shard_map/edge_strips/pallas_call | solution.py:63
  3.7 3.1 collective-permute-start.18
  6.7 2.5 collective-permute-start.19
  9.2 3.0 collective-permute-done.18.near_ref
  12.1 5.8 %collective-permute-done.19.far_ref = f32[366,128]{1,0:T(8,128)S(1)} collective-permute-done((f32[366,128]{1,0:T(8,128)}, f32[366,128]{1,0:T(8,128)S(1)}, u32[]{:S(2)}, u32[]{:S(2)}) %collective-permute-start.19) | collective-permute-done | bytes 187424 | tf_op jit(solution)/shard_map/ppermute | solution.py:418
  18.7 15.9 %advance.5 = (f32[60,8,128]{2,1,0:T(8,128)}, f32[60,8,128]{2,1,0:T(8,128)}, f32[60,8,128]{2,1,0:T(8,128)}, f32[60,8,128]{2,1,0:T(8,128)}, f32[60,8,128]{2,1,0:T(...) custom-call(s32[1152]{0:T(1024)} %kinds_ref.9, ...), custom_call_target="tpu_custom_call" | custom-call | bytes 47185920 | tf_op jit(solution)/shard_map/advance/pallas_call | solution.py:175
  34.7 3.0 edge_strips.4
  38.3 2.6 collective-permute-start.10
  40.9 3.0 edge_strips.3
  43.9 1.7 collective-permute-start.1
  45.6 1.6 collective-permute-start.35
  47.2 1.3 collective-permute-done.10.far_ref
  48.7 2.6 collective-permute-done.near_ref
  51.3 1.5 collective-permute-start.37
  52.9 1.0 collective-permute-done.1.far_ref
  54.5 1.9 collective-permute-start.39
  56.4 11.7 %advance.3 = (f32[42,16,128]{2,1,0:T(8,128)}, f32[42,16,128]{2,1,0:T(8,128)}, f32[42,16,128]{2,1,0:T(8,128)}, f32[42,16,128]{2,1,0:T(8,128)}, f32[42,16,128]{2,1...) custom-call(s32[1152]{0:T(1024)} %kinds_ref.9, f32[32]{0:T(128)} %courant_ref.5, ...), custom_call_target="tpu_custom_call" | custom-call | bytes 33030144 | tf_op jit(solution)/shard_map/advance/pallas_call | solution.py:175
  71.1 1.1 collective-permute-start.4
  72.2 0.7 copy-done.20
  72.9 1.3 collective-permute-start.5
  74.8 11.8 %advance.4 = (f32[42,16,128]{2,1,0:T(8,128)}, f32[42,16,128]{2,1,0:T(8,128)}, f32[42,16,128]{2,1,0:T(8,128)}, f32[42,16,128]{2,1,0:T(8,128)}, f32[42,16,128]{2,1...) custom-call(s32[1152]{0:T(1024)} %kinds_ref.9, f32[32]{0:T(128)} %courant_ref.5, ...), custom_call_target="tpu_custom_call" | custom-call | bytes 33030144 | tf_op jit(solution)/shard_map/advance/pallas_call | solution.py:175
  86.7 6.1 %collective-permute-done.40.rest_23_ = f32[60,8,128]{2,1,0:T(8,128)S(1)} collective-permute-done((f32[60,8,128]{2,1,0:T(8,128)S(1)}, f32[60,8,128]{2,1,0:T(8,128)S(1)}, u32[]{:S(2)}, u32[]{:S(2)}) %collective-permute-start.40) | collective-permute-done | bytes 245792 | tf_op jit(solution)/shard_map/ppermute | solution.py:409
  92.7 0.7 copy-done.22
  93.4 1.1 collective-permute-start.6
  94.5 1.3 collective-permute-start.7
  95.8 0.8 collective-permute-start.8
  96.7 0.9 collective-permute-start.11
  98.1 19.5 %collective-permute-done.6.rest_5_ = f32[42,16,128]{2,1,0:T(8,128)S(1)} collective-permute-done((f32[42,16,128]{2,1,0:T(8,128)S(1)}, f32[42,16,128]{2,1,0:T(8,128)S(1)}, u32[]{:S(2)}, u32[]{:S(2)}) %collective-permute-start.6) | collective-permute-done | bytes 344096 | tf_op jit(solution)/shard_map/ppermute | solution.py:409
  117.6 1.2 collective-permute-start.13
  118.8 0.9 collective-permute-start.14
  120.1 1.7 collective-permute-start.16
  121.9 1.3 collective-permute-start.17
  123.2 4.4 %collective-permute-done.13.rest_11_ = f32[42,16,128]{2,1,0:T(8,128)S(1)} collective-permute-done((f32[42,16,128]{2,1,0:T(8,128)}, f32[42,16,128]{2,1,0:T(8,128)S(1)}, u32[]{:S(2)}, u32[]{:S(2)}) %collective-permute-start.13) | collective-permute-done | bytes 344096 | tf_op jit(solution)/shard_map/ppermute | solution.py:409
  127.6 2.1 collective-permute-start.20
  129.6 15.2 %collective-permute-done.14.rest_12_ = f32[42,16,128]{2,1,0:T(8,128)} collective-permute-done((f32[42,16,128]{2,1,0:T(8,128)}, f32[42,16,128]{2,1,0:T(8,128)}, u32[]{:S(2)}, u32[]{:S(2)}) %collective-permute-start.14) | collective-permute-done | bytes 344096 | tf_op jit(solution)/shard_map/ppermute | solution.py:409
  144.8 1.5 collective-permute-start.21
  146.3 3.8 %collective-permute-done.15.rest_13_ = f32[42,16,128]{2,1,0:T(8,128)} collective-permute-done((f32[42,16,128]{2,1,0:T(8,128)}, f32[42,16,128]{2,1,0:T(8,128)}, u32[]{:S(2)}, u32[]{:S(2)}) %collective-permute-start.15) | collective-permute-done | bytes 344096 | tf_op jit(solution)/shard_map/ppermute | solution.py:409
  150.1 1.7 collective-permute-start.22
  151.9 1.0 collective-permute-start.23
  152.9 2.2 copy.18.spread_ref
  155.1 3.2 %coupling_tables.1 = (f32[1152,128]{1,0:T(8,128)}, f32[1152,128]{1,0:T(8,128)}, f32[1152,128]{1,0:T(8,128)}, f32[1152,128]{1,0:T(8,128)}, bf16[8,144,144]{2,1,0:T(8,128)(2,1)}, /*index=5*/bf16[8,144,144]{2,1,0:T(8,128)(2,1)}) custom-call(f32[32]{0:T(128)} %growth_ref.1, f32[32]{0:T(128)} %decay_ref.1, f32[32]{0:T(128)} %weight_ref.1, ...), custom_call_target="tpu_custom_call" | custom-call | bytes 2949120 | tf_op jit(solution)/shard_map/coupling_tables/pallas_call | solution.py:239
  158.4 14.6 %couple.3 = (f32[144,8,128]{2,1,0:T(8,128)}, f32[144,8,128]{2,1,0:T(8,128)}, f32[144,8,128]{2,1,0:T(8,128)}, f32[144,8,128]{2,1,0:T(8,128)}, f32[144,8,128]{2,1,...) custom-call(s32[1152]{0:T(1024)} %kinds_ref.9, ...), custom_call_target="tpu_custom_call" | custom-call | bytes 37748736 | tf_op jit(solution)/shard_map/couple/pallas_call | solution.py:335
  172.9 1.0 collective-permute-start.41
  173.9 1.2 collective-permute-start.42
  175.1 1.4 collective-permute-start.43
  176.5 0.9 collective-permute-start.44
  177.4 1.4 collective-permute-start.25
  178.9 41.4 %collective-permute-done.25.rest_22_ = f32[60,8,128]{2,1,0:T(8,128)S(1)} collective-permute-done((f32[60,8,128]{2,1,0:T(8,128)}, f32[60,8,128]{2,1,0:T(8,128)S(1)}, u32[]{:S(2)}, u32[]{:S(2)}) %collective-permute-start.25) | collective-permute-done | bytes 245792 | tf_op jit(solution)/shard_map/ppermute | solution.py:409
  220.3 0.9 collective-permute-start.26
  221.2 8.1 %collective-permute-done.26.rest_23_ = f32[60,8,128]{2,1,0:T(8,128)S(1)} collective-permute-done((f32[60,8,128]{2,1,0:T(8,128)}, f32[60,8,128]{2,1,0:T(8,128)S(1)}, u32[]{:S(2)}, u32[]{:S(2)}) %collective-permute-start.26) | collective-permute-done | bytes 245792 | tf_op jit(solution)/shard_map/ppermute | solution.py:409
  229.4 0.8 collective-permute-start.45
  230.1 14.4 %couple.2 = (f32[144,8,128]{2,1,0:T(8,128)}, f32[144,8,128]{2,1,0:T(8,128)}, f32[144,8,128]{2,1,0:T(8,128)}, f32[144,8,128]{2,1,0:T(8,128)}, f32[144,8,128]{2,1,...) custom-call(s32[1152]{0:T(1024)} %kinds_ref.9, ...), custom_call_target="tpu_custom_call" | custom-call | bytes 37748736 | tf_op jit(solution)/shard_map/couple/pallas_call | solution.py:335
  244.6 1.7 collective-permute-start.46
  246.8 0.8 collective-permute-start.31
  248.1 12.9 %collective-permute-done.46.rest_6_ = f32[144,8,128]{2,1,0:T(8,128)} collective-permute-done((f32[144,8,128]{2,1,0:T(8,128)}, f32[144,8,128]{2,1,0:T(8,128)}, u32[]{:S(2)}, u32[]{:S(2)}) %collective-permute-start.46) | collective-permute-done | bytes 589856 | tf_op jit(solution)/shard_map/ppermute | solution.py:409
  261.0 1.0 collective-permute-start.32
  262.0 1.9 collective-permute-start.33
  264.5 9.8 %collective-permute-done.31.rest_2_ = f32[144,8,128]{2,1,0:T(8,128)} collective-permute-done((f32[144,8,128]{2,1,0:T(8,128)}, f32[144,8,128]{2,1,0:T(8,128)}, u32[]{:S(2)}, u32[]{:S(2)}) %collective-permute-start.31) | collective-permute-done | bytes 589856 | tf_op jit(solution)/shard_map/ppermute | solution.py:409
  274.8 4.4 %settle.4.rest_5_ = f32[144,128,128]{2,1,0:T(8,128)} custom-call(f32[144,8,128]{2,1,0:T(8,128)} %get-tuple-element.117.rest_0_, f32[144,8,128]{2,1,0:T(8,128)} %copy-done.10, f32[144,8,128]{2,1,0:T(8,128)} %copy-done.11, f32[144,8,128]{2,1,0:T(8,128)} %copy-done.12, f32[144,8,128]{2,1,0:T(8,128)} %copy-done.13, f32[144,8,128]{2,1,0:T(8,128)} %copy-done.14, ...), custom_call_target="tpu_custom_call" | custom-call | bytes 9437184 | tf_op jit(solution)/shard_map/settle/pallas_call | solution.py:379
  279.2 20.7 %collective-permute-done.32.rest_3_ = f32[144,8,128]{2,1,0:T(8,128)} collective-permute-done((f32[144,8,128]{2,1,0:T(8,128)}, f32[144,8,128]{2,1,0:T(8,128)}, u32[]{:S(2)}, u32[]{:S(2)}) %collective-permute-start.32) | collective-permute-done | bytes 589856 | tf_op jit(solution)/shard_map/ppermute | solution.py:409
  299.9 2.7 settle.5.rest_1_
  302.6 1.9 settle.6.rest_2_
  304.5 7.0 %collective-permute-done.28.rest_1_ = f32[144,8,128]{2,1,0:T(8,128)} collective-permute-done((f32[144,8,128]{2,1,0:T(8,128)}, f32[144,8,128]{2,1,0:T(8,128)}, u32[]{:S(2)}, u32[]{:S(2)}) %collective-permute-start.28) | collective-permute-done | bytes 589856 | tf_op jit(solution)/shard_map/ppermute | solution.py:409
  311.6 2.1 settle.7
  (116 shorter events, 8.9 us)
Async XLA Ops:
  3.7 8.5 %collective-permute-start.18 = (f32[366,128]{1,0:T(8,128)}, f32[366,128]{1,0:T(8,128)S(1)}, u32[]{:S(2)}, u32[]{:S(2)}) collective-permute-start(f32[366,128]{1,0:T(8,128)} %get-tuple-element.85), channel_id=1, source_target_pairs={{0,8},{8,0},{16,24},{24,16},{1,9},{9,1},{17,25},{25,17},{2,10},{10... | collective-permute-start | bytes 562184 | tf_op jit(solution)/shard_map/ppermute | solution.py:416
  6.7 11.3 %collective-permute-start.19 = (f32[366,128]{1,0:T(8,128)}, f32[366,128]{1,0:T(8,128)S(1)}, u32[]{:S(2)}, u32[]{:S(2)}) collective-permute-start(f32[366,128]{1,0:T(8,128)} %get-tuple-element.86), channel_id=1, source_target_pairs={{0,24},{8,16},{16,8},{24,0},{1,25},{9,17},{17,9},{25,1},{2,26},{10... | collective-permute-start | bytes 562184 | tf_op jit(solution)/shard_map/ppermute | solution.py:418
  34.6 19.9 %collective-permute-start.34 = (f32[60,8,128]{2,1,0:T(8,128)}, f32[60,8,128]{2,1,0:T(8,128)S(1)}, u32[]{:S(2)}, u32[]{:S(2)}) collective-permute-start(f32[60,8,128]{2,1,0:T(8,128)} %get-tuple-element.110), channel_id=1, source_target_pairs={{0,1},{1,0},{2,3},{3,2},{4,5},{5,4},{6,7},{7,6},{8,9},{9,8},{10,11... | collective-permute-start | bytes 737288 | tf_op jit(solution)/shard_map/ppermute | solution.py:409
  37.7 7.9 %collective-permute-start.9 = (f32[258,128]{1,0:T(8,128)}, f32[258,128]{1,0:T(8,128)S(1)}, u32[]{:S(2)}, u32[]{:S(2)}) collective-permute-start(f32[258,128]{1,0:T(8,128)} %get-tuple-element.75), channel_id=1, source_target_pairs={{0,8},{8,0},{16,24},{24,16},{1,9},{9,1},{17,25},{25,17},{2,10},{10... | collective-permute-start | bytes 396296 | tf_op jit(solution)/shard_map/ppermute | solution.py:416
  38.3 10.2 %collective-permute-start.10 = (f32[258,128]{1,0:T(8,128)}, f32[258,128]{1,0:T(8,128)S(1)}, u32[]{:S(2)}, u32[]{:S(2)}) collective-permute-start(f32[258,128]{1,0:T(8,128)} %get-tuple-element.76), channel_id=1, source_target_pairs={{0,24},{8,16},{16,8},{24,0},{1,25},{9,17},{17,9},{25,1},{2,26},{10... | collective-permute-start | bytes 396296 | tf_op jit(solution)/shard_map/ppermute | solution.py:418
  43.9 30.4 %copy-start.32 = (f32[60,8,128]{2,1,0:T(8,128)S(1)}, f32[60,8,128]{2,1,0:T(8,128)}, u32[]{:S(2)}) copy-start(f32[60,8,128]{2,1,0:T(8,128)} %get-tuple-element.116) | copy-start | bytes 737284
  43.9 7.5 %collective-permute-start = (f32[258,128]{1,0:T(8,128)}, f32[258,128]{1,0:T(8,128)S(1)}, u32[]{:S(2)}, u32[]{:S(2)}) collective-permute-start(f32[258,128]{1,0:T(8,128)} %get-tuple-element.65), channel_id=1, source_target_pairs={{0,8},{8,0},{16,24},{24,16},{1,9},{9,1},{17,25},{25,17},{2,10},{10... | collective-permute-start | bytes 396296 | tf_op jit(solution)/shard_map/ppermute | solution.py:416
  43.9 9.9 %collective-permute-start.1 = (f32[258,128]{1,0:T(8,128)}, f32[258,128]{1,0:T(8,128)S(1)}, u32[]{:S(2)}, u32[]{:S(2)}) collective-permute-start(f32[258,128]{1,0:T(8,128)} %get-tuple-element.66), channel_id=1, source_target_pairs={{0,24},{8,16},{16,8},{24,0},{1,25},{9,17},{17,9},{25,1},{2,26},{10... | collective-permute-start | bytes 396296 | tf_op jit(solution)/shard_map/ppermute | solution.py:418
  45.6 29.2 %copy-start.27 = (f32[258,128]{1,0:T(8,128)}, f32[258,128]{1,0:T(8,128)S(1)}, u32[]{:S(2)}) copy-start(f32[258,128]{1,0:T(8,128)S(1)} %collective-permute-done.9.near_ref) | copy-start | bytes 396292
  45.6 22.6 %collective-permute-start.35 = (f32[60,8,128]{2,1,0:T(8,128)}, f32[60,8,128]{2,1,0:T(8,128)S(1)}, u32[]{:S(2)}, u32[]{:S(2)}) collective-permute-start(f32[60,8,128]{2,1,0:T(8,128)} %get-tuple-element.111), channel_id=1, source_target_pairs={{0,2},{1,3},{2,0},{3,1},{4,6},{5,7},{6,4},{7,5},{8,10},{9,11},{10,... | collective-permute-start | bytes 737288 | tf_op jit(solution)/shard_map/ppermute | solution.py:409
  48.4 20.8 %collective-permute-start.36 = (f32[60,8,128]{2,1,0:T(8,128)}, f32[60,8,128]{2,1,0:T(8,128)S(1)}, u32[]{:S(2)}, u32[]{:S(2)}) collective-permute-start(f32[60,8,128]{2,1,0:T(8,128)} %get-tuple-element.112), channel_id=1, source_target_pairs={{0,3},{1,2},{2,1},{3,0},{4,7},{5,6},{6,5},{7,4},{8,11},{9,10},{10,... | collective-permute-start | bytes 737288 | tf_op jit(solution)/shard_map/ppermute | solution.py:409
  51.3 19.1 %collective-permute-start.37 = (f32[60,8,128]{2,1,0:T(8,128)}, f32[60,8,128]{2,1,0:T(8,128)S(1)}, u32[]{:S(2)}, u32[]{:S(2)}) collective-permute-start(f32[60,8,128]{2,1,0:T(8,128)} %get-tuple-element.113), channel_id=1, source_target_pairs={{0,4},{1,5},{2,6},{3,7},{4,0},{5,1},{6,2},{7,3},{8,12},{9,13},{10,... | collective-permute-start | bytes 737288 | tf_op jit(solution)/shard_map/ppermute | solution.py:409
  53.8 18.3 %collective-permute-start.38 = (f32[60,8,128]{2,1,0:T(8,128)S(1)}, f32[60,8,128]{2,1,0:T(8,128)S(1)}, u32[]{:S(2)}, u32[]{:S(2)}) collective-permute-start(f32[60,8,128]{2,1,0:T(8,128)S(1)} %copy-done.34), channel_id=1, source_target_pairs={{0,5},{1,4},{2,7},{3,6},{4,1},{5,0},{6,3},{7,2},{8,13},{9,12},{10,... | collective-permute-start | bytes 737288 | tf_op jit(solution)/shard_map/ppermute | solution.py:409
  54.5 19.7 %collective-permute-start.39 = (f32[60,8,128]{2,1,0:T(8,128)S(1)}, f32[60,8,128]{2,1,0:T(8,128)S(1)}, u32[]{:S(2)}, u32[]{:S(2)}) collective-permute-start(f32[60,8,128]{2,1,0:T(8,128)S(1)} %copy-done.33), channel_id=1, source_target_pairs={{0,6},{1,7},{2,4},{3,5},{4,2},{5,3},{6,0},{7,1},{8,14},{9,15},{10,... | collective-permute-start | bytes 737288 | tf_op jit(solution)/shard_map/ppermute | solution.py:409
  68.9 25.6 %collective-permute-start.2 = (f32[42,16,128]{2,1,0:T(8,128)}, f32[42,16,128]{2,1,0:T(8,128)S(1)}, u32[]{:S(2)}, u32[]{:S(2)}) collective-permute-start(f32[42,16,128]{2,1,0:T(8,128)} %get-tuple-element.68), channel_id=1, source_target_pairs={{0,1},{1,0},{2,3},{3,2},{4,5},{5,4},{6,7},{7,6},{8,9},{9,8},{10,11... | collective-permute-start | bytes 1032200 | tf_op jit(solution)/shard_map/ppermute | solution.py:409
  70.0 25.9 %collective-permute-start.3 = (f32[42,16,128]{2,1,0:T(8,128)}, f32[42,16,128]{2,1,0:T(8,128)S(1)}, u32[]{:S(2)}, u32[]{:S(2)}) collective-permute-start(f32[42,16,128]{2,1,0:T(8,128)} %get-tuple-element.69), channel_id=1, source_target_pairs={{0,2},{1,3},{2,0},{3,1},{4,6},{5,7},{6,4},{7,5},{8,10},{9,11},{10,... | collective-permute-start | bytes 1032200 | tf_op jit(solution)/shard_map/ppermute | solution.py:409
  71.1 25.6 %collective-permute-start.4 = (f32[42,16,128]{2,1,0:T(8,128)}, f32[42,16,128]{2,1,0:T(8,128)S(1)}, u32[]{:S(2)}, u32[]{:S(2)}) collective-permute-start(f32[42,16,128]{2,1,0:T(8,128)} %get-tuple-element.70), channel_id=1, source_target_pairs={{0,3},{1,2},{2,1},{3,0},{4,7},{5,6},{6,5},{7,4},{8,11},{9,10},{10,... | collective-permute-start | bytes 1032200 | tf_op jit(solution)/shard_map/ppermute | solution.py:409
  72.9 24.7 %collective-permute-start.5 = (f32[42,16,128]{2,1,0:T(8,128)}, f32[42,16,128]{2,1,0:T(8,128)S(1)}, u32[]{:S(2)}, u32[]{:S(2)}) collective-permute-start(f32[42,16,128]{2,1,0:T(8,128)} %get-tuple-element.71), channel_id=1, source_target_pairs={{0,4},{1,5},{2,6},{3,7},{4,0},{5,1},{6,2},{7,3},{8,12},{9,13},{10,... | collective-permute-start | bytes 1032200 | tf_op jit(solution)/shard_map/ppermute | solution.py:409
  74.2 18.5 %collective-permute-start.40 = (f32[60,8,128]{2,1,0:T(8,128)S(1)}, f32[60,8,128]{2,1,0:T(8,128)S(1)}, u32[]{:S(2)}, u32[]{:S(2)}) collective-permute-start(f32[60,8,128]{2,1,0:T(8,128)S(1)} %copy-done.32), channel_id=1, source_target_pairs={{0,7},{1,6},{2,5},{3,4},{4,3},{5,2},{6,1},{7,0},{8,15},{9,14},{10,... | collective-permute-start | bytes 737288 | tf_op jit(solution)/shard_map/ppermute | solution.py:409
  93.4 24.1 %collective-permute-start.6 = (f32[42,16,128]{2,1,0:T(8,128)S(1)}, f32[42,16,128]{2,1,0:T(8,128)S(1)}, u32[]{:S(2)}, u32[]{:S(2)}) collective-permute-start(f32[42,16,128]{2,1,0:T(8,128)S(1)} %copy-done.31), channel_id=1, source_target_pairs={{0,5},{1,4},{2,7},{3,6},{4,1},{5,0},{6,3},{7,2},{8,13},{9,12},{10,... | collective-permute-start | bytes 1032200 | tf_op jit(solution)/shard_map/ppermute | solution.py:409
  94.5 63.7 %copy-start = (f32[42,16,128]{2,1,0:T(8,128)}, f32[42,16,128]{2,1,0:T(8,128)S(1)}, u32[]{:S(2)}) copy-start(f32[42,16,128]{2,1,0:T(8,128)S(1)} %collective-permute-done.2.rest_1_) | copy-start | bytes 1032196
  94.5 24.3 %collective-permute-start.7 = (f32[42,16,128]{2,1,0:T(8,128)}, f32[42,16,128]{2,1,0:T(8,128)S(1)}, u32[]{:S(2)}, u32[]{:S(2)}) collective-permute-start(f32[42,16,128]{2,1,0:T(8,128)} %get-tuple-element.73), channel_id=1, source_target_pairs={{0,6},{1,7},{2,4},{3,5},{4,2},{5,3},{6,0},{7,1},{8,14},{9,15},{10,... | collective-permute-start | bytes 1032200 | tf_op jit(solution)/shard_map/ppermute | solution.py:409
  95.8 62.5 %copy-start.1 = (f32[42,16,128]{2,1,0:T(8,128)}, f32[42,16,128]{2,1,0:T(8,128)S(1)}, u32[]{:S(2)}) copy-start(f32[42,16,128]{2,1,0:T(8,128)S(1)} %collective-permute-done.3.rest_2_) | copy-start | bytes 1032196
  95.8 23.9 %collective-permute-start.8 = (f32[42,16,128]{2,1,0:T(8,128)}, f32[42,16,128]{2,1,0:T(8,128)S(1)}, u32[]{:S(2)}, u32[]{:S(2)}) collective-permute-start(f32[42,16,128]{2,1,0:T(8,128)} %get-tuple-element.74), channel_id=1, source_target_pairs={{0,7},{1,6},{2,5},{3,4},{4,3},{5,2},{6,1},{7,0},{8,15},{9,14},{10,... | collective-permute-start | bytes 1032200 | tf_op jit(solution)/shard_map/ppermute | solution.py:409
  96.7 61.6 %copy-start.2 = (f32[42,16,128]{2,1,0:T(8,128)}, f32[42,16,128]{2,1,0:T(8,128)S(1)}, u32[]{:S(2)}) copy-start(f32[42,16,128]{2,1,0:T(8,128)S(1)} %collective-permute-done.4.rest_3_) | copy-start | bytes 1032196
  96.7 23.4 %collective-permute-start.11 = (f32[42,16,128]{2,1,0:T(8,128)}, f32[42,16,128]{2,1,0:T(8,128)S(1)}, u32[]{:S(2)}, u32[]{:S(2)}) collective-permute-start(f32[42,16,128]{2,1,0:T(8,128)} %get-tuple-element.78), channel_id=1, source_target_pairs={{0,1},{1,0},{2,3},{3,2},{4,5},{5,4},{6,7},{7,6},{8,9},{9,8},{10,11... | collective-permute-start | bytes 1032200 | tf_op jit(solution)/shard_map/ppermute | solution.py:409
  97.6 60.7 %copy-start.3 = (f32[42,16,128]{2,1,0:T(8,128)}, f32[42,16,128]{2,1,0:T(8,128)S(1)}, u32[]{:S(2)}) copy-start(f32[42,16,128]{2,1,0:T(8,128)S(1)} %collective-permute-done.5.rest_4_) | copy-start | bytes 1032196
  97.6 24.3 %collective-permute-start.12 = (f32[42,16,128]{2,1,0:T(8,128)}, f32[42,16,128]{2,1,0:T(8,128)S(1)}, u32[]{:S(2)}, u32[]{:S(2)}) collective-permute-start(f32[42,16,128]{2,1,0:T(8,128)} %get-tuple-element.79), channel_id=1, source_target_pairs={{0,2},{1,3},{2,0},{3,1},{4,6},{5,7},{6,4},{7,5},{8,10},{9,11},{10,... | collective-permute-start | bytes 1032200 | tf_op jit(solution)/shard_map/ppermute | solution.py:409
  117.6 40.7 %copy-start.4 = (f32[42,16,128]{2,1,0:T(8,128)}, f32[42,16,128]{2,1,0:T(8,128)S(1)}, u32[]{:S(2)}) copy-start(f32[42,16,128]{2,1,0:T(8,128)S(1)} %collective-permute-done.6.rest_5_) | copy-start | bytes 1032196
  117.6 10.0 %collective-permute-start.13 = (f32[42,16,128]{2,1,0:T(8,128)}, f32[42,16,128]{2,1,0:T(8,128)S(1)}, u32[]{:S(2)}, u32[]{:S(2)}) collective-permute-start(f32[42,16,128]{2,1,0:T(8,128)} %get-tuple-element.80), channel_id=1, source_target_pairs={{0,3},{1,2},{2,1},{3,0},{4,7},{5,6},{6,5},{7,4},{8,11},{9,10},{10,... | collective-permute-start | bytes 1032200 | tf_op jit(solution)/shard_map/ppermute | solution.py:409
  118.8 39.5 %copy-start.5 = (f32[42,16,128]{2,1,0:T(8,128)}, f32[42,16,128]{2,1,0:T(8,128)S(1)}, u32[]{:S(2)}) copy-start(f32[42,16,128]{2,1,0:T(8,128)S(1)} %collective-permute-done.7.rest_6_) | copy-start | bytes 1032196
  118.8 26.0 %collective-permute-start.14 = (f32[42,16,128]{2,1,0:T(8,128)}, f32[42,16,128]{2,1,0:T(8,128)}, u32[]{:S(2)}, u32[]{:S(2)}) collective-permute-start(f32[42,16,128]{2,1,0:T(8,128)} %get-tuple-element.81), channel_id=1, source_target_pairs={{0,4},{1,5},{2,6},{3,7},{4,0},{5,1},{6,2},{7,3},{8,12},{9,13},{10,... | collective-permute-start | bytes 1032200 | tf_op jit(solution)/shard_map/ppermute | solution.py:409
  119.7 38.6 %copy-start.6 = (f32[42,16,128]{2,1,0:T(8,128)}, f32[42,16,128]{2,1,0:T(8,128)S(1)}, u32[]{:S(2)}) copy-start(f32[42,16,128]{2,1,0:T(8,128)S(1)} %collective-permute-done.8.rest_7_) | copy-start | bytes 1032196
  119.7 30.4 %collective-permute-start.15 = (f32[42,16,128]{2,1,0:T(8,128)}, f32[42,16,128]{2,1,0:T(8,128)}, u32[]{:S(2)}, u32[]{:S(2)}) collective-permute-start(f32[42,16,128]{2,1,0:T(8,128)} %get-tuple-element.82), channel_id=1, source_target_pairs={{0,5},{1,4},{2,7},{3,6},{4,1},{5,0},{6,3},{7,2},{8,13},{9,12},{10,... | collective-permute-start | bytes 1032200 | tf_op jit(solution)/shard_map/ppermute | solution.py:409
  120.1 38.2 %copy-start.7 = (f32[42,16,128]{2,1,0:T(8,128)}, f32[42,16,128]{2,1,0:T(8,128)S(1)}, u32[]{:S(2)}) copy-start(f32[42,16,128]{2,1,0:T(8,128)S(1)} %collective-permute-done.11.rest_9_) | copy-start | bytes 1032196
  120.1 31.7 %collective-permute-start.16 = (f32[42,16,128]{2,1,0:T(8,128)}, f32[42,16,128]{2,1,0:T(8,128)}, u32[]{:S(2)}, u32[]{:S(2)}) collective-permute-start(f32[42,16,128]{2,1,0:T(8,128)} %get-tuple-element.83), channel_id=1, source_target_pairs={{0,6},{1,7},{2,4},{3,5},{4,2},{5,3},{6,0},{7,1},{8,14},{9,15},{10,... | collective-permute-start | bytes 1032200 | tf_op jit(solution)/shard_map/ppermute | solution.py:409
  121.9 36.5 %copy-start.8 = (f32[42,16,128]{2,1,0:T(8,128)}, f32[42,16,128]{2,1,0:T(8,128)S(1)}, u32[]{:S(2)}) copy-start(f32[42,16,128]{2,1,0:T(8,128)S(1)} %collective-permute-done.12.rest_10_) | copy-start | bytes 1032196
  121.9 31.0 %collective-permute-start.17 = (f32[42,16,128]{2,1,0:T(8,128)}, f32[42,16,128]{2,1,0:T(8,128)}, u32[]{:S(2)}, u32[]{:S(2)}) collective-permute-start(f32[42,16,128]{2,1,0:T(8,128)} %get-tuple-element.84), channel_id=1, source_target_pairs={{0,7},{1,6},{2,5},{3,4},{4,3},{5,2},{6,1},{7,0},{8,15},{9,14},{10,... | collective-permute-start | bytes 1032200 | tf_op jit(solution)/shard_map/ppermute | solution.py:409
  127.6 30.8 %copy-start.9 = (f32[42,16,128]{2,1,0:T(8,128)}, f32[42,16,128]{2,1,0:T(8,128)S(1)}, u32[]{:S(2)}) copy-start(f32[42,16,128]{2,1,0:T(8,128)S(1)} %collective-permute-done.13.rest_11_) | copy-start | bytes 1032196
  127.6 45.4 %collective-permute-start.20 = (f32[60,8,128]{2,1,0:T(8,128)}, f32[60,8,128]{2,1,0:T(8,128)}, u32[]{:S(2)}, u32[]{:S(2)}) collective-permute-start(f32[60,8,128]{2,1,0:T(8,128)} %get-tuple-element.88), channel_id=1, source_target_pairs={{0,1},{1,0},{2,3},{3,2},{4,5},{5,4},{6,7},{7,6},{8,9},{9,8},{10,11... | collective-permute-start | bytes 737288 | tf_op jit(solution)/shard_map/ppermute | solution.py:409
  144.8 29.1 %collective-permute-start.21 = (f32[60,8,128]{2,1,0:T(8,128)}, f32[60,8,128]{2,1,0:T(8,128)}, u32[]{:S(2)}, u32[]{:S(2)}) collective-permute-start(f32[60,8,128]{2,1,0:T(8,128)} %get-tuple-element.89), channel_id=1, source_target_pairs={{0,2},{1,3},{2,0},{3,1},{4,6},{5,7},{6,4},{7,5},{8,10},{9,11},{10,... | collective-permute-start | bytes 737288 | tf_op jit(solution)/shard_map/ppermute | solution.py:409
  150.1 24.9 %collective-permute-start.22 = (f32[60,8,128]{2,1,0:T(8,128)}, f32[60,8,128]{2,1,0:T(8,128)}, u32[]{:S(2)}, u32[]{:S(2)}) collective-permute-start(f32[60,8,128]{2,1,0:T(8,128)} %get-tuple-element.90), channel_id=1, source_target_pairs={{0,3},{1,2},{2,1},{3,0},{4,7},{5,6},{6,5},{7,4},{8,11},{9,10},{10,... | collective-permute-start | bytes 737288 | tf_op jit(solution)/shard_map/ppermute | solution.py:409
  151.9 24.7 %collective-permute-start.23 = (f32[60,8,128]{2,1,0:T(8,128)}, f32[60,8,128]{2,1,0:T(8,128)}, u32[]{:S(2)}, u32[]{:S(2)}) collective-permute-start(f32[60,8,128]{2,1,0:T(8,128)} %get-tuple-element.91), channel_id=1, source_target_pairs={{0,4},{1,5},{2,6},{3,7},{4,0},{5,1},{6,2},{7,3},{8,12},{9,13},{10,... | collective-permute-start | bytes 737288 | tf_op jit(solution)/shard_map/ppermute | solution.py:409
  152.9 24.6 %collective-permute-start.24 = (f32[60,8,128]{2,1,0:T(8,128)}, f32[60,8,128]{2,1,0:T(8,128)}, u32[]{:S(2)}, u32[]{:S(2)}) collective-permute-start(f32[60,8,128]{2,1,0:T(8,128)} %get-tuple-element.92), channel_id=1, source_target_pairs={{0,5},{1,4},{2,7},{3,6},{4,1},{5,0},{6,3},{7,2},{8,13},{9,12},{10,... | collective-permute-start | bytes 737288 | tf_op jit(solution)/shard_map/ppermute | solution.py:409
  172.9 71.6 %collective-permute-start.41 = (f32[144,8,128]{2,1,0:T(8,128)}, f32[144,8,128]{2,1,0:T(8,128)S(1)}, u32[]{:S(2)}, u32[]{:S(2)}) collective-permute-start(f32[144,8,128]{2,1,0:T(8,128)} %get-tuple-element.118), channel_id=1, source_target_pairs={{0,2},{1,3},{2,0},{3,1},{4,6},{5,7},{6,4},{7,5},{8,10},{9,11},{10,... | collective-permute-start | bytes 1769480 | tf_op jit(solution)/shard_map/ppermute | solution.py:409
  173.9 72.4 %collective-permute-start.42 = (f32[144,8,128]{2,1,0:T(8,128)}, f32[144,8,128]{2,1,0:T(8,128)S(1)}, u32[]{:S(2)}, u32[]{:S(2)}) collective-permute-start(f32[144,8,128]{2,1,0:T(8,128)} %get-tuple-element.119), channel_id=1, source_target_pairs={{0,4},{1,5},{2,6},{3,7},{4,0},{5,1},{6,2},{7,3},{8,12},{9,13},{10,... | collective-permute-start | bytes 1769480 | tf_op jit(solution)/shard_map/ppermute | solution.py:409
  175.1 71.4 %collective-permute-start.43 = (f32[144,8,128]{2,1,0:T(8,128)}, f32[144,8,128]{2,1,0:T(8,128)S(1)}, u32[]{:S(2)}, u32[]{:S(2)}) collective-permute-start(f32[144,8,128]{2,1,0:T(8,128)} %get-tuple-element.120), channel_id=1, source_target_pairs={{0,6},{1,7},{2,4},{3,5},{4,2},{5,3},{6,0},{7,1},{8,14},{9,15},{10,... | collective-permute-start | bytes 1769480 | tf_op jit(solution)/shard_map/ppermute | solution.py:409
  176.5 70.3 %collective-permute-start.44 = (f32[144,8,128]{2,1,0:T(8,128)}, f32[144,8,128]{2,1,0:T(8,128)S(1)}, u32[]{:S(2)}, u32[]{:S(2)}) collective-permute-start(f32[144,8,128]{2,1,0:T(8,128)} %get-tuple-element.121), channel_id=1, source_target_pairs={{0,3},{1,2},{2,1},{3,0},{4,7},{5,6},{6,5},{7,4},{8,11},{9,10},{10,... | collective-permute-start | bytes 1769480 | tf_op jit(solution)/shard_map/ppermute | solution.py:409
  177.4 42.9 %collective-permute-start.25 = (f32[60,8,128]{2,1,0:T(8,128)}, f32[60,8,128]{2,1,0:T(8,128)S(1)}, u32[]{:S(2)}, u32[]{:S(2)}) collective-permute-start(f32[60,8,128]{2,1,0:T(8,128)} %get-tuple-element.93), channel_id=1, source_target_pairs={{0,6},{1,7},{2,4},{3,5},{4,2},{5,3},{6,0},{7,1},{8,14},{9,15},{10,... | collective-permute-start | bytes 737288 | tf_op jit(solution)/shard_map/ppermute | solution.py:409
  220.3 9.1 %collective-permute-start.26 = (f32[60,8,128]{2,1,0:T(8,128)}, f32[60,8,128]{2,1,0:T(8,128)S(1)}, u32[]{:S(2)}, u32[]{:S(2)}) collective-permute-start(f32[60,8,128]{2,1,0:T(8,128)} %get-tuple-element.94), channel_id=1, source_target_pairs={{0,7},{1,6},{2,5},{3,4},{4,3},{5,2},{6,1},{7,0},{8,15},{9,14},{10,... | collective-permute-start | bytes 737288 | tf_op jit(solution)/shard_map/ppermute | solution.py:409
  229.4 18.3 %collective-permute-start.45 = (f32[144,8,128]{2,1,0:T(8,128)}, f32[144,8,128]{2,1,0:T(8,128)S(1)}, u32[]{:S(2)}, u32[]{:S(2)}) collective-permute-start(f32[144,8,128]{2,1,0:T(8,128)} %get-tuple-element.122), channel_id=1, source_target_pairs={{0,5},{1,4},{2,7},{3,6},{4,1},{5,0},{6,3},{7,2},{8,13},{9,12},{10,... | collective-permute-start | bytes 1769480 | tf_op jit(solution)/shard_map/ppermute | solution.py:409
  244.6 30.2 %copy-start.10 = (f32[144,8,128]{2,1,0:T(8,128)}, f32[144,8,128]{2,1,0:T(8,128)S(1)}, u32[]{:S(2)}) copy-start(f32[144,8,128]{2,1,0:T(8,128)S(1)} %collective-permute-done.41.rest_1_) | copy-start | bytes 1769476
  244.6 16.4 %collective-permute-start.46 = (f32[144,8,128]{2,1,0:T(8,128)}, f32[144,8,128]{2,1,0:T(8,128)}, u32[]{:S(2)}, u32[]{:S(2)}) collective-permute-start(f32[144,8,128]{2,1,0:T(8,128)} %get-tuple-element.123), channel_id=1, source_target_pairs={{0,7},{1,6},{2,5},{3,4},{4,3},{5,2},{6,1},{7,0},{8,15},{9,14},{10,... | collective-permute-start | bytes 1769480 | tf_op jit(solution)/shard_map/ppermute | solution.py:409
  246.3 28.5 %copy-start.11 = (f32[144,8,128]{2,1,0:T(8,128)}, f32[144,8,128]{2,1,0:T(8,128)S(1)}, u32[]{:S(2)}) copy-start(f32[144,8,128]{2,1,0:T(8,128)S(1)} %collective-permute-done.42.rest_2_) | copy-start | bytes 1769476
  246.3 15.7 %collective-permute-start.47 = (f32[144,8,128]{2,1,0:T(8,128)}, f32[144,8,128]{2,1,0:T(8,128)}, u32[]{:S(2)}, u32[]{:S(2)}) collective-permute-start(f32[144,8,128]{2,1,0:T(8,128)} %get-tuple-element.124), channel_id=1, source_target_pairs={{0,1},{1,0},{2,3},{3,2},{4,5},{5,4},{6,7},{7,6},{8,9},{9,8},{10,11... | collective-permute-start | bytes 1769480 | tf_op jit(solution)/shard_map/ppermute | solution.py:409
  246.4 28.4 %copy-start.12 = (f32[144,8,128]{2,1,0:T(8,128)}, f32[144,8,128]{2,1,0:T(8,128)S(1)}, u32[]{:S(2)}) copy-start(f32[144,8,128]{2,1,0:T(8,128)S(1)} %collective-permute-done.43.rest_3_) | copy-start | bytes 1769476
  246.4 17.5 %collective-permute-start.30 = (f32[144,8,128]{2,1,0:T(8,128)}, f32[144,8,128]{2,1,0:T(8,128)}, u32[]{:S(2)}, u32[]{:S(2)}) collective-permute-start(f32[144,8,128]{2,1,0:T(8,128)} %get-tuple-element.106), channel_id=1, source_target_pairs={{0,1},{1,0},{2,3},{3,2},{4,5},{5,4},{6,7},{7,6},{8,9},{9,8},{10,11... | collective-permute-start | bytes 1769480 | tf_op jit(solution)/shard_map/ppermute | solution.py:409
  246.8 28.0 %copy-start.13 = (f32[144,8,128]{2,1,0:T(8,128)}, f32[144,8,128]{2,1,0:T(8,128)S(1)}, u32[]{:S(2)}) copy-start(f32[144,8,128]{2,1,0:T(8,128)S(1)} %collective-permute-done.44.rest_4_) | copy-start | bytes 1769476
  246.8 27.5 %collective-permute-start.31 = (f32[144,8,128]{2,1,0:T(8,128)}, f32[144,8,128]{2,1,0:T(8,128)}, u32[]{:S(2)}, u32[]{:S(2)}) collective-permute-start(f32[144,8,128]{2,1,0:T(8,128)} %get-tuple-element.107), channel_id=1, source_target_pairs={{0,2},{1,3},{2,0},{3,1},{4,6},{5,7},{6,4},{7,5},{8,10},{9,11},{10,... | collective-permute-start | bytes 1769480 | tf_op jit(solution)/shard_map/ppermute | solution.py:409
  247.6 56.9 %collective-permute-start.27 = (f32[144,8,128]{2,1,0:T(8,128)}, f32[144,8,128]{2,1,0:T(8,128)S(1)}, u32[]{:S(2)}, u32[]{:S(2)}) collective-permute-start(f32[144,8,128]{2,1,0:T(8,128)} %get-tuple-element.102), channel_id=1, source_target_pairs={{0,5},{1,4},{2,7},{3,6},{4,1},{5,0},{6,3},{7,2},{8,13},{9,12},{10,... | collective-permute-start | bytes 1769480 | tf_op jit(solution)/shard_map/ppermute | solution.py:409
  261.0 38.9 %collective-permute-start.32 = (f32[144,8,128]{2,1,0:T(8,128)}, f32[144,8,128]{2,1,0:T(8,128)}, u32[]{:S(2)}, u32[]{:S(2)}) collective-permute-start(f32[144,8,128]{2,1,0:T(8,128)} %get-tuple-element.108), channel_id=1, source_target_pairs={{0,4},{1,5},{2,6},{3,7},{4,0},{5,1},{6,2},{7,3},{8,12},{9,13},{10,... | collective-permute-start | bytes 1769480 | tf_op jit(solution)/shard_map/ppermute | solution.py:409
  262.0 37.9 %collective-permute-start.33 = (f32[144,8,128]{2,1,0:T(8,128)}, f32[144,8,128]{2,1,0:T(8,128)}, u32[]{:S(2)}, u32[]{:S(2)}) collective-permute-start(f32[144,8,128]{2,1,0:T(8,128)} %get-tuple-element.109), channel_id=1, source_target_pairs={{0,6},{1,7},{2,4},{3,5},{4,2},{5,3},{6,0},{7,1},{8,14},{9,15},{10,... | collective-permute-start | bytes 1769480 | tf_op jit(solution)/shard_map/ppermute | solution.py:409
  263.9 38.7 %collective-permute-start.29 = (f32[144,8,128]{2,1,0:T(8,128)}, f32[144,8,128]{2,1,0:T(8,128)}, u32[]{:S(2)}, u32[]{:S(2)}) collective-permute-start(f32[144,8,128]{2,1,0:T(8,128)} %get-tuple-element.104), channel_id=1, source_target_pairs={{0,3},{1,2},{2,1},{3,0},{4,7},{5,6},{6,5},{7,4},{8,11},{9,10},{10,... | collective-permute-start | bytes 1769480 | tf_op jit(solution)/shard_map/ppermute | solution.py:409
  274.3 37.3 %collective-permute-start.28 = (f32[144,8,128]{2,1,0:T(8,128)}, f32[144,8,128]{2,1,0:T(8,128)}, u32[]{:S(2)}, u32[]{:S(2)}) collective-permute-start(f32[144,8,128]{2,1,0:T(8,128)} %get-tuple-element.103), channel_id=1, source_target_pairs={{0,7},{1,6},{2,5},{3,4},{4,3},{5,2},{6,1},{7,0},{8,15},{9,14},{10,... | collective-permute-start | bytes 1769480 | tf_op jit(solution)/shard_map/ppermute | solution.py:409
  (19 other events, 178.2 us)
